TPU v7x, 32 devices: a whole 2x2x4 slice. The times are simulated.
32 devices in a mesh: groups: 2 (over x), dp: 2 (over core), ctx: 8 (over z, y).
Axes of the slice: x: 2, y: 2, z: 4, core: 2. Of those that a mesh axis runs over, the one named last changes fastest.
Arguments:
- h_fwd: bfloat16 [4, 1024, 1024], P(('groups', 'dp'), 'ctx'), parts along dimension 0, may hold values from -6 to 6
- h_rc: bfloat16 [4, 1024, 1024], P(('groups', 'dp'), 'ctx'), parts along dimension 0, may hold values from -6 to 6
- tokens: int32 [4, 1024], P(('groups', 'dp'), 'ctx'), parts along dimension 0, may hold values from 0 to 4
- loss_mask: int32 [4, 1024], P(('groups', 'dp'), 'ctx'), parts along dimension 0, may hold values from 0 to 1
- species: int32 [4], P(('groups', 'dp')), parts along dimension 0, may hold values from 0 to 7, as said below
- w_in: bfloat16 [1024, 2192], replicated, may hold values from -0.1875 to 0.1875
- a_log: float32 [16], replicated, may hold values from -6 to 0.5
- dt_bias: float32 [16], replicated, may hold values from -7 to 1
- d_skip: float32 [16], replicated, may hold values from 0.5 to 1.5
- norm_gain: float32 [1024], replicated, may hold values from 0.5 to 1.5
- w_out: bfloat16 [1024, 1024], replicated, may hold values from -0.1875 to 0.1875
- final_gain: float32 [1024], replicated, may hold values from 0.5 to 1.5
- w_head: float32 [5, 1024], replicated, may hold values from -0.5 to 0.5
- log_var: float32 [8], replicated, may hold values from -1 to 1
Outputs:
- loss: float32 [2], P('groups'), parts along dimension 0
- grad_log_var: float32 [16], P('groups'), parts along dimension 0
- grad_h_fwd: bfloat16 [4, 1024, 1024], P(('groups', 'dp'), 'ctx'), parts along dimension 0
- grad_h_rc: bfloat16 [4, 1024, 1024], P(('groups', 'dp'), 'ctx'), parts along dimension 0
- grad_w_in: float32 [2048, 2192], P(('groups', 'dp', 'ctx')), parts along dimension 0
- grad_w_out: float32 [2048, 1024], P(('groups', 'dp', 'ctx')), parts along dimension 0
There are 2 independent parts, one for each index of `groups`. A program takes and returns all parts, laid end to end along the dimension named above; an argument that names none is the same for every part. Nothing has to cross between parts.
Inputs may be any that keep to these rules, and one draw needn't show every extreme that they name: Neighbouring sequences of one part belong to different species.
All inputs are finite; a program needn't handle non-finite values.
Results may differ from a plain program's by a relative error of at most 0.012.
The roundings to bfloat16 on the way count: a program that leaves them out, or rounds other values in their place, can miss the bound.
Values may be sent and summed in bfloat16 or wider, within the bound.
No kernel may reach another device: no remote copies, remote signals or barrier semaphores. Data moves between devices by JAX's collectives and lax.ppermute only.
A program may use at most 256 MiB of HBM per device.

v0:
```python
import jax
import jax.numpy as jnp
from jax import lax
from jax.sharding import PartitionSpec as P

HEADS = 16
HEAD_DIM = 64
STATE = 64


PRECISE = lax.Precision.HIGHEST
EPSILON = 1e-05
MASKED = -1e30


def partner(array, axis, distance):
    return lax.ppermute(array, axis, [(i, i ^ 1 << distance) for i in range(lax.axis_size(axis))])


def prefix(array, axis, combine, identity, reverse):
    length, position = (lax.axis_size(axis), lax.axis_index(axis))
    everything = jax.tree.map(lambda part: lax.all_gather(part, axis), array)
    start = jax.tree.map(
        lambda part, zero: jnp.broadcast_to(jnp.asarray(zero, part.dtype), part.shape),
        array,
        identity,
    )

    def step(k, before):
        at = length - 1 - k if reverse else k
        reached = at > position if reverse else at < position
        new = combine(before, jax.tree.map(lambda part: part[at], everything))
        return jax.tree.map(lambda a, b: jnp.where(reached, a, b), new, before)

    return lax.fori_loop(0, length, step, start)


def entering(array, axis, join, neutral, backward):
    count = lax.axis_size(axis)
    place = lax.axis_index(axis)
    ahead = count - 1 - place if backward else place
    gathered = jax.tree.map(
        lambda a, kind: lax.all_gather(a.astype(kind), axis),
        array,
        jax.tree.map(lambda a: jnp.bfloat16 if a.dtype == jnp.float32 else a.dtype, array),
    )
    state = jax.tree.map(lambda a, e: jnp.zeros_like(a) + jnp.asarray(e, a.dtype), array, neutral)

    def one(step, state):
        source = count - 1 - step if backward else step
        return join(
            state,
            jax.tree.map(
                lambda a, own: lax.dynamic_index_in_dim(a, source, 0, False).astype(own.dtype),
                gathered,
                array,
            ),
        )

    return lax.fori_loop(0, ahead, one, state)


def prepare(proj_f32, dt_bias, a_log):
    inner_width = HEADS * HEAD_DIM
    batch_rows, length = (proj_f32.shape[0], proj_f32.shape[1])
    values = proj_f32[..., :inner_width].reshape(batch_rows, length, HEADS, HEAD_DIM)
    gate_in = proj_f32[..., inner_width : 2 * inner_width]
    keys_in = proj_f32[..., 2 * inner_width : 2 * inner_width + STATE]
    read_vec = proj_f32[..., 2 * inner_width + STATE : 2 * inner_width + 2 * STATE]
    step_size = jax.nn.softplus(proj_f32[..., 2 * inner_width + 2 * STATE :] + dt_bias)
    logdec = -jnp.exp(a_log) * step_size
    return (values, gate_in, keys_in, read_vec, step_size, logdec)


def summary(values, step_size, logdec, keys_in):
    cumulative = jnp.cumsum(logdec, axis=1)
    final_log = cumulative[:, -1]
    weights = jnp.exp(final_log[:, None] - cumulative) * step_size
    end_state = jnp.einsum("gth,gthp,gtn->ghpn", weights, values, keys_in, precision=PRECISE)
    return (jnp.exp(final_log), end_state)


def local_out(values, step_size, logdec, keys_in, read_vec, carry_in, d_skip):
    cumulative = jnp.cumsum(logdec, axis=1)
    length = values.shape[1]
    scores = jnp.einsum("gtn,gsn->gts", read_vec, keys_in, precision=PRECISE)
    lower_tri = lax.broadcasted_iota(jnp.int32, (length, length), 0) >= lax.broadcasted_iota(
        jnp.int32, (length, length), 1
    )
    cum_heads = jnp.swapaxes(cumulative, 1, 2)
    step_heads = jnp.swapaxes(step_size, 1, 2)
    segment = cum_heads[:, :, :, None] - cum_heads[:, :, None, :]
    segment = jnp.where(lower_tri[None, None, :, :], segment, MASKED)
    mixing = jnp.exp(segment) * scores[:, None, :, :] * step_heads[:, :, None, :]
    output = jnp.einsum("ghts,gshp->gthp", mixing, values, precision=PRECISE)
    output = output + jnp.einsum(
        "gth,gtn,ghpn->gthp", jnp.exp(cumulative), read_vec, carry_in, precision=PRECISE
    )
    return output + d_skip[:, None] * values


def tail_mid(out_left, out_right, gate_in, norm_gain):

    def gated_norm(direction_out):
        gated_flat = direction_out.reshape(gate_in.shape) * jax.nn.silu(gate_in)
        return (
            gated_flat
            * lax.rsqrt(jnp.mean(gated_flat * gated_flat, axis=-1, keepdims=True) + EPSILON)
            * norm_gain
        )

    return gated_norm(out_left) + gated_norm(out_right)


def head_fn(mixed_in, hidden_in, final_gain, w_head):
    residual = hidden_in + mixed_in
    normed = (
        residual
        * lax.rsqrt(jnp.mean(residual * residual, axis=-1, keepdims=True) + EPSILON)
        * final_gain
    )
    return jnp.einsum("gtd,vd->gtv", normed, w_head, precision=PRECISE)


def complement(logits):
    return jnp.concatenate([logits[..., 3::-1], logits[..., 4:]], axis=-1)


def chain_step(earlier, later):
    return (earlier[0] * later[0], later[0][..., None, None] * earlier[1] + later[1])


def local_adjoint(inputs, carry_in, d_out, d_skip):

    def local_fn(values, step_size, logdec, keys_in, read_vec, carry_part):
        return local_out(values, step_size, logdec, keys_in, read_vec, carry_part, d_skip)

    unused, pull = jax.vjp(
        local_fn, inputs[0], inputs[1], inputs[2], inputs[3], inputs[4], carry_in
    )
    return pull(d_out)


def summary_adjoint(inputs, carry_in, next_grad):
    unused, pull = jax.vjp(summary, inputs[0], inputs[1], inputs[2], inputs[3])
    return pull((jnp.sum(next_grad * carry_in, axis=(-2, -1)), next_grad))


def merge_grads(local_part, summary_part):
    return (
        local_part[0] + summary_part[0],
        local_part[1] + summary_part[1],
        local_part[2] + summary_part[2],
        local_part[3] + summary_part[3],
        local_part[4],
    )


def mirror_blocks(block):
    for bit_index in range(lax.axis_size("ctx").bit_length() - 1):
        block = partner(block, "ctx", bit_index)
    return block[:, ::-1]


def mirror_block_grads(block):
    for bit_index in range(lax.axis_size("ctx").bit_length() - 1):
        block = partner(block, "ctx", bit_index)
    return block[:, ::-1]


def on_device(
    h_fwd,
    h_rc,
    tokens,
    loss_mask,
    species,
    w_in,
    a_log,
    dt_bias,
    d_skip,
    norm_gain,
    w_out,
    final_gain,
    w_head,
    log_var,
):
    seq_count = h_fwd.shape[0]
    mask_float = loss_mask.astype(jnp.float32)
    species_hot = (
        species[:, None] == jnp.arange(log_var.shape[0], dtype=jnp.int32)[None, :]
    ).astype(jnp.float32)
    counts_local = jnp.sum(jnp.sum(mask_float, axis=1)[:, None] * species_hot, axis=0)
    counts = lax.psum(counts_local, ("dp", "ctx"))
    rc_block = mirror_blocks(h_rc)
    hidden = jnp.concatenate([h_fwd, rc_block], axis=0)
    batch_rows, length, width = hidden.shape
    hidden_flat = hidden.reshape(batch_rows * length, width)
    proj_b = jnp.dot(hidden_flat, w_in, preferred_element_type=jnp.float32).astype(jnp.bfloat16)
    proj_f32 = proj_b.astype(jnp.float32).reshape(batch_rows, length, -1)

    def prepare_local(proj_in):
        return prepare(proj_in, dt_bias, a_log)

    prepared, prep_pull = jax.vjp(prepare_local, proj_f32)
    values, gate_in, keys_in, read_vec, step_size, logdec = prepared
    left_in = (values, step_size, logdec, keys_in, read_vec)
    right_in = tuple((member[:, ::-1] for member in left_in))
    left_decay, left_state = summary(left_in[0], left_in[1], left_in[2], left_in[3])
    right_decay, right_state = summary(right_in[0], right_in[1], right_in[2], right_in[3])
    identity_pair = (jnp.ones_like(left_decay), jnp.zeros_like(left_state))
    left_carry = prefix((left_decay, left_state), "ctx", chain_step, identity_pair, False)[1]
    right_carry = prefix((right_decay, right_state), "ctx", chain_step, identity_pair, True)[1]
    out_left = local_out(
        left_in[0], left_in[1], left_in[2], left_in[3], left_in[4], left_carry, d_skip
    )
    out_right = local_out(
        right_in[0], right_in[1], right_in[2], right_in[3], right_in[4], right_carry, d_skip
    )[:, ::-1]

    def mid_local(left_part, right_part, gate_part):
        return tail_mid(left_part, right_part, gate_part, norm_gain)

    nsum, mid_pull = jax.vjp(mid_local, out_left, out_right, gate_in)
    nsum_b = nsum.astype(jnp.bfloat16)
    nsum_flat = nsum_b.reshape(batch_rows * length, -1)
    mixed_out = jnp.dot(nsum_flat, w_out, preferred_element_type=jnp.float32).reshape(
        batch_rows, length, width
    )
    hidden32 = hidden.astype(jnp.float32)

    def head_local(mixed_in, hidden_in):
        return head_fn(mixed_in, hidden_in, final_gain, w_head)

    logits, head_pull = jax.vjp(head_local, mixed_out, hidden32)
    rc_logits = logits[seq_count:]
    total_logits = logits[:seq_count] + complement(rc_logits)
    vocab_hot = (tokens[..., None] == jnp.arange(total_logits.shape[-1], dtype=jnp.int32)).astype(
        jnp.float32
    )
    expsum = jnp.sum(jnp.exp(total_logits), axis=-1)
    cross = jnp.log(expsum) - jnp.sum(total_logits * vocab_hot, axis=-1)
    ce_local = jnp.sum(jnp.sum(mask_float * cross, axis=1)[:, None] * species_hot, axis=0)
    scaled = jnp.exp(-log_var) / jnp.maximum(counts, 1.0)
    loss_scale = float(length * lax.axis_size("ctx"))
    row_weight = loss_scale * mask_float * jnp.sum(species_hot * scaled[None, :], axis=1)[:, None]
    d_total = row_weight[..., None] * (jnp.exp(total_logits) / expsum[..., None] - vocab_hot)
    d_rc = complement(d_total)
    d_mixed, d_hidden_head = head_pull(jnp.concatenate([d_total, d_rc], axis=0))
    d_mixed_flat = d_mixed.astype(jnp.bfloat16).reshape(batch_rows * length, width)
    d_nsum = lax.dot_general(
        d_mixed_flat, w_out, (((1,), (1,)), ((), ())), preferred_element_type=jnp.float32
    ).reshape(nsum.shape)
    d_left, d_right, d_gate = mid_pull(d_nsum)
    left_local = local_adjoint(left_in, left_carry, d_left, d_skip)
    right_local = local_adjoint(right_in, right_carry, d_right[:, ::-1], d_skip)
    left_next = entering((left_decay, left_local[5]), "ctx", chain_step, identity_pair, True)[1]
    right_next = entering((right_decay, right_local[5]), "ctx", chain_step, identity_pair, False)[1]
    left_grads = merge_grads(left_local, summary_adjoint(left_in, left_carry, left_next))
    right_grads = tuple(
        (
            member[:, ::-1]
            for member in merge_grads(
                right_local, summary_adjoint(right_in, right_carry, right_next)
            )
        )
    )
    summed = tuple((left_grads[index_one] + right_grads[index_one] for index_one in range(5)))
    d_proj = prep_pull((summed[0], d_gate, summed[3], summed[4], summed[1], summed[2]))[0]
    d_proj_b = d_proj.astype(jnp.bfloat16).reshape(batch_rows * length, -1)
    piece = hidden_flat
    grad_w_in = lax.psum_scatter(
        lax.dot_general(
            piece, d_proj_b, (((0,), (0,)), ((), ())), preferred_element_type=jnp.float32
        ),
        ("dp", "ctx"),
        scatter_dimension=0,
        tiled=True,
    )
    piece = nsum_flat
    grad_w_out = lax.psum_scatter(
        lax.dot_general(
            piece, d_mixed_flat, (((0,), (0,)), ((), ())), preferred_element_type=jnp.float32
        ),
        ("dp", "ctx"),
        scatter_dimension=0,
        tiled=True,
    )
    grad_hidden = lax.dot_general(
        d_proj_b, w_in, (((1,), (1,)), ((), ())), preferred_element_type=jnp.float32
    )
    grad_hidden = (grad_hidden.reshape(batch_rows, length, width) + d_hidden_head).astype(
        jnp.bfloat16
    )
    grad_rc = grad_hidden[seq_count:]
    grad_rc = mirror_block_grads(grad_rc)
    ce_sums = lax.psum(ce_local, ("dp", "ctx"))
    loss = jnp.sum(scaled * ce_sums + log_var).reshape(1)
    grad_log_var = 1.0 - scaled * ce_sums
    return (loss, grad_log_var, grad_hidden[:seq_count], grad_rc, grad_w_in, grad_w_out)


def solution(mesh):
    return jax.shard_map(
        on_device,
        mesh=mesh,
        in_specs=(
            P(("groups", "dp"), "ctx", None),
            P(("groups", "dp"), "ctx", None),
            P(("groups", "dp"), "ctx"),
            P(("groups", "dp"), "ctx"),
            P(("groups", "dp")),
            P(),
            P(),
            P(),
            P(),
            P(),
            P(),
            P(),
            P(),
            P(),
        ),
        out_specs=(
            P("groups"),
            P("groups"),
            P(("groups", "dp"), "ctx", None),
            P(("groups", "dp"), "ctx", None),
            P(("groups", "dp", "ctx"), None),
            P(("groups", "dp", "ctx"), None),
        ),
        check_vma=False,
    )
```

profile of v0, /device:TPU:0, one launch (start us, length us, event | category | flops | bytes accessed | tf_op | source)
XLA Modules:
  0.0 743.0 jit_solution(8574647250358380171)
XLA Ops:
  10.3 6.5 collective-permute-done
  18.6 5.7 collective-permute-done.1
  27.9 9.5 %collective-permute-done.2 = bf16[1,128,1024]{2,1,0:T(8,128)(2,1)S(1)} collective-permute-done((bf16[1,128,1024]{2,1,0:T(8,128)(2,1)S(1)}, bf16[1,128,1024]{2,1,0:T(8,128)(2,1)S(1)}, u32[]{:S(2)}, u32[]{:S(2)}) %collective-permute-start.2) | collective-permute-done | bytes 262176 | tf_op jit(solution)/shard_map/ppermute | solution.py:17
  38.7 4.7 convolution_convert_fusion
  80.6 22.3 %all-gather = f32[16,1,16]{2,1,0:T(1,128)} all-gather(f32[2,1,16]{2,1,0:T(1,128)} %copy.212), channel_id=2, replica_groups=mesh['groups'=2,'dp'=2,'ctx'=8] {'ctx'}, dimensions={0}, use_global_device_ids=true | all-gather | bytes 1152 | tf_op jit(solution)/shard_map/all_gather | solution.py:22
  102.9 17.9 %all-gather.2 = f32[16,1,16]{2,1,0:T(1,128)} all-gather(f32[2,1,16]{2,1,0:T(1,128)} %copy.219), channel_id=4, replica_groups=mesh['groups'=2,'dp'=2,'ctx'=8] {'ctx'}, dimensions={0}, use_global_device_ids=true | all-gather | bytes 1152 | tf_op jit(solution)/shard_map/all_gather | solution.py:22
  123.8 4.4 fusion.40
  128.3 5.2 fusion.46
  133.5 55.4 %all-gather.15.cloned.1.call-done = f32[16,16,64,64]{3,2,1,0:T(8,128)} async-done(((f32[2,16,64,64]{3,2,1,0:T(8,128)}), f32[16,16,64,64]{3,2,1,0:T(8,128)}) %all-gather.15.cloned.1.call-update) | async-done | bytes 4194320 | tf_op jit(solution)/shard_map/all_gather | solution.py:22
  188.9 26.6 %while.59 = (s32[]{:T(128)}, f32[2,16,64,64]{3,2,1,0:T(8,128)}, s32[]{:T(128)}, f32[8,2,16]{2,1,0:T(2,128)}, f32[8,2,16,64,64]{4,3,2,1,0:T(8,128)}, /*index=5*/s32[]{:T(128)}, s32[]{:T(128)}, s32[]{:T(128)}, s32[]{:T(128)}) while((s32[]{:T(128)}, f32[2,16,64,64]{3,2,1,0:T(8,128)}, s32[]{:T(128)}, f32[8,2,16]{2,1,0:T(2,128)}, ...), condition=%wide.region_8.9_spmd.clone, body=%wide.region_7.8_spmd.clone.sunk | while | flops 524296 | bytes 1573423 | solution.py:35
  221.8 91.9 %all-gather.13.cloned.1.call-done = f32[16,16,64,64]{3,2,1,0:T(8,128)} async-done(((f32[2,16,64,64]{3,2,1,0:T(8,128)}), f32[16,16,64,64]{3,2,1,0:T(8,128)}) %all-gather.13.cloned.1.call-update) | async-done | bytes 4194320 | tf_op jit(solution)/shard_map/all_gather | solution.py:22
  313.7 17.2 %while.58 = (s32[]{:T(128)}, f32[2,16,64,64]{3,2,1,0:T(8,128)S(1)}, s32[]{:T(128)}, f32[8,2,16]{2,1,0:T(2,128)}, f32[8,2,16,64,64]{4,3,2,1,0:T(8,128)}, /*index=5*/s32[]{:T(128)}, s32[]{:T(128)}) while((s32[]{:T(128)}, f32[2,16,64,64]{3,2,1,0:T(8,128)S(1)}, s32[]{:T(128)}, f32[8,2,16]{2,1,0:T(2,128)}, ...), condition=%wide.region_4.5_spmd.clone, body=%wide.region_3.4_spmd.clone.sunk | while | flops 524292 | bytes 1573361 | solution.py:35
  345.7 31.5 %all-reduce.7 = (f32[8]{0:T(128)}, f32[8]{0:T(128)}) all-reduce(f32[8]{0:T(128)} %fusion.188, f32[8]{0:T(128)} %fusion.187), channel_id=1, replica_groups=mesh['groups'=2,'dp'=2,'ctx'=8] {'dp','ctx'}, use_global_device_ids=true, to_apply=%region_1.0 | all-reduce | flops 16 | bytes 128 | tf_op jit(solution)/shard_map/psum | solution.py:193
  402.5 18.3 %all-gather.6 = bf16[16,1,16]{2,1,0:T(2,128)(2,1)S(1)} all-gather(bf16[2,1,16]{2,1,0:T(2,128)(2,1)} %copy.223), channel_id=8, replica_groups=mesh['groups'=2,'dp'=2,'ctx'=8] {'ctx'}, dimensions={0}, use_global_device_ids=true | all-gather | bytes 576 | tf_op jit(solution)/shard_map/all_gather | solution.py:43
  422.7 18.2 %all-gather.7 = bf16[16,1,16]{2,1,0:T(2,128)(2,1)S(1)} all-gather(bf16[2,1,16]{2,1,0:T(2,128)(2,1)} %copy.224), channel_id=9, replica_groups=mesh['groups'=2,'dp'=2,'ctx'=8] {'ctx'}, dimensions={0}, use_global_device_ids=true | all-gather | bytes 576 | tf_op jit(solution)/shard_map/all_gather | solution.py:43
  449.2 5.9 fusion.91
  472.0 69.9 %all-gather.17.cloned.1.call-done = bf16[16,16,64,64]{3,2,1,0:T(8,128)(2,1)} async-done(((bf16[2,16,64,64]{3,2,1,0:T(8,128)(2,1)}), bf16[16,16,64,64]{3,2,1,0:T(8,128)(2,1)}) %all-gather.17.cloned.1.call-update) | async-done | bytes 2097168 | tf_op jit(solution)/shard_map/all_gather | solution.py:43
  542.0 14.0 %while.56 = (s32[]{:T(128)}, f32[2,16,64,64]{3,2,1,0:T(8,128)S(1)}, s32[]{:T(128)}, bf16[8,2,16]{2,1,0:T(2,128)(2,1)}, bf16[8,2,16,64,64]{4,3,2,1,0:T(8,128)(2,1...) while((s32[]{:T(128)}, f32[2,16,64,64]{3,2,1,0:T(8,128)S(1)}, s32[]{:T(128)}, ...), condition=%wide.region_21.22_spmd, body=%wide.region_20.21_spmd.sunk | while | flops 393254 | bytes 1311195 | solution.py:60
  594.7 5.1 convolution_bitcast_fusion
  601.1 5.0 fusion.79
  606.8 6.7 collective-permute-done.3
  613.5 8.3 %collective-permute-done.4 = bf16[1,128,1024]{2,1,0:T(8,128)(2,1)S(1)} collective-permute-done((bf16[1,128,1024]{2,1,0:T(8,128)(2,1)S(1)}, bf16[1,128,1024]{2,1,0:T(8,128)(2,1)S(1)}, u32[]{:S(2)}, u32[]{:S(2)}) %collective-permute-start.4) | collective-permute-done | bytes 262176 | tf_op jit(solution)/shard_map/ppermute | solution.py:17
  621.8 13.1 %collective-permute-done.5 = bf16[1,128,1024]{2,1,0:T(8,128)(2,1)S(1)} collective-permute-done((bf16[1,128,1024]{2,1,0:T(8,128)(2,1)S(1)}, bf16[1,128,1024]{2,1,0:T(8,128)(2,1)S(1)}, u32[]{:S(2)}, u32[]{:S(2)}) %collective-permute-start.5) | collective-permute-done | bytes 262176 | tf_op jit(solution)/shard_map/ppermute | solution.py:17
  637.5 98.5 %reduce-scatter.3.cloned.1.call-done = f32[64,2192]{1,0:T(8,128)} async-done(((f32[1024,2192]{1,0:T(8,128)}), f32[64,2192]{1,0:T(8,128)}) %reduce-scatter.3.cloned.1.call-update) | async-done | bytes 561168 | tf_op jit(solution)/shard_map/reduce_scatter | solution.py:271
  (407 shorter events, 221.8 us)
Async XLA Ops:
  7.2 328.3 %copy-start = (bf16[1024,1024]{1,0:T(8,128)(2,1)S(1)}, bf16[1024,1024]{1,0:T(8,128)(2,1)}, u32[]{:S(2)}) copy-start(bf16[1024,1024]{1,0:T(8,128)(2,1)} %param.32) | copy-start | bytes 6291460
  7.2 181.7 %all-gather.15.cloned.1.call-start = ((), (), s32[]{:S(2)}) async-start(), calls=%async_computation.5 | async-start | bytes 9437184 | tf_op jit(solution)/shard_map/all_gather | solution.py:22
  7.2 9.6 %collective-permute-start = (bf16[1,128,1024]{2,1,0:T(8,128)(2,1)}, bf16[1,128,1024]{2,1,0:T(8,128)(2,1)S(1)}, u32[]{:S(2)}, u32[]{:S(2)}) collective-permute-start(bf16[1,128,1024]{2,1,0:T(8,128)(2,1)} %param.23), channel_id=1, source_target_pairs={{0,1},{1,0},{2,3},{3,2},{4,5},{5,4},{6,7},{7,6},{8,9},{9,8},{10,11... | collective-permute-start | bytes 786440 | tf_op jit(solution)/shard_map/ppermute | solution.py:17
  16.8 7.5 %collective-permute-start.1 = (bf16[1,128,1024]{2,1,0:T(8,128)(2,1)S(1)}, bf16[1,128,1024]{2,1,0:T(8,128)(2,1)S(1)}, u32[]{:S(2)}, u32[]{:S(2)}) collective-permute-start(bf16[1,128,1024]{2,1,0:T(8,128)(2,1)S(1)} %collective-permute-done), channel_id=1, source_target_pairs={{0,2},{1,3},{2,0},{3,1},{4,6},{5,7},{6,4},{7,5},{8,10},{9,11},{10,... | collective-permute-start | bytes 786440 | tf_op jit(solution)/shard_map/ppermute | solution.py:17
  24.3 13.1 %collective-permute-start.2 = (bf16[1,128,1024]{2,1,0:T(8,128)(2,1)S(1)}, bf16[1,128,1024]{2,1,0:T(8,128)(2,1)S(1)}, u32[]{:S(2)}, u32[]{:S(2)}) collective-permute-start(bf16[1,128,1024]{2,1,0:T(8,128)(2,1)S(1)} %collective-permute-done.1), channel_id=1, source_target_pairs={{0,4},{1,5},{2,6},{3,7},{4,0},{5,1},{6,2},{7,3},{8,12},{9,13},{10,... | collective-permute-start | bytes 786440 | tf_op jit(solution)/shard_map/ppermute | solution.py:17
  63.3 250.4 %all-gather.13.cloned.1.call-start = ((), (), s32[]{:S(2)}) async-start(), calls=%async_computation.4 | async-start | bytes 9437184 | tf_op jit(solution)/shard_map/all_gather | solution.py:22
  72.4 397.3 %all-gather.19.cloned.1.call-start = ((), (), s32[]{:S(2)}) async-start(), calls=%async_computation.7 | async-start | bytes 4718592 | tf_op jit(solution)/shard_map/all_gather | solution.py:43
  80.5 47.7 %copy-start.4 = (f32[2,128,16,64]{1,3,2,0:T(8,128)S(1)}, f32[2,128,16,64]{1,3,2,0:T(8,128)}, u32[]{:S(2)}) copy-start(f32[2,128,16,64]{1,3,2,0:T(8,128)} %copy-done.3) | copy-start | bytes 3145732
  80.5 47.7 %copy-start.61 = (f32[2,128,16]{1,2,0:T(8,128)S(1)}, f32[2,128,16]{1,2,0:T(8,128)}, u32[]{:S(2)}) copy-start(f32[2,128,16]{1,2,0:T(8,128)} %copy-done.60) | copy-start | bytes 49156
  80.6 47.7 %copy-start.68 = (pred[128,128]{1,0:T(8,128)(4,1)S(1)}, pred[128,128]{1,0:T(8,128)(4,1)}, u32[]{:S(2)}) copy-start(pred[128,128]{1,0:T(8,128)(4,1)} %iota_compare_fusion) | copy-start | bytes 49156
  80.6 47.7 %copy-start.80 = (f32[2,16,128]{2,1,0:T(8,128)S(1)}, f32[2,16,128]{2,1,0:T(8,128)}, u32[]{:S(2)}) copy-start(f32[2,16,128]{2,1,0:T(8,128)} %copy.215) | copy-start | bytes 49156
  393.7 47.8 %copy-start.2 = (f32[2,16,64,64]{3,2,1,0:T(8,128)S(1)}, f32[2,16,64,64]{3,2,1,0:T(8,128)}, u32[]{:S(2)}) copy-start(f32[2,16,64,64]{3,2,1,0:T(8,128)} %get-tuple-element.361) | copy-start | bytes 1572868
  397.6 144.4 %all-gather.17.cloned.1.call-start = ((), (), s32[]{:S(2)}) async-start(), calls=%async_computation.6 | async-start | bytes 4718592 | tf_op jit(solution)/shard_map/all_gather | solution.py:43
  401.0 44.5 %copy-start.5 = (f32[2,128,16,64]{1,3,2,0:T(8,128)S(1)}, f32[2,128,16,64]{1,3,2,0:T(8,128)}, u32[]{:S(2)}) copy-start(f32[2,128,16,64]{1,3,2,0:T(8,128)} %copy-done.3) | copy-start | bytes 3145732
  401.1 236.4 %reduce-scatter.5.cloned.1.call-start = ((), (), s32[]{:S(2)}) async-start(), calls=%async_computation.3 | async-start | bytes 4456448 | tf_op jit(solution)/shard_map/reduce_scatter | solution.py:280
  422.7 22.8 %copy-start.14 = (f32[2,128,16,64]{1,3,2,0:T(8,128)S(1)}, f32[2,128,16,64]{1,3,2,0:T(8,128)}, u32[]{:S(2)}) copy-start(f32[2,128,16,64]{1,3,2,0:T(8,128)} %rev.57) | copy-start | bytes 3145732
  467.1 268.8 %reduce-scatter.3.cloned.1.call-start = ((), (), s32[]{:S(2)}) async-start(), calls=%async_computation.2 | async-start | bytes 10027008 | tf_op jit(solution)/shard_map/reduce_scatter | solution.py:271
  570.8 15.3 %copy-start.50 = (f32[2,128,16]{1,2,0:T(8,128)S(1)}, f32[2,128,16]{1,2,0:T(8,128)}, u32[]{:S(2)}) copy-start(f32[2,128,16]{1,2,0:T(8,128)} %copy-done.49) | copy-start | bytes 49156
  574.3 14.8 %copy-start.46 = (f32[2,128,128]{2,1,0:T(8,128)S(1)}, f32[2,128,128]{2,1,0:T(8,128)}, u32[]{:S(2)}) copy-start(f32[2,128,128]{2,1,0:T(8,128)} %get-tuple-element.410) | copy-start | bytes 393220
  574.3 14.8 %copy-start.54 = (f32[2,128,64]{1,2,0:T(8,128)S(1)}, f32[2,128,64]{1,2,0:T(8,128)}, u32[]{:S(2)}) copy-start(f32[2,128,64]{1,2,0:T(8,128)} %rev.61) | copy-start | bytes 196612
  601.1 134.8 %copy-start.1 = (bf16[1024,1024]{1,0:T(8,128)(2,1)S(1)}, bf16[1024,1024]{1,0:T(8,128)(2,1)}, u32[]{:S(2)}) copy-start(bf16[1024,1024]{1,0:T(8,128)(2,1)} %param.32) | copy-start | bytes 6291460
  606.8 6.7 collective-permute-start.3
  613.5 8.3 %collective-permute-start.4 = (bf16[1,128,1024]{2,1,0:T(8,128)(2,1)S(1)}, bf16[1,128,1024]{2,1,0:T(8,128)(2,1)S(1)}, u32[]{:S(2)}, u32[]{:S(2)}) collective-permute-start(bf16[1,128,1024]{2,1,0:T(8,128)(2,1)S(1)} %collective-permute-done.3), channel_id=1, source_target_pairs={{0,2},{1,3},{2,0},{3,1},{4,6},{5,7},{6,4},{7,5},{8,10},{9,11},{10,... | collective-permute-start | bytes 786440 | tf_op jit(solution)/shard_map/ppermute | solution.py:17
  621.8 13.1 %collective-permute-start.5 = (bf16[1,128,1024]{2,1,0:T(8,128)(2,1)S(1)}, bf16[1,128,1024]{2,1,0:T(8,128)(2,1)S(1)}, u32[]{:S(2)}, u32[]{:S(2)}) collective-permute-start(bf16[1,128,1024]{2,1,0:T(8,128)(2,1)S(1)} %collective-permute-done.4), channel_id=1, source_target_pairs={{0,4},{1,5},{2,6},{3,7},{4,0},{5,1},{6,2},{7,3},{8,12},{9,13},{10,... | collective-permute-start | bytes 786440 | tf_op jit(solution)/shard_map/ppermute | solution.py:17
  (95 other events, 307.9 us)
Sparse Core Ops, SparseCore 0:
  63.4 125.4 all-gather.14
  191.0 122.6 all-gather.12
  397.7 70.8 all-gather.18
  470.5 71.3 all-gather.16
  546.2 74.3 reduce-scatter.4
  625.1 110.7 reduce-scatter.2
where the time goes:
time: 751 us; the launch traced here: 743 us
  waiting for transfers between devices  365 us (49%)
  blocking collectives  108 us (14%)
  matrix products  89.6 us (12%)
  other arithmetic  88.3 us (12%)
  local copies, waits for them, and re-layouts  66.4 us (9%)
  between operations  16.8 us (2%)
  starting transfers between devices  7.64 us (1%)
    all_gather x2, waiting for transfers between devices, prefix(): everything = jax.tree.map(lambda part: lax.all_gather(part, axis), array)  147 us
    reduce_scatter x1, waiting for transfers between devices, on_device(): lax.psum_scatter(lax.dot_general(piece, d_proj_b, (((0,), (0,)), ((), ())...  98.5 us
    all_gather x2, waiting for transfers between devices, entering(): lax.all_gather(a.astype(kind), axis)  69.9 us
    ppermute x6, waiting for transfers between devices, partner(): lax.ppermute(array, axis, [(i, i ^ 1 << distance) for i in range(lax.axis...  49.7 us
    all_gather x2, blocking collectives, prefix(): everything = jax.tree.map(lambda part: lax.all_gather(part, axis), array)  40.2 us
    all_gather x2, blocking collectives, entering(): lax.all_gather(a.astype(kind), axis)  36.5 us
    select_n x16, other arithmetic, step(): return jax.tree.map(lambda a, b: jnp.where(reached, a, b), new, before)  33.2 us
    psum x1, blocking collectives, on_device(): counts = lax.psum(counts_local, ('dp', 'ctx'))  31.5 us
  transfers between devices with their start and end apart: 12, of which 10 were waited for; matrix products, arithmetic and copies ran while one was open for 22% of the time, Pallas kernels for 0%

commit v1 on v0

v1 whole, which is shorter than its diff:
```python
import functools

import jax
import jax.numpy as jnp
from jax import lax
from jax.experimental import pallas as pl
from jax.experimental.pallas import tpu as pltpu
from jax.sharding import PartitionSpec as P

HEADS = 16
HEAD_DIM = 64
STATE = 64
INNER = HEADS * HEAD_DIM
PAIRS = HEADS // 2
LANES = 2 * HEAD_DIM
EPSILON = 1e-05

F32 = jnp.float32
BF16 = jnp.bfloat16
HIGH = lax.Precision.HIGHEST
VMEM_BYTES = 48 * 1024 * 1024


def mm(a, b, ca=1, cb=0, precision=None):
    return lax.dot_general(
        a, b, (((ca,), (cb,)), ((), ())), precision=precision, preferred_element_type=F32
    )


def iota(shape, dim):
    return lax.broadcasted_iota(jnp.int32, shape, dim)


def pair_wide(x, j):
    first = iota((x.shape[0], LANES), 1) < HEAD_DIM
    return jnp.where(first, x[:, 2 * j : 2 * j + 1], x[:, 2 * j + 1 : 2 * j + 2])


def lanes_of(j):
    return slice(j * LANES, (j + 1) * LANES)


def softplus(x):
    return jnp.maximum(x, 0.0) + jnp.log1p(jnp.exp(-jnp.abs(x)))


def tri(length, kind):
    rows, cols = iota((length, length), 0), iota((length, length), 1)
    return jnp.where(rows >= cols if kind == "ge" else rows > cols, 1.0, 0.0).astype(F32)


def head_sum(x):
    pick = (iota((INNER, HEADS), 0) // HEAD_DIM == iota((INNER, HEADS), 1)).astype(F32).astype(BF16)
    return mm(x.astype(BF16), pick)


def steps(proj_ref, bias_ref, alog_ref):
    raw = proj_ref[0, :, 2 * INNER + 2 * STATE :].astype(F32) + bias_ref[...]
    dt = softplus(raw)
    a = -jnp.exp(alog_ref[...]) * dt
    cum = mm(tri(a.shape[0], "ge"), a, precision=HIGH)
    return raw, dt, a, cum, cum - a, cum[-1:, :]


def turned(x):
    n = x.shape[0]
    eye = jnp.where(iota((n, n), 0) == iota((n, n), 1), 1.0, 0.0).astype(F32)
    return mm(x, eye, 0, 0, HIGH)


def turned_back(x):
    n = x.shape[0]
    eye = jnp.where(iota((n, n), 0) == iota((n, n), 1), 1.0, 0.0).astype(F32)
    return mm(x, eye, 0, 0, HIGH)


def keys_of(proj_ref):
    return proj_ref[0, :, 2 * INNER : 2 * INNER + STATE]


def reads_of(proj_ref):
    return proj_ref[0, :, 2 * INNER + STATE : 2 * INNER + 2 * STATE]


def states_kernel(proj_ref, bias_ref, alog_ref, total_ref, decay_ref, wide_l, wide_r):
    unused, dt, a, cum, cex, tot = steps(proj_ref, bias_ref, alog_ref)
    w_l = jnp.exp(tot - cum) * dt
    w_r = jnp.exp(cex) * dt
    block = jnp.exp(tot)
    for j in range(PAIRS):
        s = lanes_of(j)
        v = proj_ref[0, :, s].astype(F32)
        wide_l[:, s] = (v * pair_wide(w_l, j)).astype(BF16)
        wide_r[:, s] = (v * pair_wide(w_r, j)).astype(BF16)
        decay_ref[0, :, s] = pair_wide(block, j)
    keys = keys_of(proj_ref)
    total_ref[0, 0] = mm(keys, wide_l[...], 0, 0).astype(BF16)
    total_ref[1, 0] = mm(keys, wide_r[...], 0, 0).astype(BF16)


def local_kernel(proj_ref, bias_ref, alog_ref, skip_ref, left_ref, right_ref):
    unused, dt, a, cum, cex, tot = steps(proj_ref, bias_ref, alog_ref)
    n = cum.shape[0]
    cum_t, cex_t, dt_t = turned(cum), turned(cex), turned(dt)
    score = mm(reads_of(proj_ref), keys_of(proj_ref), 1, 1)
    t, s = iota((n, n), 0), iota((n, n), 1)
    first = iota((n, LANES), 1) < HEAD_DIM
    zero = jnp.zeros((n, LANES), BF16)
    for j in range(PAIRS):
        lanes = lanes_of(j)
        v = proj_ref[0, :, lanes]
        left, right = [], []
        for h in (2 * j, 2 * j + 1):
            gap = jnp.where(
                t >= s,
                cum[:, h : h + 1] - cum_t[h : h + 1, :],
                cex_t[h : h + 1, :] - cex[:, h : h + 1],
            )
            mix = jnp.exp(jnp.minimum(gap, 0.0)) * score * dt_t[h : h + 1, :]
            left.append(jnp.where(t >= s, mix, 0.0).astype(BF16))
            right.append(jnp.where(t <= s, mix, 0.0).astype(BF16))
        stacked = jnp.concatenate([jnp.where(first, v, zero), jnp.where(first, zero, v)], axis=0)
        skip = pair_wide(skip_ref[...], j) * v.astype(F32)
        left_ref[0, :, lanes] = mm(jnp.concatenate(left, axis=1), stacked) + skip
        right_ref[0, :, lanes] = mm(jnp.concatenate(right, axis=1), stacked) + skip


def out_kernel(
    proj_ref,
    carry_ref,
    left_in,
    right_in,
    hidden_ref,
    bias_ref,
    alog_ref,
    gain_ref,
    wout_ref,
    final_ref,
    head_ref,
    left_ref,
    right_ref,
    nsum_ref,
    res_ref,
    logit_ref,
):
    unused, dt, a, cum, cex, tot = steps(proj_ref, bias_ref, alog_ref)
    e_l, e_r = jnp.exp(cum), jnp.exp(tot - cex)
    reads = reads_of(proj_ref)
    from_l = mm(reads, carry_ref[0, 0])
    from_r = mm(reads, carry_ref[1, 0])
    for j in range(PAIRS):
        s = lanes_of(j)
        left_ref[0, :, s] = left_in[0, :, s] + pair_wide(e_l, j) * from_l[:, s]
        right_ref[0, :, s] = right_in[0, :, s] + pair_wide(e_r, j) * from_r[:, s]
    gate = proj_ref[0, :, INNER : 2 * INNER].astype(F32)
    gated = gate * jax.nn.sigmoid(gate)
    u_l = left_ref[0] * gated
    u_r = right_ref[0] * gated
    k_l = lax.rsqrt(jnp.mean(u_l * u_l, axis=1, keepdims=True) + EPSILON)
    k_r = lax.rsqrt(jnp.mean(u_r * u_r, axis=1, keepdims=True) + EPSILON)
    nsum = ((u_l * k_l + u_r * k_r) * gain_ref[...]).astype(BF16)
    nsum_ref[0] = nsum
    res = hidden_ref[0].astype(F32) + mm(nsum, wout_ref[...])
    res_ref[0] = res
    normed = res * lax.rsqrt(jnp.mean(res * res, axis=1, keepdims=True) + EPSILON) * final_ref[...]
    logit_ref[0] = mm(head_ref[...], normed, 1, 1, HIGH)


def head_kernel(
    proj_ref,
    pack_ref,
    res_ref,
    left_ref,
    right_ref,
    bias_ref,
    alog_ref,
    gain_ref,
    wout_ref,
    final_ref,
    head_ref,
    ce_ref,
    dres_ref,
    dmix_ref,
    dleft_ref,
    dright_ref,
    dgate_ref,
    dstate_ref,
    wide_l,
    wide_r,
    *,
    vocab,
):
    total = pack_ref[0, :8]
    token, weight, mask = pack_ref[0, 8:9], pack_ref[0, 9:10], pack_ref[0, 10:11]
    which = iota(total.shape, 0)
    powers = jnp.where(which < vocab, jnp.exp(total), 0.0)
    expsum = jnp.sum(powers, axis=0, keepdims=True)
    hot = jnp.where(which.astype(F32) == token, 1.0, 0.0)
    ce_ref[0] = mask * (jnp.log(expsum) - jnp.sum(total * hot, axis=0, keepdims=True))
    d_logit = weight * (powers / expsum - hot)
    d_normed = mm(d_logit, head_ref[...], 0, 0, HIGH) * final_ref[...]
    res = res_ref[0]
    k = lax.rsqrt(jnp.mean(res * res, axis=1, keepdims=True) + EPSILON)
    d_res = k * (d_normed - res * (k * k * jnp.mean(d_normed * res, axis=1, keepdims=True)))
    dres_ref[0] = d_res
    d_mix = d_res.astype(BF16)
    dmix_ref[0] = d_mix
    d_sum = mm(d_mix, wout_ref[...], 1, 1) * gain_ref[...]
    gate = proj_ref[0, :, INNER : 2 * INNER].astype(F32)
    sig = jax.nn.sigmoid(gate)
    gated = gate * sig
    d_gated = jnp.zeros_like(gate)
    for source, target in ((left_ref, dleft_ref), (right_ref, dright_ref)):
        out = source[0]
        u = out * gated
        k = lax.rsqrt(jnp.mean(u * u, axis=1, keepdims=True) + EPSILON)
        d_u = k * (d_sum - u * (k * k * jnp.mean(d_sum * u, axis=1, keepdims=True)))
        target[0] = (d_u * gated).astype(BF16)
        d_gated = d_gated + d_u * out
    dgate_ref[0] = (d_gated * (sig + gated * (1.0 - sig))).astype(BF16)
    unused, dt, a, cum, cex, tot = steps(proj_ref, bias_ref, alog_ref)
    e_l, e_r = jnp.exp(cum), jnp.exp(tot - cex)
    for j in range(PAIRS):
        s = lanes_of(j)
        wide_l[:, s] = (dleft_ref[0, :, s].astype(F32) * pair_wide(e_l, j)).astype(BF16)
        wide_r[:, s] = (dright_ref[0, :, s].astype(F32) * pair_wide(e_r, j)).astype(BF16)
    reads = reads_of(proj_ref)
    dstate_ref[0, 0] = mm(reads, wide_l[...], 0, 0).astype(BF16)
    dstate_ref[1, 0] = mm(reads, wide_r[...], 0, 0).astype(BF16)


def adjoint_kernel(
    proj_ref,
    carry_ref,
    dleft_ref,
    dright_ref,
    bias_ref,
    alog_ref,
    skip_ref,
    dval_ref,
    dkey_ref,
    dread_ref,
    da_ref,
    ddt_ref,
    cols_l,
    cols_r,
    wide_l,
    wide_r,
):
    unused, dt, a, cum, cex, tot = steps(proj_ref, bias_ref, alog_ref)
    n = cum.shape[0]
    cum_t, cex_t = turned(cum), turned(cex)
    keys, reads = keys_of(proj_ref), reads_of(proj_ref)
    score = mm(keys, reads, 1, 1)
    s, t = iota((n, n), 0), iota((n, n), 1)
    first = iota((n, LANES), 1) < HEAD_DIM
    zero = jnp.zeros((n, LANES), BF16)
    d_score = jnp.zeros((n, n), F32)
    row_h = jnp.zeros((n, LANES), F32)
    row_l = jnp.zeros((n, LANES), F32)
    row_r = jnp.zeros((n, LANES), F32)
    e_l, e_r = jnp.exp(cum), jnp.exp(tot - cex)
    for j in range(PAIRS):
        lanes = lanes_of(j)
        v = proj_ref[0, :, lanes]
        d_l, d_r = dleft_ref[0, :, lanes], dright_ref[0, :, lanes]
        v_split = jnp.concatenate([jnp.where(first, v, zero), jnp.where(first, zero, v)], axis=0)
        d_mix = mm(v_split, jnp.concatenate([d_l, d_r], axis=0), 1, 1)
        mixes, sums_h, sums_l, sums_r = [], [], [], []
        for i, h in enumerate((2 * j, 2 * j + 1)):
            gap = jnp.where(
                t >= s,
                cum_t[h : h + 1, :] - cum[:, h : h + 1],
                cex[:, h : h + 1] - cex_t[h : h + 1, :],
            )
            decay = jnp.exp(jnp.minimum(gap, 0.0))
            step = dt[:, h : h + 1]
            d_l_mix = d_mix[i * n : (i + 1) * n, :n]
            d_r_mix = d_mix[i * n : (i + 1) * n, n:]
            scaled = decay * (
                jnp.where(t >= s, d_l_mix, 0.0) + jnp.where(t <= s, d_r_mix, 0.0)
            )
            with_step = scaled * step
            d_score = d_score + with_step
            flow = with_step * score
            flow_l = jnp.where(t > s, flow, 0.0)
            flow_r = jnp.where(t < s, flow, 0.0)
            cols_l[h : h + 1, :] = jnp.sum(flow_l, axis=0, keepdims=True)
            cols_r[h : h + 1, :] = jnp.sum(flow_r, axis=0, keepdims=True)
            sums_h.append((scaled * score).astype(BF16))
            sums_l.append(flow_l.astype(BF16))
            sums_r.append(flow_r.astype(BF16))
            mix = decay * score * step
            mixes.append(jnp.where(t >= s, mix, 0.0).astype(BF16))
            mixes.append(jnp.where(t <= s, mix, 0.0).astype(BF16))
        pick_rows, pick_cols = iota((2 * n, LANES), 0), iota((2 * n, LANES), 1)
        pick = (
            jnp.where(pick_cols == 2 * j + (pick_rows >= n).astype(jnp.int32), 1.0, 0.0)
            .astype(F32)
            .astype(BF16)
        )
        row_h = row_h + mm(jnp.concatenate(sums_h, axis=1), pick)
        row_l = row_l + mm(jnp.concatenate(sums_l, axis=1), pick)
        row_r = row_r + mm(jnp.concatenate(sums_r, axis=1), pick)
        d_split = jnp.concatenate(
            [
                jnp.where(first, d_l, zero),
                jnp.where(first, d_r, zero),
                jnp.where(first, zero, d_l),
                jnp.where(first, zero, d_r),
            ],
            axis=0,
        )
        both = d_l.astype(F32) + d_r.astype(F32)
        dval_ref[0, :, lanes] = (
            mm(jnp.concatenate(mixes, axis=1), d_split) + pair_wide(skip_ref[...], j) * both
        )
        wide_l[:, lanes] = (d_l.astype(F32) * pair_wide(e_l, j)).astype(BF16)
        wide_r[:, lanes] = (d_r.astype(F32) * pair_wide(e_r, j)).astype(BF16)
    carry_l, carry_r = carry_ref[0, 0], carry_ref[1, 0]
    d_score_b = d_score.astype(BF16)
    dkey_ref[0] = mm(d_score_b, reads)
    dread_ref[0] = (
        mm(d_score_b, keys, 0, 0)
        + mm(wide_l[...], carry_l, 1, 1)
        + mm(wide_r[...], carry_r, 1, 1)
    )
    d_cum = (
        head_sum(wide_l[...].astype(F32) * mm(reads, carry_l))
        + turned_back(cols_l[...])
        - row_l[:, :HEADS]
    )
    d_rcum = head_sum(wide_r[...].astype(F32) * mm(reads, carry_r))
    d_cex = row_r[:, :HEADS] - turned_back(cols_r[...])
    ge, gt = tri(n, "ge"), tri(n, "gt")
    da_ref[0] = mm(ge, d_cum, 0, 0, HIGH) + mm(gt, d_cex, 0, 0, HIGH) + mm(ge, d_rcum, 1, 0, HIGH)
    ddt_ref[0] = row_h[:, :HEADS]


def finish_kernel(
    proj_ref,
    carry_ref,
    next_ref,
    dval_in,
    dkey_in,
    dread_in,
    da_in,
    ddt_in,
    bias_ref,
    alog_ref,
    dproj_ref,
    wide_l,
    wide_r,
):
    raw, dt, a, cum, cex, tot = steps(proj_ref, bias_ref, alog_ref)
    keys = keys_of(proj_ref)
    f_l, f_r = jnp.exp(tot - cum), jnp.exp(cex)
    w_l, w_r = f_l * dt, f_r * dt
    next_l, next_r = next_ref[0, 0], next_ref[1, 0]
    z_l, z_r = mm(keys, next_l), mm(keys, next_r)
    for j in range(PAIRS):
        s = lanes_of(j)
        v = proj_ref[0, :, s].astype(F32)
        wide_w_l, wide_w_r = pair_wide(w_l, j), pair_wide(w_r, j)
        dproj_ref[0, :, s] = (
            dval_in[0, :, s] + wide_w_l * z_l[:, s] + wide_w_r * z_r[:, s]
        ).astype(BF16)
        wide_l[:, s] = (v * wide_w_l).astype(BF16)
        wide_r[:, s] = (v * wide_w_r).astype(BF16)
    values = proj_ref[0, :, :INNER].astype(F32)
    dw_l, dw_r = head_sum(values * z_l), head_sum(values * z_r)
    d_key = dkey_in[0] + mm(wide_l[...], next_l, 1, 1) + mm(wide_r[...], next_r, 1, 1)
    dproj_ref[0, :, INNER : INNER + STATE] = d_key.astype(BF16)
    dproj_ref[0, :, INNER + STATE : INNER + 2 * STATE] = dread_in[0].astype(BF16)
    through = jnp.sum(
        next_l.astype(F32) * carry_ref[0, 0].astype(F32)
        + next_r.astype(F32) * carry_ref[1, 0].astype(F32),
        axis=0,
        keepdims=True,
    )
    through = head_sum(jnp.broadcast_to(through, (8, INNER)))[:1]
    q_l, q_r = dw_l * w_l, dw_r * w_r
    n = cum.shape[0]
    ge, gt = tri(n, "ge"), tri(n, "gt")
    d_tot = jnp.exp(tot) * through + jnp.sum(q_l, axis=0, keepdims=True)
    d_a = da_in[0] + mm(gt, q_r, 0, 0, HIGH) - mm(ge, q_l, 0, 0, HIGH) + d_tot
    d_dt = ddt_in[0] + dw_l * f_l + dw_r * f_r - d_a * jnp.exp(alog_ref[...])
    dproj_ref[0, :, INNER + 2 * STATE :] = (d_dt * jax.nn.sigmoid(raw)).astype(BF16)


def by_row(shape):
    rest = (0,) * (len(shape) - 1)
    return pl.BlockSpec((1,) + tuple(shape[1:]), lambda g: (g,) + rest)


def by_dir(shape):
    rest = (0,) * (len(shape) - 2)
    return pl.BlockSpec((shape[0], 1) + tuple(shape[2:]), lambda g: (0, g) + rest)


def whole(shape):
    zeros = (0,) * len(shape)
    return pl.BlockSpec(tuple(shape), lambda g: zeros)


def call(kernel, name, operands, results, scratch=(), cost=None):
    specs = {"row": by_row, "dir": by_dir, "all": whole}
    return pl.pallas_call(
        kernel,
        name=name,
        grid=(2,),
        in_specs=[specs[kind](array.shape) for array, kind in operands],
        out_specs=[specs[kind](shape) for shape, dtype, kind in results],
        out_shape=[jax.ShapeDtypeStruct(shape, dtype) for shape, dtype, kind in results],
        scratch_shapes=[pltpu.VMEM(shape, dtype) for shape, dtype in scratch],
        compiler_params=pltpu.CompilerParams(
            dimension_semantics=("arbitrary",), vmem_limit_bytes=VMEM_BYTES
        ),
        cost_estimate=cost,
    )(*[array for array, kind in operands])


def cost(flops, moved):
    return pl.CostEstimate(flops=int(flops), transcendentals=0, bytes_accessed=int(moved))


def bits_of(axis):
    return lax.axis_size(axis).bit_length() - 1


def partner(array, axis, bit):
    return lax.ppermute(array, axis, [(i, i ^ (1 << bit)) for i in range(lax.axis_size(axis))])


def butterfly_sum(array):
    array = array + partner(array, "dp", 0) if lax.axis_size("dp") > 1 else array
    for bit in range(bits_of("ctx")):
        array = array + partner(array, "ctx", bit)
    return array


def decay_rounds(decay):
    me = lax.axis_index("ctx")
    lead_l = jnp.ones_like(decay)
    lead_r = jnp.ones_like(decay)
    rounds = []
    for bit in range(bits_of("ctx")):
        upper = ((me >> bit) & 1) == 1
        theirs = partner(decay, "ctx", bit)
        one, zero = jnp.ones_like(decay), jnp.zeros_like(decay)
        into = jnp.stack([jnp.where(upper, lead_l, zero), jnp.where(upper, zero, lead_r)])
        keep = jnp.stack([jnp.where(upper, one, theirs), jnp.where(upper, theirs, one)])
        take = jnp.stack([jnp.where(upper, decay, one), jnp.where(upper, one, decay)])
        rounds.append((upper, into, keep, take))
        lead_l = jnp.where(upper, lead_l * theirs, lead_l)
        lead_r = jnp.where(upper, lead_r, lead_r * theirs)
        decay = decay * theirs
    return rounds


def scan_blocks(total, rounds):
    entering = jnp.zeros(total.shape, F32)
    last = len(rounds) - 1
    for number, (upper, into, keep, take) in enumerate(rounds):
        if number < last:
            theirs = partner(total, "ctx", number).astype(F32)
            entering = entering + into * theirs
            total = (keep * total.astype(F32) + take * theirs).astype(BF16)
        else:
            theirs = partner(jnp.where(upper, total[1], total[0]), "ctx", number).astype(F32)
            entering = entering + into * theirs[None]
    return entering.astype(BF16)


def share_rows(mine, other_half):
    if lax.axis_size("dp") > 1:
        mine = mine + partner(other_half, "dp", 0).astype(F32)
    bits = bits_of("ctx")
    count = lax.axis_size("ctx")
    me = lax.axis_index("ctx")
    rows, cols = mine.shape
    cut = cols // 2 // 128 * 128
    parts = []
    for part, order in (
        (mine[:, :cut], list(range(bits))),
        (mine[:, cut:], list(range(1, bits)) + [0]),
    ):
        part = part.reshape((2,) * bits + (rows // count, part.shape[1]))
        left = list(range(bits - 1, -1, -1))
        for bit in order:
            at = left.index(bit)
            mine_bit = (me >> bit) & 1
            keep = lax.dynamic_index_in_dim(part, mine_bit, at, False)
            send = lax.dynamic_index_in_dim(part, 1 - mine_bit, at, False).astype(BF16)
            part = keep + partner(send, "ctx", bit).astype(F32)
            left.remove(bit)
        parts.append(part)
    return jnp.concatenate(parts, axis=1)


def weight_grad(rows_of, cotangent):
    half = rows_of.shape[1] // lax.axis_size("dp")
    me = lax.axis_index("dp")

    def part(which):
        piece = lax.dynamic_slice_in_dim(rows_of, which * half, half, 1)
        return mm(piece, cotangent, 0, 0)

    return part(me), part(1 - me).astype(BF16)


def complement(rows):
    return jnp.concatenate([rows[3::-1], rows[4:]], axis=0)


def on_device(
    h_fwd,
    h_rc,
    tokens,
    loss_mask,
    species,
    w_in,
    a_log,
    dt_bias,
    d_skip,
    norm_gain,
    w_out,
    final_gain,
    w_head,
    log_var,
):
    length, width = h_fwd.shape[1], h_fwd.shape[2]
    vocab = w_head.shape[0]
    ctx = lax.axis_size("ctx")
    rows = 2
    flat = rows * length

    hidden = jnp.concatenate([h_fwd, h_rc], axis=0)
    hidden_flat = hidden.reshape(flat, width)
    proj = mm(hidden_flat, w_in).astype(BF16).reshape(rows, length, -1)

    bias, alog, skip = dt_bias[None], a_log[None], d_skip[None]
    gain, final = norm_gain[None], final_gain[None]
    head = jnp.concatenate([w_head, jnp.zeros((8 - vocab, width), F32)], axis=0)

    mask_row = loss_mask.astype(F32)
    species_hot = (
        species[:, None] == jnp.arange(log_var.shape[0], dtype=jnp.int32)[None, :]
    ).astype(F32)
    counts = butterfly_sum(jnp.sum(mask_row, axis=1, keepdims=True) * species_hot)[0]
    scaled = jnp.exp(-log_var) / jnp.maximum(counts, 1.0)

    state_shape = (2, rows, STATE, INNER)
    wide = ((length, INNER), BF16)
    full = (rows, length, INNER)
    total, decay = call(
        states_kernel,
        "states",
        [(proj, "row"), (bias, "all"), (alog, "all")],
        [(state_shape, BF16, "dir"), ((rows, 1, INNER), F32, "row")],
        [wide, wide],
        cost(1e9, 3e6),
    )
    rounds = decay_rounds(decay)
    left_own, right_own = call(
        local_kernel,
        "local",
        [(proj, "row"), (bias, "all"), (alog, "all"), (skip, "all")],
        [(full, F32, "row"), (full, F32, "row")],
        (),
        cost(4e9, 4e6),
    )
    carry = scan_blocks(total, rounds)
    out_left, out_right, nsum, res, logits = call(
        out_kernel,
        "out",
        [
            (proj, "row"),
            (carry, "dir"),
            (left_own, "row"),
            (right_own, "row"),
            (hidden, "row"),
            (bias, "all"),
            (alog, "all"),
            (gain, "all"),
            (w_out, "all"),
            (final, "all"),
            (head, "all"),
        ],
        [
            (full, F32, "row"),
            (full, F32, "row"),
            (full, BF16, "row"),
            ((rows, length, width), F32, "row"),
            ((rows, 8, length), F32, "row"),
        ],
        (),
        cost(2e9, 8e6),
    )

    token_row = tokens.astype(F32)
    sent = jnp.concatenate([logits[0, :vocab], logits[1, :vocab], token_row, mask_row], axis=0)
    got = lax.ppermute(sent, "ctx", [(i, ctx - 1 - i) for i in range(ctx)])[:, ::-1]
    their_token = got[2 * vocab : 2 * vocab + 1]
    weight = float(length * ctx) * jnp.sum(species_hot[0] * scaled)
    unused_rows = jnp.zeros((8 - vocab, length), F32)
    their_mask = got[2 * vocab + 1 :]
    pack = jnp.stack(
        [
            jnp.concatenate(
                [
                    logits[0, :vocab] + complement(got[vocab : 2 * vocab]),
                    unused_rows,
                    token_row,
                    weight * mask_row,
                    mask_row,
                ]
            ),
            jnp.concatenate(
                [
                    logits[1, :vocab] + complement(got[:vocab]),
                    unused_rows,
                    jnp.where(their_token < 4.0, 3.0 - their_token, their_token),
                    weight * their_mask,
                    their_mask,
                ]
            ),
        ]
    )
    ce, d_res, d_mix, d_left, d_right, d_gate, d_state = call(
        functools.partial(head_kernel, vocab=vocab),
        "head",
        [
            (proj, "row"),
            (pack, "row"),
            (res, "row"),
            (out_left, "row"),
            (out_right, "row"),
            (bias, "all"),
            (alog, "all"),
            (gain, "all"),
            (w_out, "all"),
            (final, "all"),
            (head, "all"),
        ],
        [
            ((rows, 1, length), F32, "row"),
            ((rows, length, width), F32, "row"),
            ((rows, length, width), BF16, "row"),
            (full, BF16, "row"),
            (full, BF16, "row"),
            (full, BF16, "row"),
            (state_shape, BF16, "dir"),
        ],
        [wide, wide],
        cost(2e9, 8e6),
    )
    ce_sums = butterfly_sum(jnp.sum(ce[0], axis=1, keepdims=True) * species_hot)[0]
    d_mix_flat = d_mix.reshape(flat, width)
    d_gate_flat = d_gate.reshape(flat, INNER)
    following = scan_blocks(d_state[::-1], rounds)[::-1]
    d_val, d_key, d_read, d_a, d_dt = call(
        adjoint_kernel,
        "adjoint",
        [
            (proj, "row"),
            (carry, "dir"),
            (d_left, "row"),
            (d_right, "row"),
            (bias, "all"),
            (alog, "all"),
            (skip, "all"),
        ],
        [
            (full, F32, "row"),
            ((rows, length, STATE), F32, "row"),
            ((rows, length, STATE), F32, "row"),
            ((rows, length, HEADS), F32, "row"),
            ((rows, length, HEADS), F32, "row"),
        ],
        [((HEADS, length), F32), ((HEADS, length), F32), wide, wide],
        cost(8e9, 6e6),
    )
    early = [weight_grad(nsum.reshape(flat, INNER), d_mix_flat), weight_grad(hidden_flat, d_gate_flat)]
    early = share_rows(
        jnp.concatenate([early[0][0], early[1][0]], axis=1),
        jnp.concatenate([early[0][1], early[1][1]], axis=1),
    )
    grad_hidden = mm(d_gate_flat, w_in[:, INNER : 2 * INNER], 1, 1) + d_res.reshape(flat, width)
    (d_rest,) = call(
        finish_kernel,
        "finish",
        [
            (proj, "row"),
            (carry, "dir"),
            (following, "dir"),
            (d_val, "row"),
            (d_key, "row"),
            (d_read, "row"),
            (d_a, "row"),
            (d_dt, "row"),
            (bias, "all"),
            (alog, "all"),
        ],
        [((rows, length, INNER + 2 * STATE + HEADS), BF16, "row")],
        [wide, wide],
        cost(2e9, 5e6),
    )
    d_rest = d_rest.reshape(flat, -1)
    late = share_rows(*weight_grad(hidden_flat, d_rest))
    grad_hidden = (
        grad_hidden
        + mm(d_rest[:, :INNER], w_in[:, :INNER], 1, 1)
        + mm(d_rest[:, INNER:], w_in[:, 2 * INNER :], 1, 1)
    ).astype(BF16)
    grad_hidden = grad_hidden.reshape(rows, length, width)
    grad_w_in = jnp.concatenate([late[:, :INNER], early[:, width:], late[:, INNER:]], axis=1)
    grad_w_out = early[:, :width]
    loss = jnp.sum(scaled * ce_sums + log_var).reshape(1)
    grad_log_var = 1.0 - scaled * ce_sums
    return (loss, grad_log_var, grad_hidden[:1], grad_hidden[1:], grad_w_in, grad_w_out)


def solution(mesh):
    return jax.shard_map(
        on_device,
        mesh=mesh,
        in_specs=(
            P(("groups", "dp"), "ctx", None),
            P(("groups", "dp"), "ctx", None),
            P(("groups", "dp"), "ctx"),
            P(("groups", "dp"), "ctx"),
            P(("groups", "dp")),
            P(),
            P(),
            P(),
            P(),
            P(),
            P(),
            P(),
            P(),
            P(),
        ),
        out_specs=(
            P("groups"),
            P("groups"),
            P(("groups", "dp"), "ctx", None),
            P(("groups", "dp"), "ctx", None),
            P(("groups", "dp", "ctx"), None),
            P(("groups", "dp", "ctx"), None),
        ),
        check_vma=False,
    )
```

time: 751 us -> 218 us (0.29); the launches traced: 743 us -> 218 us
  waiting for transfers between devices: 365 us -> 73.2 us
  blocking collectives: 108 us -> 0 us
  matrix products: 89.6 us -> 16.6 us
  other arithmetic: 88.3 us -> 19.7 us
  local copies, waits for them, and re-layouts: 66.4 us -> 32.7 us
  starting transfers between devices: 7.64 us -> 40.2 us
  Pallas kernels: 0 us -> 32.2 us
  between operations: 16.8 us -> 2.94 us
    all_gather x4 -> x0, waiting for transfers between devices: 217 us -> none  [the longest x2 147 us: prefix(): everything = jax.tree.map(lambda part: lax.all_gather(part, axis), array)]
    reduce_scatter x2 -> x0, waiting for transfers between devices: 98.5 us -> none  [the longest x1 98.5 us: on_device(): lax.psum_scatter(lax.dot_general(piece, d_proj_b, (((0,), (0,)), ((), ())...]
    all_gather x4 -> x0, blocking collectives: 76.7 us -> none  [the longest x2 40.2 us: prefix(): everything = jax.tree.map(lambda part: lax.all_gather(part, axis), array)]
    dot_general x32 -> x10, matrix products: 89.6 us -> 16.6 us  [mm(): lax.dot_general(a, b, (((ca,), (cb,)), ((), ())), precision=precision, pr...]
    select_n x16 -> x3, other arithmetic: 33.2 us -> 0.07 us  [the longest x2 0.06 us: scan_blocks(): jnp.where(upper, total[1], total[0])]
    ppermute x6 -> x31, starting transfers between devices: 7.4 us -> 40.2 us  [the longest x30 37.9 us: partner(): lax.ppermute(array, axis, [(i, i ^ 1 << bit) for i in range(lax.axis_size...]
    pallas_call x0 -> x6, Pallas kernels: none -> 32.2 us  [call(): pl.pallas_call(kernel, name=name, grid=(2,), in_specs=[specs[kind](array....]
    psum x1 -> x0, blocking collectives: 31.5 us -> none  [on_device(): counts = lax.psum(counts_local, ('dp', 'ctx'))]
  transfers between devices with their start and end apart: 12 -> 31, of which waited for: 10 -> 19; matrix products, arithmetic and copies ran while one was open for 22% -> 23% of each run, Pallas kernels for 0% -> 8%
where the time goes in v1:
time: 218 us
  waiting for transfers between devices  73.2 us (34%)
  starting transfers between devices  40.2 us (18%)
  local copies, waits for them, and re-layouts  32.7 us (15%)
  Pallas kernels  32.2 us (15%)
  other arithmetic  19.7 us (9%)
  matrix products  16.6 us (8%)
  between operations  2.94 us (1%)
    ppermute x30, waiting for transfers between devices, partner(): lax.ppermute(array, axis, [(i, i ^ 1 << bit) for i in range(lax.axis_size...  69 us
    ppermute x30, starting transfers between devices, partner(): lax.ppermute(array, axis, [(i, i ^ 1 << bit) for i in range(lax.axis_size...  37.9 us
    pallas_call x6, Pallas kernels, call(): pl.pallas_call(kernel, name=name, grid=(2,), in_specs=[specs[kind](array....  32.2 us
    dot_general x10, matrix products, mm(): lax.dot_general(a, b, (((ca,), (cb,)), ((), ())), precision=precision, pr...  16.6 us
    unnamed x95, local copies, waits for them, and re-layouts  15.7 us
    add x12, other arithmetic, share_rows(): part = keep + partner(send, 'ctx', bit).astype(F32)  4.54 us
  transfers between devices with their start and end apart: 31, of which 19 were waited for; matrix products, arithmetic and copies ran while one was open for 23% of the time, Pallas kernels for 8%

profile of v1, /device:TPU:0, one launch (start us, length us, event | category | flops | bytes accessed | tf_op | source)
XLA Modules:
  0.0 217.6 jit_solution(16456929003225076383)
XLA Ops:
  5.7 4.6 %convolution_convert_fusion = bf16[256,2192]{0,1:T(8,128)(2,1)} fusion(bf16[256,1024]{1,0:T(8,128)(2,1)S(1)} %bitcast.155, bf16[1024,2192]{0,1:T(8,128)(2,1)} %param.19), kind=kOutput, calls=%fused_computation.1 | convolution fusion | flops 1149800448 | bytes 6135808 | tf_op jit(solution)/shard_map/dot_general | solution.py:25
  12.0 2.5 %states.1 = (bf16[2,2,64,1024]{3,2,1,0:T(8,128)(2,1)S(1)}, f32[2,1,1024]{2,1,0:T(1,128)S(1)}) custom-call(bf16[2,128,2192]{2,1,0:T(8,128)(2,1)S(1)} %bitcast.166, f32[1,16]{1,0:T(1,128)S(1)} %bitcast.181, f32[1,16]{1,0:T(1,128)S(1)} %bitcast.187), custom_call_target="tpu_custom_call" | custom-call | flops 1000000000 | bytes 3000000 | tf_op jit(solution)/shard_map/states/pallas_call | solution.py:408
  14.5 2.6 %collective-permute-start.4 = (bf16[2,2,64,1024]{3,2,1,0:T(8,128)(2,1)S(1)}, bf16[2,2,64,1024]{3,2,1,0:T(8,128)(2,1)S(1)}, u32[]{:S(2)}, u32[]{:S(2)}) collective-permute-start(bf16[2,2,64,1024]{3,2,1,0:T(8,128)(2,1)S(1)} %get-tuple-element.27), channel_id=1, source_target_pairs={{0,1},{1,0},{2,3},{3,2},{4,5},{5,4},{6,7},{7,6},{8,9},{9,8},{10,11... | collective-permute-start | bytes 1572872 | tf_op jit(solution)/shard_map/ppermute | solution.py:432
  17.2 2.6 %local.1 = (f32[2,128,1024]{2,1,0:T(8,128)S(1)}, f32[2,128,1024]{2,1,0:T(8,128)S(1)}) custom-call(bf16[2,128,2192]{2,1,0:T(8,128)(2,1)S(1)} %bitcast.167, f32[1,16]{1,0:T(1,128)S(1)} %bitcast.182, f32[1,16]{1,0:T(1,128)S(1)} %bitcast.188, f32[1,16]{1,0:T(1,128)S(1)} %bitcast.179), custom_call_target="tpu_custom_call" | custom-call | flops 4000000000 | bytes 4000000 | tf_op jit(solution)/shard_map/local/pallas_call | solution.py:408
  24.5 5.4 %collective-permute-done.1 = f32[1,8]{1,0:T(1,128)S(1)} collective-permute-done((f32[1,8]{1,0:T(1,128)S(1)}, f32[1,8]{1,0:T(1,128)S(1)}, u32[]{:S(2)}, u32[]{:S(2)}) %collective-permute-start.1) | collective-permute-done | bytes 64 | tf_op jit(solution)/shard_map/ppermute | solution.py:432
  34.2 2.8 %collective-permute-start.3 = (f32[1,8]{1,0:T(1,128)S(1)}, f32[1,8]{1,0:T(1,128)S(1)}, u32[]{:S(2)}, u32[]{:S(2)}) collective-permute-start(f32[1,8]{1,0:T(1,128)S(1)} %add.174), channel_id=1, source_target_pairs={{0,4},{1,5},{2,6},{3,7},{4,0},{5,1},{6,2},{7,3},{8,12},{9,13},{10,... | collective-permute-start | bytes 104 | tf_op jit(solution)/shard_map/ppermute | solution.py:432
  42.8 10.1 %collective-permute-done.6 = bf16[2,2,64,1024]{3,2,1,0:T(8,128)(2,1)S(1)} collective-permute-done((bf16[2,2,64,1024]{3,2,1,0:T(8,128)(2,1)S(1)}, bf16[2,2,64,1024]{3,2,1,0:T(8,128)(2,1)S(1)}, u32[]{:S(2)}, u32[]{:S(2)}) %collective-permute-start.6) | collective-permute-done | bytes 524320 | tf_op jit(solution)/shard_map/ppermute | solution.py:432
  54.7 8.7 %collective-permute-done.8 = bf16[2,64,1024]{2,1,0:T(8,128)(2,1)S(1)} collective-permute-done((bf16[2,64,1024]{2,1,0:T(8,128)(2,1)S(1)}, bf16[2,64,1024]{2,1,0:T(8,128)(2,1)S(1)}, u32[]{:S(2)}, u32[]{:S(2)}) %collective-permute-start.8) | collective-permute-done | bytes 262176 | tf_op jit(solution)/shard_map/ppermute | solution.py:432
  65.2 7.6 %out.1 = (f32[2,128,1024]{2,1,0:T(8,128)S(1)}, f32[2,128,1024]{2,1,0:T(8,128)S(1)}, bf16[2,128,1024]{2,1,0:T(8,128)(2,1)S(1)}, f32[2,128,1024]{2,1,0:T(8,128)S(1)}, f32[2,8,128]{2,1,0:T(8,128)S(1)}) custom-call(bf16[2,128,2192]{2,1,0:T(8,128)(2,1)} %bitcast.168, bf16[2,2,64,1024]{3,2,1,0:T(8,128)(2,1)S(1)} %fusion.13.carry_ref, ...), custom_call_target="tpu_custom_call" | custom-call | flops 2000000000 | bytes 8000000 | tf_op jit(solution)/shard_map/out/pallas_call | solution.py:408
  78.1 4.2 %collective-permute-done.9 = f32[12,128]{1,0:T(8,128)S(1)} collective-permute-done((f32[12,128]{1,0:T(8,128)S(1)}, f32[12,128]{1,0:T(8,128)S(1)}, u32[]{:S(2)}, u32[]{:S(2)}) %collective-permute-start.9) | collective-permute-done | bytes 6176 | tf_op jit(solution)/shard_map/ppermute | solution.py:603
  85.4 8.0 %head.1 = (f32[2,1,128]{2,1,0:T(1,128)S(1)}, f32[2,128,1024]{2,1,0:T(8,128)S(1)}, bf16[2,128,1024]{2,1,0:T(8,128)(2,1)S(1)}, bf16[2,128,1024]{2,1,0:T(8,128)(2,1...) custom-call(bf16[2,128,2192]{2,1,0:T(8,128)(2,1)} %bitcast.169, ...), custom_call_target="tpu_custom_call" | custom-call | flops 2000000000 | bytes 8000000 | tf_op jit(solution)/shard_map/head/pallas_call | solution.py:408
  103.9 8.1 %collective-permute-done.14 = bf16[2,2,64,1024]{3,2,1,0:T(8,128)(2,1)S(1)} collective-permute-done((bf16[2,2,64,1024]{3,2,1,0:T(8,128)(2,1)}, bf16[2,2,64,1024]{3,2,1,0:T(8,128)(2,1)S(1)}, u32[]{:S(2)}, u32[]{:S(2)}) %collective-permute-start.14) | collective-permute-done | bytes 524320 | tf_op jit(solution)/shard_map/ppermute | solution.py:432
  112.4 8.6 %adjoint.1 = (f32[2,128,1024]{2,1,0:T(8,128)S(1)}, f32[2,128,64]{2,1,0:T(8,128)S(1)}, f32[2,128,64]{2,1,0:T(8,128)S(1)}, f32[2,128,16]{2,1,0:T(8,128)S(1)}, f32[2,128,16]{2,1,0:T(8,128)S(1)}) custom-call(bf16[2,128,2192]{2,1,0:T(8,128)(2,1)S(1)} %bitcast.170, bf16[2,2,64,1024]{3,2,1,0:T(8,128)(2,1)S(1)} %copy-done.5, bf16[2,128,1024]{2,1,0:T(8,128)(2,1)S(1)} %copy-done.23, ...), custom_call_target="tpu_custom_call" | custom-call | flops 8000000000 | bytes 6000000 | tf_op jit(solution)/shard_map/adjoint/pallas_call | solution.py:408
  132.1 3.9 %collective-permute-start.13 = (f32[1,8]{1,0:T(1,128)S(1)}, f32[1,8]{1,0:T(1,128)S(1)}, u32[]{:S(2)}, u32[]{:S(2)}) collective-permute-start(f32[1,8]{1,0:T(1,128)S(1)} %add.184), channel_id=1, source_target_pairs={{0,4},{1,5},{2,6},{3,7},{4,0},{5,1},{6,2},{7,3},{8,12},{9,13},{10,... | collective-permute-start | bytes 104 | tf_op jit(solution)/shard_map/ppermute | solution.py:432
  136.0 4.0 %collective-permute-done.13 = f32[1,8]{1,0:T(1,128)S(1)} collective-permute-done((f32[1,8]{1,0:T(1,128)S(1)}, f32[1,8]{1,0:T(1,128)S(1)}, u32[]{:S(2)}, u32[]{:S(2)}) %collective-permute-start.13) | collective-permute-done | bytes 64 | tf_op jit(solution)/shard_map/ppermute | solution.py:432
  147.3 3.0 %finish.1 = bf16[2,128,1168]{2,1,0:T(8,128)(2,1)S(1)} custom-call(bf16[2,128,2192]{2,1,0:T(8,128)(2,1)S(1)} %bitcast.171, bf16[2,2,64,1024]{3,2,1,0:T(8,128)(2,1)S(1)} %copy-done.6, bf16[2,2,64,1024]{3,2,1,0:T(8,128)(2,1)S(1)} %rev.16.next_ref, f32[2,128,1024]{2,1,0:T(8,128)S(1)} %copy-done.27, f32[2,128,64]{2,1,0:T(8,128)S(1)} %get-tuple-element.42.dkey_in, ...), custom_call_target="tpu_custom_call" | custom-call | flops 2000000000 | bytes 5000000 | tf_op jit(solution)/shard_map/finish/pallas_call | solution.py:408
  150.9 2.4 %fusion = f32[256,1024]{1,0:T(8,128)S(1)} fusion(bf16[1024,2192]{0,1:T(8,128)(2,1)} %param.19, bf16[256,1168]{1,0:T(8,128)(2,1)S(1)} %bitcast.161), kind=kOutput, calls=%fused_computation.5 | convolution fusion | flops 536870912 | bytes 3670016 | tf_op jit(solution)/shard_map/dot_general | solution.py:25
  153.3 2.5 %fusion.7 = f32[256,1024]{1,0:T(8,128)S(1)} fusion(f32[256,1024]{1,0:T(8,128)S(1)} %fusion, f32[256,1024]{1,0:T(8,128)S(1)} %bitcast.172, bf16[256,1024]{1,0:T(8,128)(2,1)S(1)} %bitcast.154, bf16[1024,2192]{0,1:T(8,128)(2,1)} %param.19), kind=kOutput, calls=%fused_computation.13 | convolution fusion | flops 537395200 | bytes 5767168 | tf_op jit(solution)/shard_map/dot_general | solution.py:25
  158.1 2.5 %maximum_add_fusion = f32[512,2048]{1,0:T(8,128)S(1)} fusion(f32[512,1024]{1,0:T(8,128)S(1)} %copy-done.34, f32[512,1024]{1,0:T(8,128)S(1)} %copy-done.35, bf16[512,2048]{1,0:T(8,128)(2,1)} %collective-permute-done.24), kind=kLoop, calls=%fused_computation | loop fusion | flops 3145728 | bytes 10485760 | tf_op jit(solution)/shard_map/add | solution.py:477
  166.8 3.0 %copy.30 = f32[512,656]{1,0:T(8,128)} copy(f32[512,656]{0,1:T(8,128)} %slice.155) | data formatting | bytes 2686976 | tf_op jit(solution)/shard_map/slice | solution.py:486
  185.0 4.5 %collective-permute-done.21 = bf16[2,2,64,656]{3,2,1,0:T(8,128)(2,1)} collective-permute-done((bf16[2,2,64,656]{3,2,1,0:T(8,128)(2,1)S(1)}, bf16[2,2,64,656]{3,2,1,0:T(8,128)(2,1)}, u32[]{:S(2)}, u32[]{:S(2)}) %collective-permute-start.21) | collective-permute-done | bytes 335904 | tf_op jit(solution)/shard_map/ppermute | solution.py:432
  194.2 6.8 %collective-permute-done.29 = bf16[2,64,1024]{2,1,0:T(8,128)(2,1)S(1)} collective-permute-done((bf16[2,64,1024]{2,1,0:T(8,128)(2,1)S(1)}, bf16[2,64,1024]{2,1,0:T(8,128)(2,1)S(1)}, u32[]{:S(2)}, u32[]{:S(2)}) %collective-permute-start.29) | collective-permute-done | bytes 262176 | tf_op jit(solution)/shard_map/ppermute | solution.py:432
  203.5 3.0 %collective-permute-start.30 = (bf16[64,1024]{1,0:T(8,128)(2,1)S(1)}, bf16[64,1024]{1,0:T(8,128)(2,1)S(1)}, u32[]{:S(2)}, u32[]{:S(2)}) collective-permute-start(bf16[64,1024]{1,0:T(8,128)(2,1)S(1)} %fusion.51), channel_id=1, source_target_pairs={{0,4},{1,5},{2,6},{3,7},{4,0},{5,1},{6,2},{7,3},{8,12},{9,13},{10,... | collective-permute-start | bytes 393224 | tf_op jit(solution)/shard_map/ppermute | solution.py:432
  206.4 5.4 %collective-permute-done.20 = bf16[64,512]{1,0:T(8,128)(2,1)S(1)} collective-permute-done((bf16[64,512]{1,0:T(8,128)(2,1)S(1)}, bf16[64,512]{1,0:T(8,128)(2,1)S(1)}, u32[]{:S(2)}, u32[]{:S(2)}) %collective-permute-start.20) | collective-permute-done | bytes 65568 | tf_op jit(solution)/shard_map/ppermute | solution.py:432
  (239 shorter events, 98.0 us)
Async XLA Ops:
  3.2 18.6 %collective-permute-start = (f32[1,8]{1,0:T(1,128)S(1)}, f32[1,8]{1,0:T(1,128)S(1)}, u32[]{:S(2)}, u32[]{:S(2)}) collective-permute-start(f32[1,8]{1,0:T(1,128)S(1)} %compare_select_fusion.3), channel_id=1, source_target_pairs={{0,8},{8,0},{1,9},{9,1},{2,10},{10,2},{3,11},{11,3},{4,12},{12,4},... | collective-permute-start | bytes 104 | tf_op jit(solution)/shard_map/ppermute | solution.py:432
  14.5 26.4 %collective-permute-start.4 = (bf16[2,2,64,1024]{3,2,1,0:T(8,128)(2,1)S(1)}, bf16[2,2,64,1024]{3,2,1,0:T(8,128)(2,1)S(1)}, u32[]{:S(2)}, u32[]{:S(2)}) collective-permute-start(bf16[2,2,64,1024]{3,2,1,0:T(8,128)(2,1)S(1)} %get-tuple-element.27), channel_id=1, source_target_pairs={{0,1},{1,0},{2,3},{3,2},{4,5},{5,4},{6,7},{7,6},{8,9},{9,8},{10,11... | collective-permute-start | bytes 1572872 | tf_op jit(solution)/shard_map/ppermute | solution.py:432
  17.0 20.0 %collective-permute-start.5 = (f32[2,1,1024]{2,1,0:T(1,128)S(1)}, f32[2,1,1024]{2,1,0:T(1,128)S(1)}, u32[]{:S(2)}, u32[]{:S(2)}) collective-permute-start(f32[2,1,1024]{2,1,0:T(1,128)S(1)} %get-tuple-element.28), channel_id=1, source_target_pairs={{0,1},{1,0},{2,3},{3,2},{4,5},{5,4},{6,7},{7,6},{8,9},{9,8},{10,11... | collective-permute-start | bytes 24584 | tf_op jit(solution)/shard_map/ppermute | solution.py:432
  34.2 19.1 %collective-permute-start.3 = (f32[1,8]{1,0:T(1,128)S(1)}, f32[1,8]{1,0:T(1,128)S(1)}, u32[]{:S(2)}, u32[]{:S(2)}) collective-permute-start(f32[1,8]{1,0:T(1,128)S(1)} %add.174), channel_id=1, source_target_pairs={{0,4},{1,5},{2,6},{3,7},{4,0},{5,1},{6,2},{7,3},{8,12},{9,13},{10,... | collective-permute-start | bytes 104 | tf_op jit(solution)/shard_map/ppermute | solution.py:432
  41.1 11.8 %collective-permute-start.6 = (bf16[2,2,64,1024]{3,2,1,0:T(8,128)(2,1)S(1)}, bf16[2,2,64,1024]{3,2,1,0:T(8,128)(2,1)S(1)}, u32[]{:S(2)}, u32[]{:S(2)}) collective-permute-start(bf16[2,2,64,1024]{3,2,1,0:T(8,128)(2,1)S(1)} %fusion.15), channel_id=1, source_target_pairs={{0,2},{1,3},{2,0},{3,1},{4,6},{5,7},{6,4},{7,5},{8,10},{9,11},{10,... | collective-permute-start | bytes 1572872 | tf_op jit(solution)/shard_map/ppermute | solution.py:432
  53.2 10.1 %collective-permute-start.8 = (bf16[2,64,1024]{2,1,0:T(8,128)(2,1)S(1)}, bf16[2,64,1024]{2,1,0:T(8,128)(2,1)S(1)}, u32[]{:S(2)}, u32[]{:S(2)}) collective-permute-start(bf16[2,64,1024]{2,1,0:T(8,128)(2,1)S(1)} %fusion.36), channel_id=1, source_target_pairs={{0,4},{1,5},{2,6},{3,7},{4,0},{5,1},{6,2},{7,3},{8,12},{9,13},{10,... | collective-permute-start | bytes 786440 | tf_op jit(solution)/shard_map/ppermute | solution.py:432
  96.5 26.4 %collective-permute-start.10 = (f32[1,8]{1,0:T(1,128)S(1)}, f32[1,8]{1,0:T(1,128)S(1)}, u32[]{:S(2)}, u32[]{:S(2)}) collective-permute-start(f32[1,8]{1,0:T(1,128)S(1)} %compare_select_fusion.2), channel_id=1, source_target_pairs={{0,8},{8,0},{1,9},{9,1},{2,10},{10,2},{3,11},{11,3},{4,12},{12,4},... | collective-permute-start | bytes 104 | tf_op jit(solution)/shard_map/ppermute | solution.py:432
  97.4 14.6 %collective-permute-start.14 = (bf16[2,2,64,1024]{3,2,1,0:T(8,128)(2,1)}, bf16[2,2,64,1024]{3,2,1,0:T(8,128)(2,1)S(1)}, u32[]{:S(2)}, u32[]{:S(2)}) collective-permute-start(bf16[2,2,64,1024]{3,2,1,0:T(8,128)(2,1)} %rev.15), channel_id=1, source_target_pairs={{0,1},{1,0},{2,3},{3,2},{4,5},{5,4},{6,7},{7,6},{8,9},{9,8},{10,11... | collective-permute-start | bytes 1572872 | tf_op jit(solution)/shard_map/ppermute | solution.py:432
  101.8 56.3 %collective-permute-start.24 = (bf16[512,2048]{1,0:T(8,128)(2,1)}, bf16[512,2048]{1,0:T(8,128)(2,1)}, u32[]{:S(2)}, u32[]{:S(2)}) collective-permute-start(bf16[512,2048]{1,0:T(8,128)(2,1)} %pad_maximum_fusion), channel_id=1, source_target_pairs={{0,8},{8,0},{1,9},{9,1},{2,10},{10,2},{3,11},{11,3},{4,12},{12,4},... | collective-permute-start | bytes 6291464 | tf_op jit(solution)/shard_map/ppermute | solution.py:432
  112.2 13.6 %collective-permute-start.15 = (bf16[2,2,64,1024]{3,2,1,0:T(8,128)(2,1)S(1)}, bf16[2,2,64,1024]{3,2,1,0:T(8,128)(2,1)S(1)}, u32[]{:S(2)}, u32[]{:S(2)}) collective-permute-start(bf16[2,2,64,1024]{3,2,1,0:T(8,128)(2,1)S(1)} %fusion.22), channel_id=1, source_target_pairs={{0,2},{1,3},{2,0},{3,1},{4,6},{5,7},{6,4},{7,5},{8,10},{9,11},{10,... | collective-permute-start | bytes 1572872 | tf_op jit(solution)/shard_map/ppermute | solution.py:432
  126.2 14.9 %collective-permute-start.16 = (bf16[2,64,1024]{2,1,0:T(8,128)(2,1)S(1)}, bf16[2,64,1024]{2,1,0:T(8,128)(2,1)S(1)}, u32[]{:S(2)}, u32[]{:S(2)}) collective-permute-start(bf16[2,64,1024]{2,1,0:T(8,128)(2,1)S(1)} %fusion.35), channel_id=1, source_target_pairs={{0,4},{1,5},{2,6},{3,7},{4,0},{5,1},{6,2},{7,3},{8,12},{9,13},{10,... | collective-permute-start | bytes 786440 | tf_op jit(solution)/shard_map/ppermute | solution.py:432
  132.1 7.9 %collective-permute-start.13 = (f32[1,8]{1,0:T(1,128)S(1)}, f32[1,8]{1,0:T(1,128)S(1)}, u32[]{:S(2)}, u32[]{:S(2)}) collective-permute-start(f32[1,8]{1,0:T(1,128)S(1)} %add.184), channel_id=1, source_target_pairs={{0,4},{1,5},{2,6},{3,7},{4,0},{5,1},{6,2},{7,3},{8,12},{9,13},{10,... | collective-permute-start | bytes 104 | tf_op jit(solution)/shard_map/ppermute | solution.py:432
  150.9 14.2 %collective-permute-start.17 = (bf16[512,1168]{0,1:T(8,128)(2,1)S(1)}, bf16[512,1168]{0,1:T(8,128)(2,1)S(1)}, u32[]{:S(2)}, u32[]{:S(2)}) collective-permute-start(bf16[512,1168]{0,1:T(8,128)(2,1)S(1)} %convolution_convert_fusion.1), channel_id=1, source_target_pairs={{0,8},{8,0},{1,9},{9,1},{2,10},{10,2},{3,11},{11,3},{4,12},{12,4},... | collective-permute-start | bytes 3588104 | tf_op jit(solution)/shard_map/ppermute | solution.py:432
  162.2 15.1 %collective-permute-start.25 = (bf16[2,2,64,1024]{3,2,1,0:T(8,128)(2,1)}, bf16[2,2,64,1024]{3,2,1,0:T(8,128)(2,1)}, u32[]{:S(2)}, u32[]{:S(2)}) collective-permute-start(bf16[2,2,64,1024]{3,2,1,0:T(8,128)(2,1)} %fusion.28), channel_id=1, source_target_pairs={{0,2},{1,3},{2,0},{3,1},{4,6},{5,7},{6,4},{7,5},{8,10},{9,11},{10,... | collective-permute-start | bytes 1572872 | tf_op jit(solution)/shard_map/ppermute | solution.py:432
  163.5 15.6 %collective-permute-start.28 = (bf16[2,2,64,1024]{3,2,0,1:T(8,128)(2,1)}, bf16[2,2,64,1024]{3,2,0,1:T(8,128)(2,1)}, u32[]{:S(2)}, u32[]{:S(2)}) collective-permute-start(bf16[2,2,64,1024]{3,2,0,1:T(8,128)(2,1)} %fusion.27), channel_id=1, source_target_pairs={{0,1},{1,0},{2,3},{3,2},{4,5},{5,4},{6,7},{7,6},{8,9},{9,8},{10,11... | collective-permute-start | bytes 1572872 | tf_op jit(solution)/shard_map/ppermute | solution.py:432
  172.0 17.6 %collective-permute-start.21 = (bf16[2,2,64,656]{3,2,1,0:T(8,128)(2,1)S(1)}, bf16[2,2,64,656]{3,2,1,0:T(8,128)(2,1)}, u32[]{:S(2)}, u32[]{:S(2)}) collective-permute-start(bf16[2,2,64,656]{3,2,1,0:T(8,128)(2,1)S(1)} %fusion.30), channel_id=1, source_target_pairs={{0,2},{1,3},{2,0},{3,1},{4,6},{5,7},{6,4},{7,5},{8,10},{9,11},{10,... | collective-permute-start | bytes 1007624 | tf_op jit(solution)/shard_map/ppermute | solution.py:432
  175.2 8.4 %collective-permute-start.18 = (bf16[2,2,64,512]{3,2,1,0:T(8,128)(2,1)S(1)}, bf16[2,2,64,512]{3,2,1,0:T(8,128)(2,1)S(1)}, u32[]{:S(2)}, u32[]{:S(2)}) collective-permute-start(bf16[2,2,64,512]{3,2,1,0:T(8,128)(2,1)S(1)} %fusion.32), channel_id=1, source_target_pairs={{0,1},{1,0},{2,3},{3,2},{4,5},{5,4},{6,7},{7,6},{8,9},{9,8},{10,11... | collective-permute-start | bytes 786440 | tf_op jit(solution)/shard_map/ppermute | solution.py:432
  178.6 14.0 %collective-permute-start.26 = (bf16[2,64,1024]{2,1,0:T(8,128)(2,1)S(1)}, bf16[2,64,1024]{2,1,0:T(8,128)(2,1)S(1)}, u32[]{:S(2)}, u32[]{:S(2)}) collective-permute-start(bf16[2,64,1024]{2,1,0:T(8,128)(2,1)S(1)} %fusion.33), channel_id=1, source_target_pairs={{0,4},{1,5},{2,6},{3,7},{4,0},{5,1},{6,2},{7,3},{8,12},{9,13},{10,... | collective-permute-start | bytes 786440 | tf_op jit(solution)/shard_map/ppermute | solution.py:432
  180.4 20.7 %collective-permute-start.29 = (bf16[2,64,1024]{2,1,0:T(8,128)(2,1)S(1)}, bf16[2,64,1024]{2,1,0:T(8,128)(2,1)S(1)}, u32[]{:S(2)}, u32[]{:S(2)}) collective-permute-start(bf16[2,64,1024]{2,1,0:T(8,128)(2,1)S(1)} %fusion.34), channel_id=1, source_target_pairs={{0,2},{1,3},{2,0},{3,1},{4,6},{5,7},{6,4},{7,5},{8,10},{9,11},{10,... | collective-permute-start | bytes 786440 | tf_op jit(solution)/shard_map/ppermute | solution.py:432
  183.7 19.6 %collective-permute-start.19 = (bf16[2,64,512]{2,1,0:T(8,128)(2,1)S(1)}, bf16[2,64,512]{2,1,0:T(8,128)(2,1)S(1)}, u32[]{:S(2)}, u32[]{:S(2)}) collective-permute-start(bf16[2,64,512]{2,1,0:T(8,128)(2,1)S(1)} %fusion.49), channel_id=1, source_target_pairs={{0,2},{1,3},{2,0},{3,1},{4,6},{5,7},{6,4},{7,5},{8,10},{9,11},{10,... | collective-permute-start | bytes 393224 | tf_op jit(solution)/shard_map/ppermute | solution.py:432
  190.7 21.2 %collective-permute-start.22 = (bf16[2,64,656]{2,1,0:T(8,128)(2,1)S(1)}, bf16[2,64,656]{2,1,0:T(8,128)(2,1)S(1)}, u32[]{:S(2)}, u32[]{:S(2)}) collective-permute-start(bf16[2,64,656]{2,1,0:T(8,128)(2,1)S(1)} %fusion.48), channel_id=1, source_target_pairs={{0,4},{1,5},{2,6},{3,7},{4,0},{5,1},{6,2},{7,3},{8,12},{9,13},{10,... | collective-permute-start | bytes 503816 | tf_op jit(solution)/shard_map/ppermute | solution.py:432
  192.6 21.0 %collective-permute-start.27 = (bf16[64,1024]{1,0:T(8,128)(2,1)S(1)}, bf16[64,1024]{1,0:T(8,128)(2,1)S(1)}, u32[]{:S(2)}, u32[]{:S(2)}) collective-permute-start(bf16[64,1024]{1,0:T(8,128)(2,1)S(1)} %fusion.50), channel_id=1, source_target_pairs={{0,1},{1,0},{2,3},{3,2},{4,5},{5,4},{6,7},{7,6},{8,9},{9,8},{10,11... | collective-permute-start | bytes 393224 | tf_op jit(solution)/shard_map/ppermute | solution.py:432
  203.4 8.5 %collective-permute-start.20 = (bf16[64,512]{1,0:T(8,128)(2,1)S(1)}, bf16[64,512]{1,0:T(8,128)(2,1)S(1)}, u32[]{:S(2)}, u32[]{:S(2)}) collective-permute-start(bf16[64,512]{1,0:T(8,128)(2,1)S(1)} %fusion.54), channel_id=1, source_target_pairs={{0,4},{1,5},{2,6},{3,7},{4,0},{5,1},{6,2},{7,3},{8,12},{9,13},{10,... | collective-permute-start | bytes 196616 | tf_op jit(solution)/shard_map/ppermute | solution.py:432
  203.5 10.7 %collective-permute-start.30 = (bf16[64,1024]{1,0:T(8,128)(2,1)S(1)}, bf16[64,1024]{1,0:T(8,128)(2,1)S(1)}, u32[]{:S(2)}, u32[]{:S(2)}) collective-permute-start(bf16[64,1024]{1,0:T(8,128)(2,1)S(1)} %fusion.51), channel_id=1, source_target_pairs={{0,4},{1,5},{2,6},{3,7},{4,0},{5,1},{6,2},{7,3},{8,12},{9,13},{10,... | collective-permute-start | bytes 393224 | tf_op jit(solution)/shard_map/ppermute | solution.py:432
  (52 other events, 278.6 us)

commit v2 on v1

v2 whole, which is shorter than its diff:
```python
import functools

import jax
import jax.numpy as jnp
from jax import lax
from jax.experimental import pallas as pl
from jax.experimental.pallas import tpu as pltpu
from jax.sharding import PartitionSpec as P

HEADS = 16
HEAD_DIM = 64
STATE = 64
INNER = HEADS * HEAD_DIM
PAIRS = HEADS // 2
LANES = 2 * HEAD_DIM
EPSILON = 1e-05

F32 = jnp.float32
BF16 = jnp.bfloat16
HIGH = lax.Precision.HIGHEST
VMEM_BYTES = 24 * 1024 * 1024


def mm(a, b, ca=1, cb=0, precision=None):
    return lax.dot_general(
        a, b, (((ca,), (cb,)), ((), ())), precision=precision, preferred_element_type=F32
    )


def iota(shape, dim):
    return lax.broadcasted_iota(jnp.int32, shape, dim)


def pair_wide(x, j):
    first = iota((x.shape[0], LANES), 1) < HEAD_DIM
    return jnp.where(first, x[:, 2 * j : 2 * j + 1], x[:, 2 * j + 1 : 2 * j + 2])


def lanes_of(j):
    return slice(j * LANES, (j + 1) * LANES)


def softplus(x):
    return jnp.maximum(x, 0.0) + jnp.log1p(jnp.exp(-jnp.abs(x)))


def tri(length, kind):
    rows, cols = iota((length, length), 0), iota((length, length), 1)
    return jnp.where(rows >= cols if kind == "ge" else rows > cols, 1.0, 0.0).astype(F32)


def head_sum(x):
    pick = (iota((INNER, HEADS), 0) // HEAD_DIM == iota((INNER, HEADS), 1)).astype(F32).astype(BF16)
    return mm(x.astype(BF16), pick)


def steps(proj_ref, bias_ref, alog_ref):
    raw = proj_ref[0, :, 2 * INNER + 2 * STATE :].astype(F32) + bias_ref[...]
    dt = softplus(raw)
    a = -jnp.exp(alog_ref[...]) * dt
    cum = mm(tri(a.shape[0], "ge"), a, precision=HIGH)
    return raw, dt, a, cum, cum - a, cum[-1:, :]


def turned(x):
    n = x.shape[0]
    eye = jnp.where(iota((n, n), 0) == iota((n, n), 1), 1.0, 0.0).astype(F32)
    return mm(x, eye, 0, 0, HIGH)


def turned_back(x):
    n = x.shape[0]
    eye = jnp.where(iota((n, n), 0) == iota((n, n), 1), 1.0, 0.0).astype(F32)
    return mm(x, eye, 0, 0, HIGH)


def keys_of(proj_ref):
    return proj_ref[0, :, 2 * INNER : 2 * INNER + STATE]


def reads_of(proj_ref):
    return proj_ref[0, :, 2 * INNER + STATE : 2 * INNER + 2 * STATE]


def front_kernel(
    fwd_ref,
    rc_ref,
    win_ref,
    bias_ref,
    alog_ref,
    mask_ref,
    species_ref,
    proj_ref,
    total_ref,
    small_ref,
    wide_l,
    wide_r,
):
    row = pl.program_id(0)
    hidden = jnp.where(row == 0, fwd_ref[0], rc_ref[0])
    proj_ref[0] = mm(hidden, win_ref[...], 1, 1).astype(BF16)
    unused, dt, a, cum, cex, tot = steps(proj_ref, bias_ref, alog_ref)
    w_l = jnp.exp(tot - cum) * dt
    w_r = jnp.exp(cex) * dt
    block = jnp.exp(tot)
    for j in range(PAIRS):
        s = lanes_of(j)
        v = proj_ref[0, :, s].astype(F32)
        wide_l[:, s] = (v * pair_wide(w_l, j)).astype(BF16)
        wide_r[:, s] = (v * pair_wide(w_r, j)).astype(BF16)
        small_ref[pl.ds(row, 1), :, s] = pair_wide(block, j)[None]
    keys = keys_of(proj_ref)
    total_ref[0, 0] = mm(keys, wide_l[...], 0, 0).astype(BF16)
    total_ref[0, 1] = mm(keys, wide_r[...], 0, 0).astype(BF16)

    @pl.when(row == 0)
    def _():
        scored = jnp.sum(mask_ref[...].astype(F32), axis=1, keepdims=True)
        small_ref[2] = jnp.where(iota((1, INNER), 1) == species_ref[...], scored, 0.0)


def local_kernel(proj_ref, bias_ref, alog_ref, skip_ref, left_ref, right_ref):
    unused, dt, a, cum, cex, tot = steps(proj_ref, bias_ref, alog_ref)
    n = cum.shape[0]
    cum_t, cex_t, dt_t = turned(cum), turned(cex), turned(dt)
    score = mm(reads_of(proj_ref), keys_of(proj_ref), 1, 1)
    t, s = iota((n, n), 0), iota((n, n), 1)
    first = iota((n, LANES), 1) < HEAD_DIM
    zero = jnp.zeros((n, LANES), BF16)
    for j in range(PAIRS):
        lanes = lanes_of(j)
        v = proj_ref[0, :, lanes]
        left, right = [], []
        for h in (2 * j, 2 * j + 1):
            gap = jnp.where(
                t >= s,
                cum[:, h : h + 1] - cum_t[h : h + 1, :],
                cex_t[h : h + 1, :] - cex[:, h : h + 1],
            )
            mix = jnp.exp(jnp.minimum(gap, 0.0)) * score * dt_t[h : h + 1, :]
            left.append(jnp.where(t >= s, mix, 0.0).astype(BF16))
            right.append(jnp.where(t <= s, mix, 0.0).astype(BF16))
        stacked = jnp.concatenate([jnp.where(first, v, zero), jnp.where(first, zero, v)], axis=0)
        skip = pair_wide(skip_ref[...], j) * v.astype(F32)
        left_ref[0, :, lanes] = mm(jnp.concatenate(left, axis=1), stacked) + skip
        right_ref[0, :, lanes] = mm(jnp.concatenate(right, axis=1), stacked) + skip


def out_kernel(
    proj_ref,
    carry_ref,
    left_in,
    right_in,
    fwd_ref,
    rc_ref,
    bias_ref,
    alog_ref,
    gain_ref,
    wout_ref,
    final_ref,
    head_ref,
    token_ref,
    mask_ref,
    left_ref,
    right_ref,
    nsum_ref,
    res_ref,
    sent_ref,
):
    row = pl.program_id(0)
    unused, dt, a, cum, cex, tot = steps(proj_ref, bias_ref, alog_ref)
    e_l, e_r = jnp.exp(cum), jnp.exp(tot - cex)
    reads = reads_of(proj_ref)
    from_l = mm(reads, carry_ref[0, 0])
    from_r = mm(reads, carry_ref[0, 1])
    for j in range(PAIRS):
        s = lanes_of(j)
        left_ref[0, :, s] = left_in[0, :, s] + pair_wide(e_l, j) * from_l[:, s]
        right_ref[0, :, s] = right_in[0, :, s] + pair_wide(e_r, j) * from_r[:, s]
    gate = proj_ref[0, :, INNER : 2 * INNER].astype(F32)
    gated = gate * jax.nn.sigmoid(gate)
    u_l = left_ref[0] * gated
    u_r = right_ref[0] * gated
    k_l = lax.rsqrt(jnp.mean(u_l * u_l, axis=1, keepdims=True) + EPSILON)
    k_r = lax.rsqrt(jnp.mean(u_r * u_r, axis=1, keepdims=True) + EPSILON)
    nsum = ((u_l * k_l + u_r * k_r) * gain_ref[...]).astype(BF16)
    nsum_ref[...] = nsum
    hidden = jnp.where(row == 0, fwd_ref[0], rc_ref[0])
    res = hidden.astype(F32) + mm(nsum, wout_ref[...])
    res_ref[0] = res
    normed = res * lax.rsqrt(jnp.mean(res * res, axis=1, keepdims=True) + EPSILON) * final_ref[...]
    sent_ref[pl.ds(row * 8, 8), :] = mm(head_ref[...], normed, 1, 1, HIGH)

    @pl.when(row == 0)
    def _():
        line = iota((8, normed.shape[0]), 0)
        sent_ref[16:24, :] = jnp.where(
            line == 0,
            token_ref[...].astype(F32),
            jnp.where(line == 1, mask_ref[...].astype(F32), 0.0),
        )


def head_kernel(
    proj_ref,
    sent_ref,
    got_ref,
    counts_ref,
    species_ref,
    logvar_ref,
    res_ref,
    left_ref,
    right_ref,
    bias_ref,
    alog_ref,
    gain_ref,
    wout_ref,
    final_ref,
    head_ref,
    ce_ref,
    dres_ref,
    dmix_ref,
    dleft_ref,
    dright_ref,
    dgate_ref,
    dstate_ref,
    wide_l,
    wide_r,
    *,
    vocab,
    loss_scale,
):
    row = pl.program_id(0)
    n = sent_ref.shape[1]
    mirror = jnp.where(iota((n, n), 0) + iota((n, n), 1) == n - 1, 1.0, 0.0).astype(F32)
    to, of = iota((8, 8), 0), iota((8, 8), 1)
    swap = jnp.where(jnp.where(to < 4, 3 - to, to) == of, 1.0, 0.0).astype(F32)
    other = mm(got_ref[pl.ds((1 - row) * 8, 8), :], mirror, precision=HIGH)
    total = sent_ref[pl.ds(row * 8, 8), :] + mm(swap, other, precision=HIGH)
    seen = mm(got_ref[16:24, :], mirror, precision=HIGH)
    their_token = jnp.where(seen[0:1] < 4.0, 3.0 - seen[0:1], seen[0:1])
    token = jnp.where(row == 0, sent_ref[16:17, :], their_token)
    mask = jnp.where(row == 0, sent_ref[17:18, :], seen[1:2])
    kinds = logvar_ref.shape[1]
    scaled = jnp.exp(-logvar_ref[...]) / jnp.maximum(counts_ref[0, :, :kinds], 1.0)
    chosen = iota((1, kinds), 1) == species_ref[...]
    weight = loss_scale * mask * jnp.sum(jnp.where(chosen, scaled, 0.0), axis=1, keepdims=True)
    which = iota(total.shape, 0)
    powers = jnp.where(which < vocab, jnp.exp(total), 0.0)
    expsum = jnp.sum(powers, axis=0, keepdims=True)
    hot = jnp.where(which.astype(F32) == token, 1.0, 0.0)

    @pl.when(row == 0)
    def _():
        ce = mask * (jnp.log(expsum) - jnp.sum(total * hot, axis=0, keepdims=True))
        ce = jnp.sum(ce, axis=1, keepdims=True)
        ce_ref[...] = jnp.where(iota((1, n), 1) == species_ref[...], ce, 0.0)

    d_logit = weight * (powers / expsum - hot)
    d_normed = mm(d_logit, head_ref[...], 0, 0, HIGH) * final_ref[...]
    res = res_ref[0]
    k = lax.rsqrt(jnp.mean(res * res, axis=1, keepdims=True) + EPSILON)
    d_res = k * (d_normed - res * (k * k * jnp.mean(d_normed * res, axis=1, keepdims=True)))
    dres_ref[0] = d_res
    d_mix = d_res.astype(BF16)
    dmix_ref[...] = d_mix
    d_sum = mm(d_mix, wout_ref[...], 1, 1) * gain_ref[...]
    gate = proj_ref[0, :, INNER : 2 * INNER].astype(F32)
    sig = jax.nn.sigmoid(gate)
    gated = gate * sig
    d_gated = jnp.zeros_like(gate)
    for source, target in ((left_ref, dleft_ref), (right_ref, dright_ref)):
        out = source[0]
        u = out * gated
        k = lax.rsqrt(jnp.mean(u * u, axis=1, keepdims=True) + EPSILON)
        d_u = k * (d_sum - u * (k * k * jnp.mean(d_sum * u, axis=1, keepdims=True)))
        target[0] = (d_u * gated).astype(BF16)
        d_gated = d_gated + d_u * out
    dgate_ref[...] = (d_gated * (sig + gated * (1.0 - sig))).astype(BF16)
    unused, dt, a, cum, cex, tot = steps(proj_ref, bias_ref, alog_ref)
    e_l, e_r = jnp.exp(cum), jnp.exp(tot - cex)
    for j in range(PAIRS):
        s = lanes_of(j)
        wide_l[:, s] = (dleft_ref[0, :, s].astype(F32) * pair_wide(e_l, j)).astype(BF16)
        wide_r[:, s] = (dright_ref[0, :, s].astype(F32) * pair_wide(e_r, j)).astype(BF16)
    reads = reads_of(proj_ref)
    dstate_ref[0, 1] = mm(reads, wide_l[...], 0, 0).astype(BF16)
    dstate_ref[0, 0] = mm(reads, wide_r[...], 0, 0).astype(BF16)


def adjoint_kernel(
    proj_ref,
    carry_ref,
    dleft_ref,
    dright_ref,
    bias_ref,
    alog_ref,
    skip_ref,
    dval_ref,
    dkey_ref,
    dread_ref,
    da_ref,
    ddt_ref,
    cols_l,
    cols_r,
    wide_l,
    wide_r,
):
    unused, dt, a, cum, cex, tot = steps(proj_ref, bias_ref, alog_ref)
    n = cum.shape[0]
    cum_t, cex_t = turned(cum), turned(cex)
    keys, reads = keys_of(proj_ref), reads_of(proj_ref)
    score = mm(keys, reads, 1, 1)
    s, t = iota((n, n), 0), iota((n, n), 1)
    first = iota((n, LANES), 1) < HEAD_DIM
    zero = jnp.zeros((n, LANES), BF16)
    d_score = jnp.zeros((n, n), F32)
    row_h = jnp.zeros((n, LANES), F32)
    row_l = jnp.zeros((n, LANES), F32)
    row_r = jnp.zeros((n, LANES), F32)
    e_l, e_r = jnp.exp(cum), jnp.exp(tot - cex)
    for j in range(PAIRS):
        lanes = lanes_of(j)
        v = proj_ref[0, :, lanes]
        d_l, d_r = dleft_ref[0, :, lanes], dright_ref[0, :, lanes]
        v_split = jnp.concatenate([jnp.where(first, v, zero), jnp.where(first, zero, v)], axis=0)
        d_mix = mm(v_split, jnp.concatenate([d_l, d_r], axis=0), 1, 1)
        mixes, sums_h, sums_l, sums_r = [], [], [], []
        for i, h in enumerate((2 * j, 2 * j + 1)):
            gap = jnp.where(
                t >= s,
                cum_t[h : h + 1, :] - cum[:, h : h + 1],
                cex[:, h : h + 1] - cex_t[h : h + 1, :],
            )
            decay = jnp.exp(jnp.minimum(gap, 0.0))
            step = dt[:, h : h + 1]
            d_l_mix = d_mix[i * n : (i + 1) * n, :n]
            d_r_mix = d_mix[i * n : (i + 1) * n, n:]
            scaled = decay * (
                jnp.where(t >= s, d_l_mix, 0.0) + jnp.where(t <= s, d_r_mix, 0.0)
            )
            with_step = scaled * step
            d_score = d_score + with_step
            flow = with_step * score
            flow_l = jnp.where(t > s, flow, 0.0)
            flow_r = jnp.where(t < s, flow, 0.0)
            cols_l[h : h + 1, :] = jnp.sum(flow_l, axis=0, keepdims=True)
            cols_r[h : h + 1, :] = jnp.sum(flow_r, axis=0, keepdims=True)
            sums_h.append((scaled * score).astype(BF16))
            sums_l.append(flow_l.astype(BF16))
            sums_r.append(flow_r.astype(BF16))
            mix = decay * score * step
            mixes.append(jnp.where(t >= s, mix, 0.0).astype(BF16))
            mixes.append(jnp.where(t <= s, mix, 0.0).astype(BF16))
        pick_rows, pick_cols = iota((2 * n, LANES), 0), iota((2 * n, LANES), 1)
        pick = (
            jnp.where(pick_cols == 2 * j + (pick_rows >= n).astype(jnp.int32), 1.0, 0.0)
            .astype(F32)
            .astype(BF16)
        )
        row_h = row_h + mm(jnp.concatenate(sums_h, axis=1), pick)
        row_l = row_l + mm(jnp.concatenate(sums_l, axis=1), pick)
        row_r = row_r + mm(jnp.concatenate(sums_r, axis=1), pick)
        d_split = jnp.concatenate(
            [
                jnp.where(first, d_l, zero),
                jnp.where(first, d_r, zero),
                jnp.where(first, zero, d_l),
                jnp.where(first, zero, d_r),
            ],
            axis=0,
        )
        both = d_l.astype(F32) + d_r.astype(F32)
        dval_ref[0, :, lanes] = (
            mm(jnp.concatenate(mixes, axis=1), d_split) + pair_wide(skip_ref[...], j) * both
        )
        wide_l[:, lanes] = (d_l.astype(F32) * pair_wide(e_l, j)).astype(BF16)
        wide_r[:, lanes] = (d_r.astype(F32) * pair_wide(e_r, j)).astype(BF16)
    carry_l, carry_r = carry_ref[0, 0], carry_ref[0, 1]
    d_score_b = d_score.astype(BF16)
    dkey_ref[0] = mm(d_score_b, reads)
    dread_ref[0] = (
        mm(d_score_b, keys, 0, 0)
        + mm(wide_l[...], carry_l, 1, 1)
        + mm(wide_r[...], carry_r, 1, 1)
    )
    d_cum = (
        head_sum(wide_l[...].astype(F32) * mm(reads, carry_l))
        + turned_back(cols_l[...])
        - row_l[:, :HEADS]
    )
    d_rcum = head_sum(wide_r[...].astype(F32) * mm(reads, carry_r))
    d_cex = row_r[:, :HEADS] - turned_back(cols_r[...])
    ge, gt = tri(n, "ge"), tri(n, "gt")
    da_ref[0] = mm(ge, d_cum, 0, 0, HIGH) + mm(gt, d_cex, 0, 0, HIGH) + mm(ge, d_rcum, 1, 0, HIGH)
    ddt_ref[0] = row_h[:, :HEADS]


def finish_kernel(
    proj_ref,
    carry_ref,
    next_ref,
    dval_in,
    dkey_in,
    dread_in,
    da_in,
    ddt_in,
    bias_ref,
    alog_ref,
    dproj_ref,
    wide_l,
    wide_r,
):
    raw, dt, a, cum, cex, tot = steps(proj_ref, bias_ref, alog_ref)
    keys = keys_of(proj_ref)
    f_l, f_r = jnp.exp(tot - cum), jnp.exp(cex)
    w_l, w_r = f_l * dt, f_r * dt
    next_r, next_l = next_ref[0, 0], next_ref[0, 1]
    z_l, z_r = mm(keys, next_l), mm(keys, next_r)
    for j in range(PAIRS):
        s = lanes_of(j)
        v = proj_ref[0, :, s].astype(F32)
        wide_w_l, wide_w_r = pair_wide(w_l, j), pair_wide(w_r, j)
        dproj_ref[:, s] = (
            dval_in[0, :, s] + wide_w_l * z_l[:, s] + wide_w_r * z_r[:, s]
        ).astype(BF16)
        wide_l[:, s] = (v * wide_w_l).astype(BF16)
        wide_r[:, s] = (v * wide_w_r).astype(BF16)
    values = proj_ref[0, :, :INNER].astype(F32)
    dw_l, dw_r = head_sum(values * z_l), head_sum(values * z_r)
    d_key = dkey_in[0] + mm(wide_l[...], next_l, 1, 1) + mm(wide_r[...], next_r, 1, 1)
    dproj_ref[:, INNER : INNER + STATE] = d_key.astype(BF16)
    dproj_ref[:, INNER + STATE : INNER + 2 * STATE] = dread_in[0].astype(BF16)
    through = jnp.sum(
        next_l.astype(F32) * carry_ref[0, 0].astype(F32)
        + next_r.astype(F32) * carry_ref[0, 1].astype(F32),
        axis=0,
        keepdims=True,
    )
    through = head_sum(jnp.broadcast_to(through, (8, INNER)))[:1]
    q_l, q_r = dw_l * w_l, dw_r * w_r
    n = cum.shape[0]
    ge, gt = tri(n, "ge"), tri(n, "gt")
    d_tot = jnp.exp(tot) * through + jnp.sum(q_l, axis=0, keepdims=True)
    d_a = da_in[0] + mm(gt, q_r, 0, 0, HIGH) - mm(ge, q_l, 0, 0, HIGH) + d_tot
    d_dt = ddt_in[0] + dw_l * f_l + dw_r * f_r - d_a * jnp.exp(alog_ref[...])
    dproj_ref[:, INNER + 2 * STATE :] = (d_dt * jax.nn.sigmoid(raw)).astype(BF16)


def input_kernel(rest_ref, gate_ref, win_ref, dres_ref, fwd_ref, rc_ref):
    row = pl.program_id(0)
    grad = (
        dres_ref[0]
        + mm(gate_ref[...], win_ref[INNER : 2 * INNER])
        + mm(rest_ref[:, :INNER], win_ref[:INNER])
        + mm(rest_ref[:, INNER:], win_ref[2 * INNER :])
    ).astype(BF16)

    @pl.when(row == 0)
    def _():
        fwd_ref[0] = grad

    @pl.when(row == 1)
    def _():
        rc_ref[0] = grad


def weight_kernel(
    place_ref, rows_ref, their_rows_ref, cot_ref, their_cot_ref, send_ref, keep_ref, both, *, block
):
    half = their_rows_ref.shape[1]
    mine = jnp.where(place_ref[0] == 0, rows_ref[:, :half], rows_ref[:, half:])
    both[...] = mm(mine, cot_ref[...], 0, 0) + mm(their_rows_ref[...], their_cot_ref[...], 0, 0)
    side = place_ref[1]
    for i in range(keep_ref.shape[0] // block):
        here = slice(i * block, (i + 1) * block)
        keep_ref[here, :] = both[pl.ds((2 * i + side) * block, block), :]
        send_ref[here, :] = both[pl.ds((2 * i + 1 - side) * block, block), :].astype(BF16)


def by_row(shape):
    rest = (0,) * (len(shape) - 1)
    return pl.BlockSpec((1,) + tuple(shape[1:]), lambda g: (g,) + rest)


def by_half(shape):
    return pl.BlockSpec((shape[0] // 2, shape[1]), lambda g: (g, 0))


def whole(shape):
    zeros = (0,) * len(shape)
    return pl.BlockSpec(tuple(shape), lambda g: zeros)


FAR = ("row hbm", "half hbm", "all hbm")


def far(array):
    return pltpu.with_memory_space_constraint(array, pltpu.HBM)


def placed(shape, dtype, kind):
    return pltpu.HBM(shape, dtype) if kind in FAR else jax.ShapeDtypeStruct(shape, dtype)


def call(kernel, name, operands, results, scratch=(), cost=None):
    specs = {"row": by_row, "half": by_half, "all": whole}
    specs.update({kind + " hbm": spec for kind, spec in list(specs.items())})
    return pl.pallas_call(
        kernel,
        name=name,
        grid=(2,),
        in_specs=[specs[kind](array.shape) for array, kind in operands],
        out_specs=[specs[kind](shape) for shape, dtype, kind in results],
        out_shape=[placed(shape, dtype, kind) for shape, dtype, kind in results],
        scratch_shapes=[pltpu.VMEM(shape, dtype) for shape, dtype in scratch],
        compiler_params=pltpu.CompilerParams(
            dimension_semantics=("arbitrary",), vmem_limit_bytes=VMEM_BYTES
        ),
        cost_estimate=cost,
    )(*[far(array) if kind in FAR else array for array, kind in operands])


def cost(flops, moved):
    return pl.CostEstimate(flops=int(flops), transcendentals=0, bytes_accessed=int(moved))


def bits_of(axis):
    return lax.axis_size(axis).bit_length() - 1


def partner(array, axis, bit):
    return lax.ppermute(array, axis, [(i, i ^ (1 << bit)) for i in range(lax.axis_size(axis))])


def together(*arrays):
    return lax.optimization_barrier(arrays)


class Sum:
    def __init__(self, array):
        self.array = array
        self.left = [("ctx", bit) for bit in range(bits_of("ctx"))]
        self.left += [("dp", bit) for bit in range(bits_of("dp"))]

    def step(self):
        if self.left:
            axis, bit = self.left.pop(0)
            self.array = self.array + partner(self.array, axis, bit)

    def finish(self):
        while self.left:
            self.step()
        return self.array


def is_upper(bit):
    return ((lax.axis_index("ctx") >> bit) & 1) == 1


def factors(upper, lead_l, lead_r, decay, theirs):
    one, zero = jnp.ones_like(decay), jnp.zeros_like(decay)
    into = jnp.stack([jnp.where(upper, lead_l, zero), jnp.where(upper, zero, lead_r)], axis=1)
    keep = jnp.stack([jnp.where(upper, one, theirs), jnp.where(upper, theirs, one)], axis=1)
    take = jnp.stack([jnp.where(upper, decay, one), jnp.where(upper, one, decay)], axis=1)
    return into, keep, take


def scan_round(total, entering, bit, last, into_keep_take, theirs):
    into, keep, take = into_keep_take
    theirs = theirs.astype(F32)
    if last:
        return None, entering + into * theirs[:, None]
    return (
        (keep * total.astype(F32) + take * theirs).astype(BF16),
        entering + into * theirs,
    )


def to_send(total, bit, last):
    return jnp.where(is_upper(bit), total[:, 1], total[:, 0]) if last else total


def scan_states(total, small):
    bits = bits_of("ctx")
    entering = jnp.zeros(total.shape, F32)
    rows = total.shape[0]
    lead_l = jnp.ones((rows, 1, INNER), F32)
    lead_r = lead_l
    rounds = []
    for bit in range(bits):
        last, upper = bit == bits - 1, is_upper(bit)
        sent, small = together(to_send(total, bit, last), small)
        theirs = partner(sent, "ctx", bit)
        theirs_small = partner(small, "ctx", bit)
        decay, their_decay = small[:rows], theirs_small[:rows]
        rounds.append(factors(upper, lead_l, lead_r, decay, their_decay))
        total, entering = scan_round(total, entering, bit, last, rounds[-1], theirs)
        lead_l = jnp.where(upper, lead_l * their_decay, lead_l)
        lead_r = jnp.where(upper, lead_r, lead_r * their_decay)
        small = jnp.concatenate([decay * their_decay, small[rows:] + theirs_small[rows:]], axis=0)
    return entering.astype(BF16), rounds, small[rows:]


def over_cores(array):
    return lax.ppermute(array, "dp", [(0, 1), (1, 0)])


def their_half(rows_of):
    half = rows_of.shape[1] // 2
    return over_cores(
        jnp.where(lax.axis_index("dp") == 0, rows_of[:, half:], rows_of[:, :half])
    )


class RowShare:
    def __init__(self, rows_of, theirs, cotangent):
        ctx = lax.axis_size("ctx")
        their_cot = over_cores(cotangent)
        place = jnp.stack([lax.axis_index("dp"), lax.axis_index("ctx") & 1]).astype(jnp.int32)
        half, cols = rows_of.shape[1] // 2, cotangent.shape[1]
        block = half // ctx
        vmem = pl.BlockSpec(memory_space=pltpu.VMEM)
        self.send, self.mine = pl.pallas_call(
            functools.partial(weight_kernel, block=block),
            name="weight",
            in_specs=[pl.BlockSpec(memory_space=pltpu.SMEM), vmem, vmem, vmem, vmem],
            out_specs=[vmem, vmem],
            out_shape=[
                jax.ShapeDtypeStruct((half // 2, cols), BF16),
                jax.ShapeDtypeStruct((half // 2, cols), F32),
            ],
            scratch_shapes=[pltpu.VMEM((half, cols), F32)],
            compiler_params=pltpu.CompilerParams(vmem_limit_bytes=VMEM_BYTES),
            cost_estimate=cost(1.2e9, 6e6),
        )(place, rows_of, theirs, cotangent, their_cot)
        self.bit = 0
        self.bits = bits_of("ctx")
        self.block = block

    def done(self):
        return self.bit == self.bits

    def pass_on(self, got):
        self.mine = self.mine + got.astype(F32)
        self.bit += 1
        if not self.done():
            cols = self.mine.shape[1]
            pairs = self.mine.reshape(-1, 2, self.block, cols)
            side = (lax.axis_index("ctx") >> self.bit) & 1
            self.send = lax.dynamic_index_in_dim(pairs, 1 - side, 1, False).astype(BF16)
            self.send = self.send.reshape(-1, cols)
            self.mine = lax.dynamic_index_in_dim(pairs, side, 1, False).reshape(-1, cols)


def on_device(
    h_fwd,
    h_rc,
    tokens,
    loss_mask,
    species,
    w_in,
    a_log,
    dt_bias,
    d_skip,
    norm_gain,
    w_out,
    final_gain,
    w_head,
    log_var,
):
    length, width = h_fwd.shape[1], h_fwd.shape[2]
    vocab, kinds = w_head.shape[0], log_var.shape[0]
    ctx = lax.axis_size("ctx")
    bits = bits_of("ctx")
    rows = 2
    flat = rows * length

    bias, alog, skip = dt_bias[None], a_log[None], d_skip[None]
    win_t = w_in.T
    gain, final, kind = norm_gain[None], final_gain[None], species[None]
    head = jnp.concatenate([w_head, jnp.zeros((8 - vocab, width), F32)], axis=0)

    state_shape = (rows, 2, STATE, INNER)
    wide = ((length, INNER), BF16)
    full = (rows, length, INNER)
    proj, total, small = call(
        front_kernel,
        "front",
        [
            (h_fwd, "all hbm"),
            (h_rc, "all hbm"),
            (win_t, "all hbm"),
            (bias, "all"),
            (alog, "all"),
            (loss_mask, "all"),
            (kind, "all"),
        ],
        [
            ((rows, length, w_in.shape[1]), BF16, "row hbm"),
            (state_shape, BF16, "row"),
            ((rows + 1, 1, INNER), F32, "all"),
        ],
        [wide, wide],
        cost(2e9, 7e6),
    )
    left_own, right_own = call(
        local_kernel,
        "local",
        [(proj, "row hbm"), (bias, "all"), (alog, "all"), (skip, "all")],
        [(full, F32, "row hbm"), (full, F32, "row hbm")],
        (),
        cost(4e9, 4e6),
    )
    carry, rounds, counts = scan_states(total, small)
    out_left, out_right, nsum, res, sent = call(
        out_kernel,
        "out",
        [
            (proj, "row hbm"),
            (carry, "row"),
            (left_own, "row hbm"),
            (right_own, "row hbm"),
            (h_fwd, "all hbm"),
            (h_rc, "all hbm"),
            (bias, "all"),
            (alog, "all"),
            (gain, "all"),
            (w_out, "all hbm"),
            (final, "all"),
            (head, "all"),
            (tokens, "all"),
            (loss_mask, "all"),
        ],
        [
            (full, F32, "row hbm"),
            (full, F32, "row hbm"),
            ((flat, INNER), BF16, "half"),
            ((rows, length, width), F32, "row hbm"),
            ((24, length), F32, "all"),
        ],
        (),
        cost(2e9, 8e6),
    )

    sent, counts = together(sent, counts)
    got = lax.ppermute(sent, "ctx", [(i, ctx - 1 - i) for i in range(ctx)])
    for bit in range(bits_of("dp")):
        counts = counts + partner(counts, "dp", bit)
    ce, d_res, d_mix, d_left, d_right, d_gate, d_state = call(
        functools.partial(head_kernel, vocab=vocab, loss_scale=float(length * ctx)),
        "head",
        [
            (proj, "row hbm"),
            (sent, "all"),
            (got, "all"),
            (counts, "all"),
            (kind, "all"),
            (log_var[None], "all"),
            (res, "row hbm"),
            (out_left, "row hbm"),
            (out_right, "row hbm"),
            (bias, "all"),
            (alog, "all"),
            (gain, "all"),
            (w_out, "all hbm"),
            (final, "all"),
            (head, "all"),
        ],
        [
            ((1, length), F32, "all"),
            ((rows, length, width), F32, "row hbm"),
            ((flat, width), BF16, "half"),
            (full, BF16, "row hbm"),
            (full, BF16, "row hbm"),
            ((flat, INNER), BF16, "half"),
            (state_shape, BF16, "row"),
        ],
        [wide, wide],
        cost(2e9, 8e6),
    )
    ce_sum = Sum(ce)
    hidden = jnp.concatenate([h_fwd[0], h_rc[0]], axis=0)
    hidden_theirs = their_half(hidden)

    entering = jnp.zeros(state_shape, F32)
    early, early_got = [], []
    for bit in range(bits):
        last = bit == bits - 1
        send = to_send(d_state, bit, last)
        if bit == 1:
            send, early[0].send, early[1].send, ce_sum.array = together(
                send, early[0].send, early[1].send, ce_sum.array
            )
        elif bit > 1:
            send, ce_sum.array = together(send, ce_sum.array)
        theirs = partner(send, "ctx", bit)
        if bit == 1:
            early_got = [partner(share.send, "ctx", 0) for share in early]
        if bit > 0:
            ce_sum.step()
        if last:
            for share, got in zip(early, early_got):
                share.pass_on(got)
            theirs, early[0].send, early[1].send = together(theirs, early[0].send, early[1].send)
        d_state, entering = scan_round(d_state, entering, bit, last, rounds[bit], theirs)
        if bit == 0:
            early = [
                RowShare(nsum, their_half(nsum), d_mix),
                RowShare(hidden, hidden_theirs, d_gate),
            ]
    following = entering.astype(BF16)
    d_val, d_key, d_read, d_a, d_dt = call(
        adjoint_kernel,
        "adjoint",
        [
            (proj, "row hbm"),
            (carry, "row"),
            (d_left, "row hbm"),
            (d_right, "row hbm"),
            (bias, "all"),
            (alog, "all"),
            (skip, "all"),
        ],
        [
            (full, F32, "row hbm"),
            ((rows, length, STATE), F32, "row"),
            ((rows, length, STATE), F32, "row"),
            ((rows, length, HEADS), F32, "row"),
            ((rows, length, HEADS), F32, "row"),
        ],
        [((HEADS, length), F32), ((HEADS, length), F32), wide, wide],
        cost(8e9, 6e6),
    )
    (d_rest,) = call(
        finish_kernel,
        "finish",
        [
            (proj, "row hbm"),
            (carry, "row"),
            (following, "row"),
            (d_val, "row hbm"),
            (d_key, "row"),
            (d_read, "row"),
            (d_a, "row"),
            (d_dt, "row"),
            (bias, "all"),
            (alog, "all"),
        ],
        [((flat, INNER + 2 * STATE + HEADS), BF16, "half")],
        [wide, wide],
        cost(2e9, 5e6),
    )
    late = RowShare(hidden, hidden_theirs, d_rest)
    late.send, d_rest = together(late.send, d_rest)
    grad_fwd, grad_rc = call(
        input_kernel,
        "input",
        [(d_rest, "half"), (d_gate, "half"), (win_t, "all hbm"), (d_res, "row hbm")],
        [(h_fwd.shape, BF16, "all"), (h_rc.shape, BF16, "all")],
        (),
        cost(2e9, 7e6),
    )
    while not late.done():
        shares = [share for share in early + [late] if not share.done()]
        ce_sum.array, *sends = together(ce_sum.array, *[share.send for share in shares])
        got = [partner(send, "ctx", share.bit) for share, send in zip(shares, sends)]
        ce_sum.step()
        if late.bit == 0:
            grad_fwd, grad_rc, *got = together(grad_fwd, grad_rc, *got)
        else:
            got = together(*got)
        for share, arrived in zip(shares, got):
            share.pass_on(arrived)
    ce_sums = ce_sum.finish()[0, :kinds]
    grad_w_in = jnp.concatenate(
        [late.mine[:, :INNER], early[1].mine, late.mine[:, INNER:]], axis=1
    )
    scaled = jnp.exp(-log_var) / jnp.maximum(counts[0, 0, :kinds], 1.0)
    loss = jnp.sum(scaled * ce_sums + log_var).reshape(1)
    grad_log_var = 1.0 - scaled * ce_sums
    return (loss, grad_log_var, grad_fwd, grad_rc, grad_w_in, early[0].mine)


def solution(mesh):
    return jax.shard_map(
        on_device,
        mesh=mesh,
        in_specs=(
            P(("groups", "dp"), "ctx", None),
            P(("groups", "dp"), "ctx", None),
            P(("groups", "dp"), "ctx"),
            P(("groups", "dp"), "ctx"),
            P(("groups", "dp")),
            P(),
            P(),
            P(),
            P(),
            P(),
            P(),
            P(),
            P(),
            P(),
        ),
        out_specs=(
            P("groups"),
            P("groups"),
            P(("groups", "dp"), "ctx", None),
            P(("groups", "dp"), "ctx", None),
            P(("groups", "dp", "ctx"), None),
            P(("groups", "dp", "ctx"), None),
        ),
        check_vma=False,
    )
```

time: 218 us -> 182 us (0.83)
  Pallas kernels: 32.2 us -> 55.9 us
  local copies, waits for them, and re-layouts: 32.7 us -> 12.3 us
  matrix products: 16.6 us -> 0 us
  starting transfers between devices: 40.2 us -> 30.8 us
  other arithmetic: 19.7 us -> 10.5 us
  waiting for transfers between devices: 73.2 us -> 70.1 us
    pallas_call x6 -> x7, Pallas kernels: 32.2 us -> 50.6 us  [call(): pl.pallas_call(kernel, name=name, grid=(2,), in_specs=[specs[kind](array....]
    dot_general x10 -> x0, matrix products: 16.6 us -> none  [mm(): lax.dot_general(a, b, (((ca,), (cb,)), ((), ())), precision=precision, pr...]
    ppermute x30 -> x23, starting transfers between devices: 37.9 us -> 26.3 us  [partner(): lax.ppermute(array, axis, [(i, i ^ 1 << bit) for i in range(lax.axis_size...]
    unnamed x95 -> x68, local copies, waits for them, and re-layouts: 15.7 us -> 5.25 us
    slice x13 -> x2, local copies, waits for them, and re-layouts: 8.54 us -> 0.03 us  [the longest x1 0.02 us: on_device(): late.mine[:, :INNER]]
    add x20 -> x17, other arithmetic: 9.62 us -> 1.9 us  [the longest x9 1.35 us: pass_on(): self.mine = self.mine + got.astype(F32)]
    pallas_call x0 -> x3, Pallas kernels: none -> 5.26 us  [__init__(): pl.pallas_call(functools.partial(weight_kernel, block=block), name='weigh...]
    convert_element_type x13 -> x6, local copies, waits for them, and re-layouts: 5.34 us -> 1.66 us  [pass_on(): self.send = lax.dynamic_index_in_dim(pairs, 1 - side, 1, False).astype(BF16)]
  transfers between devices with their start and end apart: 31 -> 29, of which waited for: 19 -> 15; matrix products, arithmetic and copies ran while one was open for 23% -> 6% of each run, Pallas kernels for 8% -> 12%
where the time goes in v2:
time: 182 us
  waiting for transfers between devices  70.1 us (39%)
  Pallas kernels  55.9 us (31%)
  starting transfers between devices  30.8 us (17%)
  local copies, waits for them, and re-layouts  12.3 us (7%)
  other arithmetic  10.5 us (6%)
  between operations  1.99 us (1%)
    ppermute x23, waiting for transfers between devices, partner(): lax.ppermute(array, axis, [(i, i ^ 1 << bit) for i in range(lax.axis_size...  68.3 us
    pallas_call x7, Pallas kernels, call(): pl.pallas_call(kernel, name=name, grid=(2,), in_specs=[specs[kind](array....  50.6 us
    ppermute x23, starting transfers between devices, partner(): lax.ppermute(array, axis, [(i, i ^ 1 << bit) for i in range(lax.axis_size...  26.3 us
    pallas_call x3, Pallas kernels, __init__(): pl.pallas_call(functools.partial(weight_kernel, block=block), name='weigh...  5.26 us
    unnamed x68, local copies, waits for them, and re-layouts  5.25 us
  transfers between devices with their start and end apart: 29, of which 15 were waited for; matrix products, arithmetic and copies ran while one was open for 6% of the time, Pallas kernels for 12%

profile of v2, /device:TPU:0, one launch (start us, length us, event | category | flops | bytes accessed | tf_op | source)
XLA Modules:
  0.0 181.5 jit_solution(9806177383641743923)
XLA Ops:
  3.3 8.7 %front.1 = (bf16[2,128,2192]{2,1,0:T(8,128)(2,1)}, bf16[2,2,64,1024]{3,2,1,0:T(8,128)(2,1)S(1)}, f32[3,1,1024]{2,1,0:T(1,128)S(1)}) custom-call(bf16[1,128,1024]{2,1,0:T(8,128)(2,1)} %fwd_ref.3, bf16[1,128,1024]{2,1,0:T(8,128)(2,1)} %rc_ref.3, bf16[2192,1024]{1,0:T(8,128)(2,1)} %bitcast.131, f32[1,16]{1,0:T(1,128)S(1)} %bitcast.100, f32[1,16]{1,0:T(1,128)S(1)} %bitcast.106, ...), custom_call_target="tpu_custom_call" | custom-call | flops 2000000000 | bytes 7000000 | tf_op jit(solution)/shard_map/front/pallas_call | solution.py:509
  11.9 3.0 %collective-permute-start = (bf16[2,2,64,1024]{3,2,1,0:T(8,128)(2,1)S(1)}, bf16[2,2,64,1024]{3,2,1,0:T(8,128)(2,1)S(1)}, u32[]{:S(2)}, u32[]{:S(2)}) collective-permute-start(bf16[2,2,64,1024]{3,2,1,0:T(8,128)(2,1)S(1)} %get-tuple-element.76), channel_id=1, source_target_pairs={{0,1},{1,0},{2,3},{3,2},{4,5},{5,4},{6,7},{7,6},{8,9},{9,8},{10,11... | collective-permute-start | bytes 1572872 | tf_op jit(solution)/shard_map/ppermute | solution.py:533
  15.0 4.6 %local.1 = (f32[2,128,1024]{2,1,0:T(8,128)}, f32[2,128,1024]{2,1,0:T(8,128)}) custom-call(bf16[2,128,2192]{2,1,0:T(8,128)(2,1)} %get-tuple-element.73.proj_ref, f32[1,16]{1,0:T(1,128)S(1)} %bitcast.101, f32[1,16]{1,0:T(1,128)S(1)} %bitcast.107, f32[1,16]{1,0:T(1,128)S(1)} %bitcast.98), custom_call_target="tpu_custom_call" | custom-call | flops 4000000000 | bytes 4000000 | tf_op jit(solution)/shard_map/local/pallas_call | solution.py:509
  19.6 7.5 %collective-permute-done.1 = f32[3,1,1024]{2,1,0:T(1,128)S(1)} collective-permute-done((f32[3,1,1024]{2,1,0:T(1,128)S(1)}, f32[3,1,1024]{2,1,0:T(1,128)S(1)}, u32[]{:S(2)}, u32[]{:S(2)}) %collective-permute-start.1) | collective-permute-done | bytes 12320 | tf_op jit(solution)/shard_map/ppermute | solution.py:533
  27.5 1.9 %collective-permute-start.3 = (f32[3,1,1024]{2,1,0:T(1,128)S(1)}, f32[3,1,1024]{2,1,0:T(1,128)S(1)}, u32[]{:S(2)}, u32[]{:S(2)}) collective-permute-start(f32[3,1,1024]{2,1,0:T(1,128)S(1)} %pad_maximum_fusion.2), channel_id=1, source_target_pairs={{0,2},{1,3},{2,0},{3,1},{4,6},{5,7},{6,4},{7,5},{8,10},{9,11},{10,... | collective-permute-start | bytes 36872 | tf_op jit(solution)/shard_map/ppermute | solution.py:533
  31.5 10.6 %collective-permute-done.2 = bf16[2,2,64,1024]{3,2,1,0:T(8,128)(2,1)S(1)} collective-permute-done((bf16[2,2,64,1024]{3,2,1,0:T(8,128)(2,1)S(1)}, bf16[2,2,64,1024]{3,2,1,0:T(8,128)(2,1)S(1)}, u32[]{:S(2)}, u32[]{:S(2)}) %collective-permute-start.2) | collective-permute-done | bytes 524320 | tf_op jit(solution)/shard_map/ppermute | solution.py:533
  42.4 2.7 %collective-permute-start.4 = (bf16[2,64,1024]{2,1,0:T(8,128)(2,1)S(1)}, bf16[2,64,1024]{2,1,0:T(8,128)(2,1)S(1)}, u32[]{:S(2)}, u32[]{:S(2)}) collective-permute-start(bf16[2,64,1024]{2,1,0:T(8,128)(2,1)S(1)} %fusion.18), channel_id=1, source_target_pairs={{0,4},{1,5},{2,6},{3,7},{4,0},{5,1},{6,2},{7,3},{8,12},{9,13},{10,... | collective-permute-start | bytes 786440 | tf_op jit(solution)/shard_map/ppermute | solution.py:533
  45.4 10.3 %collective-permute-done.5 = f32[3,1,1024]{2,1,0:T(1,128)S(1)} collective-permute-done((f32[3,1,1024]{2,1,0:T(1,128)S(1)}, f32[3,1,1024]{2,1,0:T(1,128)S(1)}, u32[]{:S(2)}, u32[]{:S(2)}) %collective-permute-start.5) | collective-permute-done | bytes 12320 | tf_op jit(solution)/shard_map/ppermute | solution.py:533
  56.4 9.2 %out.1 = (f32[2,128,1024]{2,1,0:T(8,128)}, f32[2,128,1024]{2,1,0:T(8,128)}, bf16[256,1024]{1,0:T(8,128)(2,1)S(1)}, f32[2,128,1024]{2,1,0:T(8,128)}, f32[24,128]{1,0:T(8,128)S(1)}) custom-call(bf16[2,128,2192]{2,1,0:T(8,128)(2,1)} %get-tuple-element.73.proj_ref, bf16[2,2,64,1024]{3,2,1,0:T(8,128)(2,1)S(1)} %fusion.2.carry_ref, ...), custom_call_target="tpu_custom_call" | custom-call | flops 2000000000 | bytes 8000000 | tf_op jit(solution)/shard_map/out/pallas_call | solution.py:509
  65.6 3.4 %collective-permute-start.7 = (f32[24,128]{1,0:T(8,128)S(1)}, f32[24,128]{1,0:T(8,128)S(1)}, u32[]{:S(2)}, u32[]{:S(2)}) collective-permute-start(f32[24,128]{1,0:T(8,128)S(1)} %get-tuple-element.86.sent_ref), channel_id=1, source_target_pairs={{0,7},{1,6},{2,5},{3,4},{4,3},{5,2},{6,1},{7,0},{8,15},{9,14},{10,... | collective-permute-start | bytes 36872 | tf_op jit(solution)/shard_map/ppermute | solution.py:747
  72.0 9.7 %head.1 = (f32[1,128]{1,0:T(1,128)S(1)}, f32[2,128,1024]{2,1,0:T(8,128)}, bf16[256,1024]{1,0:T(8,128)(2,1)S(1)}, bf16[2,128,1024]{2,1,0:T(8,128)(2,1)}, bf16[2,1...) custom-call(bf16[2,128,2192]{2,1,0:T(8,128)(2,1)} %get-tuple-element.73.proj_ref, ...), custom_call_target="tpu_custom_call" | custom-call | flops 2000000000 | bytes 8000000 | tf_op jit(solution)/shard_map/head/pallas_call | solution.py:509
  90.7 3.7 %collective-permute-done.8 = bf16[2,2,64,1024]{3,2,1,0:T(8,128)(2,1)} collective-permute-done((bf16[2,2,64,1024]{3,2,1,0:T(8,128)(2,1)S(1)}, bf16[2,2,64,1024]{3,2,1,0:T(8,128)(2,1)}, u32[]{:S(2)}, u32[]{:S(2)}) %collective-permute-start.8) | collective-permute-done | bytes 524320 | tf_op jit(solution)/shard_map/ppermute | solution.py:533
  95.6 1.9 %weight.4 = (bf16[256,1024]{1,0:T(8,128)(2,1)S(1)}, f32[256,1024]{1,0:T(8,128)S(1)}) custom-call(s32[2]{0:T(128)S(1)} %pad_add_fusion.place_ref, bf16[256,1024]{1,0:T(8,128)(2,1)S(1)} %pad_maximum_fusion.rows_ref, bf16[256,512]{1,0:T(8,128)(2,1)S(1)} %collective-permute-done.11.their_rows_ref, bf16[256,1024]{1,0:T(8,128)(2,1)S(1)} %get-tuple-element.94.cot_ref.gate_ref, ...), custom_call_target="tpu_custom_call" | custom-call | flops 1200000000 | bytes 6000000 | tf_op jit(solution)/shard_map/weight/pallas_call | solution.py:624
  99.7 9.6 %adjoint.1 = (f32[2,128,1024]{2,1,0:T(8,128)}, f32[2,128,64]{2,1,0:T(8,128)S(1)}, f32[2,128,64]{2,1,0:T(8,128)S(1)}, f32[2,128,16]{2,1,0:T(8,128)S(1)}, f32[2,128,16]{2,1,0:T(8,128)S(1)}) custom-call(bf16[2,128,2192]{2,1,0:T(8,128)(2,1)} %get-tuple-element.73.proj_ref, bf16[2,2,64,1024]{3,2,1,0:T(8,128)(2,1)S(1)} %fusion.2.carry_ref, ...), custom_call_target="tpu_custom_call" | custom-call | flops 8000000000 | bytes 6000000 | tf_op jit(solution)/shard_map/adjoint/pallas_call | solution.py:509
  111.6 2.3 %collective-permute-start.16 = (bf16[2,64,1024]{2,1,0:T(8,128)(2,1)S(1)}, bf16[2,64,1024]{2,1,0:T(8,128)(2,1)S(1)}, u32[]{:S(2)}, u32[]{:S(2)}) collective-permute-start(bf16[2,64,1024]{2,1,0:T(8,128)(2,1)S(1)} %fusion.17), channel_id=1, source_target_pairs={{0,4},{1,5},{2,6},{3,7},{4,0},{5,1},{6,2},{7,3},{8,12},{9,13},{10,... | collective-permute-start | bytes 786440 | tf_op jit(solution)/shard_map/ppermute | solution.py:533
  114.1 7.6 %collective-permute-done.18 = bf16[256,1024]{1,0:T(8,128)(2,1)S(1)} collective-permute-done((bf16[256,1024]{1,0:T(8,128)(2,1)S(1)}, bf16[256,1024]{1,0:T(8,128)(2,1)S(1)}, u32[]{:S(2)}, u32[]{:S(2)}) %collective-permute-start.18) | collective-permute-done | bytes 524320 | tf_op jit(solution)/shard_map/ppermute | solution.py:533
  124.9 4.0 %finish.1.cot_ref.rest_ref = bf16[256,1168]{1,0:T(8,128)(2,1)S(1)} custom-call(bf16[2,128,2192]{2,1,0:T(8,128)(2,1)} %get-tuple-element.73.proj_ref, bf16[2,2,64,1024]{3,2,1,0:T(8,128)(2,1)S(1)} %fusion.2.carry_ref, bf16[2,2,64,1024]{3,2,1,0:T(8,128)(2,1)S(1)} %fusion.11.next_ref, f32[2,128,1024]{2,1,0:T(8,128)} %get-tuple-element.110.dval_in, ...), custom_call_target="tpu_custom_call" | custom-call | flops 2000000000 | bytes 5000000 | tf_op jit(solution)/shard_map/finish/pallas_call | solution.py:509
  130.9 1.9 %collective-permute-done.15 = f32[1,128]{1,0:T(1,128)S(1)} collective-permute-done((f32[1,128]{1,0:T(1,128)S(1)}, f32[1,128]{1,0:T(1,128)S(1)}, u32[]{:S(2)}, u32[]{:S(2)}) %collective-permute-start.15) | collective-permute-done | bytes 544 | tf_op jit(solution)/shard_map/ppermute | solution.py:533
  143.0 4.9 %input.1 = (bf16[1,128,1024]{2,1,0:T(8,128)(2,1)}, bf16[1,128,1024]{2,1,0:T(8,128)(2,1)}) custom-call(bf16[256,1168]{1,0:T(8,128)(2,1)S(1)} %finish.1.cot_ref.rest_ref, bf16[256,1024]{1,0:T(8,128)(2,1)S(1)} %copy-done.4, bf16[2192,1024]{1,0:T(8,128)(2,1)} %bitcast.132, f32[2,128,1024]{2,1,0:T(8,128)} %get-tuple-element.119.dres_ref), custom_call_target="tpu_custom_call" | custom-call | flops 2000000000 | bytes 7000000 | tf_op jit(solution)/shard_map/input/pallas_call | solution.py:509
  147.9 2.9 %collective-permute-done.20 = f32[1,128]{1,0:T(1,128)S(1)} collective-permute-done((f32[1,128]{1,0:T(1,128)S(1)}, f32[1,128]{1,0:T(1,128)S(1)}, u32[]{:S(2)}, u32[]{:S(2)}) %collective-permute-start.20) | collective-permute-done | bytes 544 | tf_op jit(solution)/shard_map/ppermute | solution.py:533
  156.3 2.0 %collective-permute-start.26 = (bf16[64,1024]{1,0:T(8,128)(2,1)S(1)}, bf16[64,1024]{1,0:T(8,128)(2,1)S(1)}, u32[]{:S(2)}, u32[]{:S(2)}) collective-permute-start(bf16[64,1024]{1,0:T(8,128)(2,1)S(1)} %fusion.21), channel_id=1, source_target_pairs={{0,4},{1,5},{2,6},{3,7},{4,0},{5,1},{6,2},{7,3},{8,12},{9,13},{10,... | collective-permute-start | bytes 393224 | tf_op jit(solution)/shard_map/ppermute | solution.py:533
  158.5 7.0 %collective-permute-done.25 = bf16[64,1024]{1,0:T(8,128)(2,1)S(1)} collective-permute-done((bf16[64,1024]{1,0:T(8,128)(2,1)S(1)}, bf16[64,1024]{1,0:T(8,128)(2,1)S(1)}, u32[]{:S(2)}, u32[]{:S(2)}) %collective-permute-start.25) | collective-permute-done | bytes 131104 | tf_op jit(solution)/shard_map/ppermute | solution.py:533
  165.5 5.2 %collective-permute-done.26 = bf16[64,1024]{1,0:T(8,128)(2,1)S(1)} collective-permute-done((bf16[64,1024]{1,0:T(8,128)(2,1)S(1)}, bf16[64,1024]{1,0:T(8,128)(2,1)S(1)}, u32[]{:S(2)}, u32[]{:S(2)}) %collective-permute-start.26) | collective-permute-done | bytes 131104 | tf_op jit(solution)/shard_map/ppermute | solution.py:533
  172.8 7.8 %collective-permute-done.28 = bf16[64,1168]{1,0:T(8,128)(2,1)S(1)} collective-permute-done((bf16[64,1168]{1,0:T(8,128)(2,1)S(1)}, bf16[64,1168]{1,0:T(8,128)(2,1)S(1)}, u32[]{:S(2)}, u32[]{:S(2)}) %collective-permute-start.28) | collective-permute-done | bytes 149536 | tf_op jit(solution)/shard_map/ppermute | solution.py:533
  (172 shorter events, 47.3 us)
Async XLA Ops:
  11.9 15.3 %collective-permute-start = (bf16[2,2,64,1024]{3,2,1,0:T(8,128)(2,1)S(1)}, bf16[2,2,64,1024]{3,2,1,0:T(8,128)(2,1)S(1)}, u32[]{:S(2)}, u32[]{:S(2)}) collective-permute-start(bf16[2,2,64,1024]{3,2,1,0:T(8,128)(2,1)S(1)} %get-tuple-element.76), channel_id=1, source_target_pairs={{0,1},{1,0},{2,3},{3,2},{4,5},{5,4},{6,7},{7,6},{8,9},{9,8},{10,11... | collective-permute-start | bytes 1572872 | tf_op jit(solution)/shard_map/ppermute | solution.py:533
  14.9 12.2 %collective-permute-start.1 = (f32[3,1,1024]{2,1,0:T(1,128)S(1)}, f32[3,1,1024]{2,1,0:T(1,128)S(1)}, u32[]{:S(2)}, u32[]{:S(2)}) collective-permute-start(f32[3,1,1024]{2,1,0:T(1,128)S(1)} %get-tuple-element.77), channel_id=1, source_target_pairs={{0,1},{1,0},{2,3},{3,2},{4,5},{5,4},{6,7},{7,6},{8,9},{9,8},{10,11... | collective-permute-start | bytes 36872 | tf_op jit(solution)/shard_map/ppermute | solution.py:533
  27.5 3.9 %collective-permute-start.3 = (f32[3,1,1024]{2,1,0:T(1,128)S(1)}, f32[3,1,1024]{2,1,0:T(1,128)S(1)}, u32[]{:S(2)}, u32[]{:S(2)}) collective-permute-start(f32[3,1,1024]{2,1,0:T(1,128)S(1)} %pad_maximum_fusion.2), channel_id=1, source_target_pairs={{0,2},{1,3},{2,0},{3,1},{4,6},{5,7},{6,4},{7,5},{8,10},{9,11},{10,... | collective-permute-start | bytes 36872 | tf_op jit(solution)/shard_map/ppermute | solution.py:533
  29.4 12.7 %collective-permute-start.2 = (bf16[2,2,64,1024]{3,2,1,0:T(8,128)(2,1)S(1)}, bf16[2,2,64,1024]{3,2,1,0:T(8,128)(2,1)S(1)}, u32[]{:S(2)}, u32[]{:S(2)}) collective-permute-start(bf16[2,2,64,1024]{3,2,1,0:T(8,128)(2,1)S(1)} %fusion.4), channel_id=1, source_target_pairs={{0,2},{1,3},{2,0},{3,1},{4,6},{5,7},{6,4},{7,5},{8,10},{9,11},{10,... | collective-permute-start | bytes 1572872 | tf_op jit(solution)/shard_map/ppermute | solution.py:533
  42.4 13.4 %collective-permute-start.4 = (bf16[2,64,1024]{2,1,0:T(8,128)(2,1)S(1)}, bf16[2,64,1024]{2,1,0:T(8,128)(2,1)S(1)}, u32[]{:S(2)}, u32[]{:S(2)}) collective-permute-start(bf16[2,64,1024]{2,1,0:T(8,128)(2,1)S(1)} %fusion.18), channel_id=1, source_target_pairs={{0,4},{1,5},{2,6},{3,7},{4,0},{5,1},{6,2},{7,3},{8,12},{9,13},{10,... | collective-permute-start | bytes 786440 | tf_op jit(solution)/shard_map/ppermute | solution.py:533
  45.0 10.6 %collective-permute-start.5 = (f32[3,1,1024]{2,1,0:T(1,128)S(1)}, f32[3,1,1024]{2,1,0:T(1,128)S(1)}, u32[]{:S(2)}, u32[]{:S(2)}) collective-permute-start(f32[3,1,1024]{2,1,0:T(1,128)S(1)} %pad_maximum_fusion.3), channel_id=1, source_target_pairs={{0,4},{1,5},{2,6},{3,7},{4,0},{5,1},{6,2},{7,3},{8,12},{9,13},{10,... | collective-permute-start | bytes 36872 | tf_op jit(solution)/shard_map/ppermute | solution.py:533
  65.6 6.4 %collective-permute-start.7 = (f32[24,128]{1,0:T(8,128)S(1)}, f32[24,128]{1,0:T(8,128)S(1)}, u32[]{:S(2)}, u32[]{:S(2)}) collective-permute-start(f32[24,128]{1,0:T(8,128)S(1)} %get-tuple-element.86.sent_ref), channel_id=1, source_target_pairs={{0,7},{1,6},{2,5},{3,4},{4,3},{5,2},{6,1},{7,0},{8,15},{9,14},{10,... | collective-permute-start | bytes 36872 | tf_op jit(solution)/shard_map/ppermute | solution.py:747
  81.7 12.6 %collective-permute-start.8 = (bf16[2,2,64,1024]{3,2,1,0:T(8,128)(2,1)S(1)}, bf16[2,2,64,1024]{3,2,1,0:T(8,128)(2,1)}, u32[]{:S(2)}, u32[]{:S(2)}) collective-permute-start(bf16[2,2,64,1024]{3,2,1,0:T(8,128)(2,1)S(1)} %get-tuple-element.90), channel_id=1, source_target_pairs={{0,1},{1,0},{2,3},{3,2},{4,5},{5,4},{6,7},{7,6},{8,9},{9,8},{10,11... | collective-permute-start | bytes 1572872 | tf_op jit(solution)/shard_map/ppermute | solution.py:533
  85.3 10.3 %collective-permute-start.11 = (bf16[256,512]{1,0:T(8,128)(2,1)}, bf16[256,512]{1,0:T(8,128)(2,1)S(1)}, u32[]{:S(2)}, u32[]{:S(2)}) collective-permute-start(bf16[256,512]{1,0:T(8,128)(2,1)} %fusion.15), channel_id=1, source_target_pairs={{0,8},{8,0},{1,9},{9,1},{2,10},{10,2},{3,11},{11,3},{4,12},{12,4},... | collective-permute-start | bytes 786440 | tf_op jit(solution)/shard_map/ppermute | solution.py:606
  85.3 10.3 %collective-permute-start.12 = (bf16[256,1024]{1,0:T(8,128)(2,1)S(1)}, bf16[256,1024]{1,0:T(8,128)(2,1)}, u32[]{:S(2)}, u32[]{:S(2)}) collective-permute-start(bf16[256,1024]{1,0:T(8,128)(2,1)S(1)} %get-tuple-element.94.cot_ref.gate_ref), channel_id=1, source_target_pairs={{0,8},{8,0},{1,9},{9,1},{2,10},{10,2},{3,11},{11,3},{4,12},{12,4},... | collective-permute-start | bytes 1572872 | tf_op jit(solution)/shard_map/ppermute | solution.py:606
  97.6 13.8 %collective-permute-start.13 = (bf16[2,2,64,1024]{3,2,1,0:T(8,128)(2,1)S(1)}, bf16[2,2,64,1024]{3,2,1,0:T(8,128)(2,1)S(1)}, u32[]{:S(2)}, u32[]{:S(2)}) collective-permute-start(bf16[2,2,64,1024]{3,2,1,0:T(8,128)(2,1)S(1)} %fusion.8), channel_id=1, source_target_pairs={{0,2},{1,3},{2,0},{3,1},{4,6},{5,7},{6,4},{7,5},{8,10},{9,11},{10,... | collective-permute-start | bytes 1572872 | tf_op jit(solution)/shard_map/ppermute | solution.py:533
  97.6 13.2 %collective-permute-start.14 = (f32[1,128]{1,0:T(1,128)S(1)}, f32[1,128]{1,0:T(1,128)S(1)}, u32[]{:S(2)}, u32[]{:S(2)}) collective-permute-start(f32[1,128]{1,0:T(1,128)S(1)} %get-tuple-element.98), channel_id=1, source_target_pairs={{0,1},{1,0},{2,3},{3,2},{4,5},{5,4},{6,7},{7,6},{8,9},{9,8},{10,11... | collective-permute-start | bytes 1544 | tf_op jit(solution)/shard_map/ppermute | solution.py:533
  99.1 14.8 %collective-permute-start.17 = (bf16[256,1024]{1,0:T(8,128)(2,1)S(1)}, bf16[256,1024]{1,0:T(8,128)(2,1)S(1)}, u32[]{:S(2)}, u32[]{:S(2)}) collective-permute-start(bf16[256,1024]{1,0:T(8,128)(2,1)S(1)} %get-tuple-element.102), channel_id=1, source_target_pairs={{0,1},{1,0},{2,3},{3,2},{4,5},{5,4},{6,7},{7,6},{8,9},{9,8},{10,11... | collective-permute-start | bytes 1572872 | tf_op jit(solution)/shard_map/ppermute | solution.py:533
  109.3 12.4 %collective-permute-start.18 = (bf16[256,1024]{1,0:T(8,128)(2,1)S(1)}, bf16[256,1024]{1,0:T(8,128)(2,1)S(1)}, u32[]{:S(2)}, u32[]{:S(2)}) collective-permute-start(bf16[256,1024]{1,0:T(8,128)(2,1)S(1)} %get-tuple-element.104), channel_id=1, source_target_pairs={{0,1},{1,0},{2,3},{3,2},{4,5},{5,4},{6,7},{7,6},{8,9},{9,8},{10,11... | collective-permute-start | bytes 1572872 | tf_op jit(solution)/shard_map/ppermute | solution.py:533
  111.6 11.8 %collective-permute-start.16 = (bf16[2,64,1024]{2,1,0:T(8,128)(2,1)S(1)}, bf16[2,64,1024]{2,1,0:T(8,128)(2,1)S(1)}, u32[]{:S(2)}, u32[]{:S(2)}) collective-permute-start(bf16[2,64,1024]{2,1,0:T(8,128)(2,1)S(1)} %fusion.17), channel_id=1, source_target_pairs={{0,4},{1,5},{2,6},{3,7},{4,0},{5,1},{6,2},{7,3},{8,12},{9,13},{10,... | collective-permute-start | bytes 786440 | tf_op jit(solution)/shard_map/ppermute | solution.py:533
  129.1 3.7 %collective-permute-start.19 = (bf16[256,1168]{0,1:T(8,128)(2,1)S(1)}, bf16[256,1168]{0,1:T(8,128)(2,1)S(1)}, u32[]{:S(2)}, u32[]{:S(2)}) collective-permute-start(bf16[256,1168]{0,1:T(8,128)(2,1)S(1)} %copy.20), channel_id=1, source_target_pairs={{0,8},{8,0},{1,9},{9,1},{2,10},{10,2},{3,11},{11,3},{4,12},{12,4},... | collective-permute-start | bytes 1794056 | tf_op jit(solution)/shard_map/ppermute | solution.py:606
  136.8 15.0 %collective-permute-start.23 = (bf16[256,1168]{0,1:T(8,128)(2,1)}, bf16[256,1168]{0,1:T(8,128)(2,1)}, u32[]{:S(2)}, u32[]{:S(2)}) collective-permute-start(bf16[256,1168]{0,1:T(8,128)(2,1)} %copy.22), channel_id=1, source_target_pairs={{0,1},{1,0},{2,3},{3,2},{4,5},{5,4},{6,7},{7,6},{8,9},{9,8},{10,11... | collective-permute-start | bytes 1794056 | tf_op jit(solution)/shard_map/ppermute | solution.py:533
  138.5 12.3 %collective-permute-start.21 = (bf16[128,1024]{1,0:T(8,128)(2,1)}, bf16[128,1024]{1,0:T(8,128)(2,1)S(1)}, u32[]{:S(2)}, u32[]{:S(2)}) collective-permute-start(bf16[128,1024]{1,0:T(8,128)(2,1)} %bitcast.130), channel_id=1, source_target_pairs={{0,2},{1,3},{2,0},{3,1},{4,6},{5,7},{6,4},{7,5},{8,10},{9,11},{10,... | collective-permute-start | bytes 786440 | tf_op jit(solution)/shard_map/ppermute | solution.py:533
  140.2 11.4 %collective-permute-start.22 = (bf16[128,1024]{1,0:T(8,128)(2,1)S(1)}, bf16[128,1024]{1,0:T(8,128)(2,1)S(1)}, u32[]{:S(2)}, u32[]{:S(2)}) collective-permute-start(bf16[128,1024]{1,0:T(8,128)(2,1)S(1)} %bitcast.129), channel_id=1, source_target_pairs={{0,2},{1,3},{2,0},{3,1},{4,6},{5,7},{6,4},{7,5},{8,10},{9,11},{10,... | collective-permute-start | bytes 786440 | tf_op jit(solution)/shard_map/ppermute | solution.py:533
  141.6 9.1 %collective-permute-start.20 = (f32[1,128]{1,0:T(1,128)S(1)}, f32[1,128]{1,0:T(1,128)S(1)}, u32[]{:S(2)}, u32[]{:S(2)}) collective-permute-start(f32[1,128]{1,0:T(1,128)S(1)} %add.119), channel_id=1, source_target_pairs={{0,4},{1,5},{2,6},{3,7},{4,0},{5,1},{6,2},{7,3},{8,12},{9,13},{10,... | collective-permute-start | bytes 1544 | tf_op jit(solution)/shard_map/ppermute | solution.py:533
  153.7 17.0 %collective-permute-start.27 = (bf16[128,1168]{1,0:T(8,128)(2,1)S(1)}, bf16[128,1168]{1,0:T(8,128)(2,1)S(1)}, u32[]{:S(2)}, u32[]{:S(2)}) collective-permute-start(bf16[128,1168]{1,0:T(8,128)(2,1)S(1)} %bitcast.128), channel_id=1, source_target_pairs={{0,2},{1,3},{2,0},{3,1},{4,6},{5,7},{6,4},{7,5},{8,10},{9,11},{10,... | collective-permute-start | bytes 897032 | tf_op jit(solution)/shard_map/ppermute | solution.py:533
  155.5 10.0 %collective-permute-start.25 = (bf16[64,1024]{1,0:T(8,128)(2,1)S(1)}, bf16[64,1024]{1,0:T(8,128)(2,1)S(1)}, u32[]{:S(2)}, u32[]{:S(2)}) collective-permute-start(bf16[64,1024]{1,0:T(8,128)(2,1)S(1)} %fusion.20), channel_id=1, source_target_pairs={{0,4},{1,5},{2,6},{3,7},{4,0},{5,1},{6,2},{7,3},{8,12},{9,13},{10,... | collective-permute-start | bytes 393224 | tf_op jit(solution)/shard_map/ppermute | solution.py:533
  156.3 14.4 %collective-permute-start.26 = (bf16[64,1024]{1,0:T(8,128)(2,1)S(1)}, bf16[64,1024]{1,0:T(8,128)(2,1)S(1)}, u32[]{:S(2)}, u32[]{:S(2)}) collective-permute-start(bf16[64,1024]{1,0:T(8,128)(2,1)S(1)} %fusion.21), channel_id=1, source_target_pairs={{0,4},{1,5},{2,6},{3,7},{4,0},{5,1},{6,2},{7,3},{8,12},{9,13},{10,... | collective-permute-start | bytes 393224 | tf_op jit(solution)/shard_map/ppermute | solution.py:533
  170.8 9.8 %collective-permute-start.28 = (bf16[64,1168]{1,0:T(8,128)(2,1)S(1)}, bf16[64,1168]{1,0:T(8,128)(2,1)S(1)}, u32[]{:S(2)}, u32[]{:S(2)}) collective-permute-start(bf16[64,1168]{1,0:T(8,128)(2,1)S(1)} %fusion.19), channel_id=1, source_target_pairs={{0,4},{1,5},{2,6},{3,7},{4,0},{5,1},{6,2},{7,3},{8,12},{9,13},{10,... | collective-permute-start | bytes 448520 | tf_op jit(solution)/shard_map/ppermute | solution.py:533
  (39 other events, 236.8 us)

commit v3 on v2

--- a/solution.py
+++ b/solution.py
@@ -13,12 +13,14 @@
 INNER = HEADS * HEAD_DIM
 PAIRS = HEADS // 2
 LANES = 2 * HEAD_DIM
+USED = INNER + 2 * STATE + HEADS
+REST = (USED + 127) // 128 * 128
 EPSILON = 1e-05
 
 F32 = jnp.float32
 BF16 = jnp.bfloat16
 HIGH = lax.Precision.HIGHEST
-VMEM_BYTES = 24 * 1024 * 1024
+VMEM_BYTES = 14 * 1024 * 1024
 
 
 def mm(a, b, ca=1, cb=0, precision=None):
@@ -54,8 +56,8 @@
     return mm(x.astype(BF16), pick)
 
 
-def steps(proj_ref, bias_ref, alog_ref):
-    raw = proj_ref[0, :, 2 * INNER + 2 * STATE :].astype(F32) + bias_ref[...]
+def steps(proj_ref, bias_ref, alog_ref, row=0):
+    raw = proj_ref[row, :, 2 * INNER + 2 * STATE :].astype(F32) + bias_ref[...]
     dt = softplus(raw)
     a = -jnp.exp(alog_ref[...]) * dt
     cum = mm(tri(a.shape[0], "ge"), a, precision=HIGH)
@@ -85,7 +87,7 @@
 def front_kernel(
     fwd_ref,
     rc_ref,
-    win_ref,
+    win_hbm,
     bias_ref,
     alog_ref,
     mask_ref,
@@ -93,30 +95,44 @@
     proj_ref,
     total_ref,
     small_ref,
+    win,
     wide_l,
     wide_r,
+    arrived,
+    *,
+    cuts,
 ):
-    row = pl.program_id(0)
-    hidden = jnp.where(row == 0, fwd_ref[0], rc_ref[0])
-    proj_ref[0] = mm(hidden, win_ref[...], 1, 1).astype(BF16)
-    unused, dt, a, cum, cex, tot = steps(proj_ref, bias_ref, alog_ref)
-    w_l = jnp.exp(tot - cum) * dt
-    w_r = jnp.exp(cex) * dt
-    block = jnp.exp(tot)
-    for j in range(PAIRS):
-        s = lanes_of(j)
-        v = proj_ref[0, :, s].astype(F32)
-        wide_l[:, s] = (v * pair_wide(w_l, j)).astype(BF16)
-        wide_r[:, s] = (v * pair_wide(w_r, j)).astype(BF16)
-        small_ref[pl.ds(row, 1), :, s] = pair_wide(block, j)[None]
-    keys = keys_of(proj_ref)
-    total_ref[0, 0] = mm(keys, wide_l[...], 0, 0).astype(BF16)
-    total_ref[0, 1] = mm(keys, wide_r[...], 0, 0).astype(BF16)
-
-    @pl.when(row == 0)
-    def _():
-        scored = jnp.sum(mask_ref[...].astype(F32), axis=1, keepdims=True)
-        small_ref[2] = jnp.where(iota((1, INNER), 1) == species_ref[...], scored, 0.0)
+    copies = [
+        pltpu.make_async_copy(
+            win_hbm.at[pl.ds(low, high - low)], win.at[pl.ds(low, high - low)], arrived.at[i]
+        )
+        for i, (low, high) in enumerate(zip(cuts, cuts[1:]))
+    ]
+    for copy in copies:
+        copy.start()
+    hidden = jnp.concatenate([fwd_ref[0], rc_ref[0]], axis=0)
+    n = fwd_ref.shape[1]
+    for copy, low, high in zip(copies, cuts, cuts[1:]):
+        copy.wait()
+        part = mm(hidden, win[low:high, :], 1, 1).astype(BF16)
+        proj_ref[0, :, low:high] = part[:n]
+        proj_ref[1, :, low:high] = part[n:]
+    for row in range(2):
+        unused, dt, a, cum, cex, tot = steps(proj_ref, bias_ref, alog_ref, row)
+        w_l = jnp.exp(tot - cum) * dt
+        w_r = jnp.exp(cex) * dt
+        block = jnp.exp(tot)
+        for j in range(PAIRS):
+            s = lanes_of(j)
+            v = proj_ref[row, :, s].astype(F32)
+            wide_l[:, s] = (v * pair_wide(w_l, j)).astype(BF16)
+            wide_r[:, s] = (v * pair_wide(w_r, j)).astype(BF16)
+            small_ref[row, :, s] = pair_wide(block, j)
+        keys = proj_ref[row, :, 2 * INNER : 2 * INNER + STATE]
+        total_ref[row, 0] = mm(keys, wide_l[...], 0, 0).astype(BF16)
+        total_ref[row, 1] = mm(keys, wide_r[...], 0, 0).astype(BF16)
+    scored = jnp.sum(mask_ref[...].astype(F32), axis=1, keepdims=True)
+    small_ref[2] = jnp.where(iota((1, INNER), 1) == species_ref[0, 0], scored, 0.0)
 
 
 def local_kernel(proj_ref, bias_ref, alog_ref, skip_ref, left_ref, right_ref):
@@ -142,8 +158,8 @@
             right.append(jnp.where(t <= s, mix, 0.0).astype(BF16))
         stacked = jnp.concatenate([jnp.where(first, v, zero), jnp.where(first, zero, v)], axis=0)
         skip = pair_wide(skip_ref[...], j) * v.astype(F32)
-        left_ref[0, :, lanes] = mm(jnp.concatenate(left, axis=1), stacked) + skip
-        right_ref[0, :, lanes] = mm(jnp.concatenate(right, axis=1), stacked) + skip
+        left_ref[0, :, lanes] = (mm(jnp.concatenate(left, axis=1), stacked) + skip).astype(BF16)
+        right_ref[0, :, lanes] = (mm(jnp.concatenate(right, axis=1), stacked) + skip).astype(BF16)
 
 
 def out_kernel(
@@ -175,12 +191,14 @@
     from_r = mm(reads, carry_ref[0, 1])
     for j in range(PAIRS):
         s = lanes_of(j)
-        left_ref[0, :, s] = left_in[0, :, s] + pair_wide(e_l, j) * from_l[:, s]
-        right_ref[0, :, s] = right_in[0, :, s] + pair_wide(e_r, j) * from_r[:, s]
+        out_l = left_in[0, :, s].astype(F32) + pair_wide(e_l, j) * from_l[:, s]
+        out_r = right_in[0, :, s].astype(F32) + pair_wide(e_r, j) * from_r[:, s]
+        left_ref[0, :, s] = out_l.astype(BF16)
+        right_ref[0, :, s] = out_r.astype(BF16)
     gate = proj_ref[0, :, INNER : 2 * INNER].astype(F32)
     gated = gate * jax.nn.sigmoid(gate)
-    u_l = left_ref[0] * gated
-    u_r = right_ref[0] * gated
+    u_l = left_ref[0].astype(F32) * gated
+    u_r = right_ref[0].astype(F32) * gated
     k_l = lax.rsqrt(jnp.mean(u_l * u_l, axis=1, keepdims=True) + EPSILON)
     k_r = lax.rsqrt(jnp.mean(u_r * u_r, axis=1, keepdims=True) + EPSILON)
     nsum = ((u_l * k_l + u_r * k_r) * gain_ref[...]).astype(BF16)
@@ -206,6 +224,7 @@
     sent_ref,
     got_ref,
     counts_ref,
+    their_counts_ref,
     species_ref,
     logvar_ref,
     res_ref,
@@ -218,11 +237,9 @@
     final_ref,
     head_ref,
     ce_ref,
-    dres_ref,
-    dmix_ref,
+    dcot_ref,
     dleft_ref,
     dright_ref,
-    dgate_ref,
     dstate_ref,
     wide_l,
     wide_r,
@@ -242,7 +259,9 @@
     token = jnp.where(row == 0, sent_ref[16:17, :], their_token)
     mask = jnp.where(row == 0, sent_ref[17:18, :], seen[1:2])
     kinds = logvar_ref.shape[1]
-    scaled = jnp.exp(-logvar_ref[...]) / jnp.maximum(counts_ref[0, :, :kinds], 1.0)
+    scaled = jnp.exp(-logvar_ref[...]) / jnp.maximum(
+        counts_ref[0, :, :kinds] + their_counts_ref[0, :, :kinds], 1.0
+    )
     chosen = iota((1, kinds), 1) == species_ref[...]
     weight = loss_scale * mask * jnp.sum(jnp.where(chosen, scaled, 0.0), axis=1, keepdims=True)
     which = iota(total.shape, 0)
@@ -261,22 +280,21 @@
     res = res_ref[0]
     k = lax.rsqrt(jnp.mean(res * res, axis=1, keepdims=True) + EPSILON)
     d_res = k * (d_normed - res * (k * k * jnp.mean(d_normed * res, axis=1, keepdims=True)))
-    dres_ref[0] = d_res
     d_mix = d_res.astype(BF16)
-    dmix_ref[...] = d_mix
+    dcot_ref[:, :INNER] = d_mix
     d_sum = mm(d_mix, wout_ref[...], 1, 1) * gain_ref[...]
     gate = proj_ref[0, :, INNER : 2 * INNER].astype(F32)
     sig = jax.nn.sigmoid(gate)
     gated = gate * sig
     d_gated = jnp.zeros_like(gate)
     for source, target in ((left_ref, dleft_ref), (right_ref, dright_ref)):
-        out = source[0]
+        out = source[0].astype(F32)
         u = out * gated
         k = lax.rsqrt(jnp.mean(u * u, axis=1, keepdims=True) + EPSILON)
         d_u = k * (d_sum - u * (k * k * jnp.mean(d_sum * u, axis=1, keepdims=True)))
         target[0] = (d_u * gated).astype(BF16)
         d_gated = d_gated + d_u * out
-    dgate_ref[...] = (d_gated * (sig + gated * (1.0 - sig))).astype(BF16)
+    dcot_ref[:, INNER:] = (d_gated * (sig + gated * (1.0 - sig))).astype(BF16)
     unused, dt, a, cum, cex, tot = steps(proj_ref, bias_ref, alog_ref)
     e_l, e_r = jnp.exp(cum), jnp.exp(tot - cex)
     for j in range(PAIRS):
@@ -373,7 +391,7 @@
         both = d_l.astype(F32) + d_r.astype(F32)
         dval_ref[0, :, lanes] = (
             mm(jnp.concatenate(mixes, axis=1), d_split) + pair_wide(skip_ref[...], j) * both
-        )
+        ).astype(BF16)
         wide_l[:, lanes] = (d_l.astype(F32) * pair_wide(e_l, j)).astype(BF16)
         wide_r[:, lanes] = (d_r.astype(F32) * pair_wide(e_r, j)).astype(BF16)
     carry_l, carry_r = carry_ref[0, 0], carry_ref[0, 1]
@@ -422,7 +440,7 @@
         v = proj_ref[0, :, s].astype(F32)
         wide_w_l, wide_w_r = pair_wide(w_l, j), pair_wide(w_r, j)
         dproj_ref[:, s] = (
-            dval_in[0, :, s] + wide_w_l * z_l[:, s] + wide_w_r * z_r[:, s]
+            dval_in[0, :, s].astype(F32) + wide_w_l * z_l[:, s] + wide_w_r * z_r[:, s]
         ).astype(BF16)
         wide_l[:, s] = (v * wide_w_l).astype(BF16)
         wide_r[:, s] = (v * wide_w_r).astype(BF16)
@@ -444,16 +462,18 @@
     d_tot = jnp.exp(tot) * through + jnp.sum(q_l, axis=0, keepdims=True)
     d_a = da_in[0] + mm(gt, q_r, 0, 0, HIGH) - mm(ge, q_l, 0, 0, HIGH) + d_tot
     d_dt = ddt_in[0] + dw_l * f_l + dw_r * f_r - d_a * jnp.exp(alog_ref[...])
-    dproj_ref[:, INNER + 2 * STATE :] = (d_dt * jax.nn.sigmoid(raw)).astype(BF16)
-
-
-def input_kernel(rest_ref, gate_ref, win_ref, dres_ref, fwd_ref, rc_ref):
+    d_raw = d_dt * jax.nn.sigmoid(raw)
+    dproj_ref[:, INNER + 2 * STATE :] = jnp.zeros((n, REST - INNER - 2 * STATE), BF16)
+    dproj_ref[:, INNER + 2 * STATE : INNER + 2 * STATE + HEADS] = d_raw.astype(BF16)
+
+
+def input_kernel(rest_ref, cot_ref, win_ref, fwd_ref, rc_ref):
     row = pl.program_id(0)
     grad = (
-        dres_ref[0]
-        + mm(gate_ref[...], win_ref[INNER : 2 * INNER])
+        cot_ref[:, :INNER].astype(F32)
+        + mm(cot_ref[:, INNER:], win_ref[INNER : 2 * INNER])
         + mm(rest_ref[:, :INNER], win_ref[:INNER])
-        + mm(rest_ref[:, INNER:], win_ref[2 * INNER :])
+        + mm(rest_ref[:, INNER:USED], win_ref[2 * INNER :])
     ).astype(BF16)
 
     @pl.when(row == 0)
@@ -465,17 +485,32 @@
         rc_ref[0] = grad
 
 
-def weight_kernel(
-    place_ref, rows_ref, their_rows_ref, cot_ref, their_cot_ref, send_ref, keep_ref, both, *, block
-):
-    half = their_rows_ref.shape[1]
-    mine = jnp.where(place_ref[0] == 0, rows_ref[:, :half], rows_ref[:, half:])
-    both[...] = mm(mine, cot_ref[...], 0, 0) + mm(their_rows_ref[...], their_cot_ref[...], 0, 0)
+def weight_kernel(place_ref, *refs, block, widths):
+    rows, theirs = refs[: len(widths)], refs[len(widths) : 2 * len(widths)]
+    cot_ref, their_cot_ref, send_ref, keep_ref, both = refs[2 * len(widths) :]
+    at = 0
+    for rows_ref, their_rows_ref, width in zip(rows, theirs, widths):
+        half = their_rows_ref.shape[1]
+        mine = jnp.where(place_ref[0] == 0, rows_ref[:, :half], rows_ref[:, half:])
+        cols = slice(at, at + width)
+        both[:, cols] = mm(mine, cot_ref[:, cols], 0, 0) + mm(
+            their_rows_ref[...], their_cot_ref[:, cols], 0, 0
+        )
+        at += width
     side = place_ref[1]
     for i in range(keep_ref.shape[0] // block):
         here = slice(i * block, (i + 1) * block)
         keep_ref[here, :] = both[pl.ds((2 * i + side) * block, block), :]
         send_ref[here, :] = both[pl.ds((2 * i + 1 - side) * block, block), :].astype(BF16)
+
+
+def halve_kernel(side_ref, mine_ref, got_ref, send_ref, keep_ref, *, block):
+    side = side_ref[0]
+    for i in range(keep_ref.shape[0] // block):
+        here = slice(i * block, (i + 1) * block)
+        kept, sent = pl.ds((2 * i + side) * block, block), pl.ds((2 * i + 1 - side) * block, block)
+        keep_ref[here, :] = mine_ref[kept, :] + got_ref[kept, :].astype(F32)
+        send_ref[here, :] = (mine_ref[sent, :] + got_ref[sent, :].astype(F32)).astype(BF16)
 
 
 def by_row(shape):
@@ -618,13 +653,15 @@
         ctx = lax.axis_size("ctx")
         their_cot = over_cores(cotangent)
         place = jnp.stack([lax.axis_index("dp"), lax.axis_index("ctx") & 1]).astype(jnp.int32)
-        half, cols = rows_of.shape[1] // 2, cotangent.shape[1]
+        half, cols = theirs[0].shape[1], cotangent.shape[1]
         block = half // ctx
         vmem = pl.BlockSpec(memory_space=pltpu.VMEM)
         self.send, self.mine = pl.pallas_call(
-            functools.partial(weight_kernel, block=block),
+            functools.partial(
+                weight_kernel, block=block, widths=(cols // len(rows_of),) * len(rows_of)
+            ),
             name="weight",
-            in_specs=[pl.BlockSpec(memory_space=pltpu.SMEM), vmem, vmem, vmem, vmem],
+            in_specs=[pl.BlockSpec(memory_space=pltpu.SMEM)] + [vmem] * (2 * len(rows_of) + 2),
             out_specs=[vmem, vmem],
             out_shape=[
                 jax.ShapeDtypeStruct((half // 2, cols), BF16),
@@ -633,7 +670,7 @@
             scratch_shapes=[pltpu.VMEM((half, cols), F32)],
             compiler_params=pltpu.CompilerParams(vmem_limit_bytes=VMEM_BYTES),
             cost_estimate=cost(1.2e9, 6e6),
-        )(place, rows_of, theirs, cotangent, their_cot)
+        )(place, *rows_of, *theirs, cotangent, their_cot)
         self.bit = 0
         self.bits = bits_of("ctx")
         self.block = block
@@ -642,15 +679,25 @@
         return self.bit == self.bits
 
     def pass_on(self, got):
-        self.mine = self.mine + got.astype(F32)
         self.bit += 1
-        if not self.done():
-            cols = self.mine.shape[1]
-            pairs = self.mine.reshape(-1, 2, self.block, cols)
-            side = (lax.axis_index("ctx") >> self.bit) & 1
-            self.send = lax.dynamic_index_in_dim(pairs, 1 - side, 1, False).astype(BF16)
-            self.send = self.send.reshape(-1, cols)
-            self.mine = lax.dynamic_index_in_dim(pairs, side, 1, False).reshape(-1, cols)
+        if self.done():
+            self.mine = self.mine + got.astype(F32)
+            return
+        rows, cols = self.mine.shape
+        side = ((lax.axis_index("ctx") >> self.bit) & 1).astype(jnp.int32).reshape(1)
+        self.send, self.mine = pl.pallas_call(
+            functools.partial(halve_kernel, block=self.block),
+            name="halve",
+            grid=(1,),
+            in_specs=[pl.BlockSpec(memory_space=pltpu.SMEM), whole((rows, cols)), whole((rows, cols))],
+            out_specs=[whole((rows // 2, cols))] * 2,
+            out_shape=[
+                jax.ShapeDtypeStruct((rows // 2, cols), BF16),
+                jax.ShapeDtypeStruct((rows // 2, cols), F32),
+            ],
+            compiler_params=pltpu.CompilerParams(vmem_limit_bytes=VMEM_BYTES),
+            cost_estimate=cost(1e6, 3e6),
+        )(side, self.mine, got)
 
 
 def on_device(
@@ -684,31 +731,45 @@
     state_shape = (rows, 2, STATE, INNER)
     wide = ((length, INNER), BF16)
     full = (rows, length, INNER)
-    proj, total, small = call(
-        front_kernel,
-        "front",
-        [
-            (h_fwd, "all hbm"),
-            (h_rc, "all hbm"),
-            (win_t, "all hbm"),
-            (bias, "all"),
-            (alog, "all"),
-            (loss_mask, "all"),
-            (kind, "all"),
-        ],
-        [
-            ((rows, length, w_in.shape[1]), BF16, "row hbm"),
-            (state_shape, BF16, "row"),
-            ((rows + 1, 1, INNER), F32, "all"),
-        ],
-        [wide, wide],
-        cost(2e9, 7e6),
-    )
+    columns = w_in.shape[1]
+    cuts = [0, INNER // 2, INNER, 3 * INNER // 2, columns]
+    proj, total, small = pl.pallas_call(
+        functools.partial(front_kernel, cuts=cuts),
+        name="front",
+        grid=(1,),
+        in_specs=[
+            whole(h_fwd.shape),
+            whole(h_rc.shape),
+            pl.BlockSpec(memory_space=pltpu.HBM),
+            whole(bias.shape),
+            whole(alog.shape),
+            whole(loss_mask.shape),
+            pl.BlockSpec(memory_space=pltpu.SMEM),
+        ],
+        out_specs=[
+            whole((rows, length, columns)),
+            whole(state_shape),
+            whole((rows + 1, 1, INNER)),
+        ],
+        out_shape=[
+            pltpu.HBM((rows, length, columns), BF16),
+            jax.ShapeDtypeStruct(state_shape, BF16),
+            jax.ShapeDtypeStruct((rows + 1, 1, INNER), F32),
+        ],
+        scratch_shapes=[
+            pltpu.VMEM((columns, width), BF16),
+            pltpu.VMEM(*wide),
+            pltpu.VMEM(*wide),
+            pltpu.SemaphoreType.DMA((len(cuts) - 1,)),
+        ],
+        compiler_params=pltpu.CompilerParams(vmem_limit_bytes=VMEM_BYTES),
+        cost_estimate=cost(2e9, 7e6),
+    )(far(h_fwd), far(h_rc), far(win_t), far(bias), far(alog), far(loss_mask), kind)
     left_own, right_own = call(
         local_kernel,
         "local",
         [(proj, "row hbm"), (bias, "all"), (alog, "all"), (skip, "all")],
-        [(full, F32, "row hbm"), (full, F32, "row hbm")],
+        [(full, BF16, "row hbm"), (full, BF16, "row hbm")],
         (),
         cost(4e9, 4e6),
     )
@@ -726,17 +787,17 @@
             (bias, "all"),
             (alog, "all"),
             (gain, "all"),
-            (w_out, "all hbm"),
+            (w_out, "all"),
             (final, "all"),
             (head, "all"),
             (tokens, "all"),
             (loss_mask, "all"),
         ],
         [
-            (full, F32, "row hbm"),
-            (full, F32, "row hbm"),
+            (full, BF16, "row"),
+            (full, BF16, "row"),
             ((flat, INNER), BF16, "half"),
-            ((rows, length, width), F32, "row hbm"),
+            ((rows, length, width), F32, "row"),
             ((24, length), F32, "all"),
         ],
         (),
@@ -745,9 +806,8 @@
 
     sent, counts = together(sent, counts)
     got = lax.ppermute(sent, "ctx", [(i, ctx - 1 - i) for i in range(ctx)])
-    for bit in range(bits_of("dp")):
-        counts = counts + partner(counts, "dp", bit)
-    ce, d_res, d_mix, d_left, d_right, d_gate, d_state = call(
+    their_counts = over_cores(counts)
+    ce, d_cot, d_left, d_right, d_state = call(
         functools.partial(head_kernel, vocab=vocab, loss_scale=float(length * ctx)),
         "head",
         [
@@ -755,11 +815,12 @@
             (sent, "all"),
             (got, "all"),
             (counts, "all"),
+            (their_counts, "all"),
             (kind, "all"),
             (log_var[None], "all"),
-            (res, "row hbm"),
-            (out_left, "row hbm"),
-            (out_right, "row hbm"),
+            (res, "row"),
+            (out_left, "row"),
+            (out_right, "row"),
             (bias, "all"),
             (alog, "all"),
             (gain, "all"),
@@ -769,11 +830,9 @@
         ],
         [
             ((1, length), F32, "all"),
-            ((rows, length, width), F32, "row hbm"),
-            ((flat, width), BF16, "half"),
+            ((flat, width + INNER), BF16, "half"),
             (full, BF16, "row hbm"),
             (full, BF16, "row hbm"),
-            ((flat, INNER), BF16, "half"),
             (state_shape, BF16, "row"),
         ],
         [wide, wide],
@@ -784,31 +843,27 @@
     hidden_theirs = their_half(hidden)
 
     entering = jnp.zeros(state_shape, F32)
-    early, early_got = [], []
+    early, early_got = None, None
     for bit in range(bits):
         last = bit == bits - 1
         send = to_send(d_state, bit, last)
         if bit == 1:
-            send, early[0].send, early[1].send, ce_sum.array = together(
-                send, early[0].send, early[1].send, ce_sum.array
-            )
+            send, early.send, ce_sum.array = together(send, early.send, ce_sum.array)
         elif bit > 1:
             send, ce_sum.array = together(send, ce_sum.array)
         theirs = partner(send, "ctx", bit)
         if bit == 1:
-            early_got = [partner(share.send, "ctx", 0) for share in early]
+            early_got = partner(early.send, "ctx", 0)
         if bit > 0:
             ce_sum.step()
+        else:
+            early = RowShare([nsum, hidden], [their_half(nsum), hidden_theirs], d_cot)
+            theirs, early.send = together(theirs, early.send)
         if last:
-            for share, got in zip(early, early_got):
-                share.pass_on(got)
-            theirs, early[0].send, early[1].send = together(theirs, early[0].send, early[1].send)
+            early.pass_on(early_got)
+            theirs, early.send = together(theirs, early.send)
+            early_got = partner(early.send, "ctx", early.bit)
         d_state, entering = scan_round(d_state, entering, bit, last, rounds[bit], theirs)
-        if bit == 0:
-            early = [
-                RowShare(nsum, their_half(nsum), d_mix),
-                RowShare(hidden, hidden_theirs, d_gate),
-            ]
     following = entering.astype(BF16)
     d_val, d_key, d_read, d_a, d_dt = call(
         adjoint_kernel,
@@ -823,7 +878,7 @@
             (skip, "all"),
         ],
         [
-            (full, F32, "row hbm"),
+            (full, BF16, "row"),
             ((rows, length, STATE), F32, "row"),
             ((rows, length, STATE), F32, "row"),
             ((rows, length, HEADS), F32, "row"),
@@ -839,7 +894,7 @@
             (proj, "row hbm"),
             (carry, "row"),
             (following, "row"),
-            (d_val, "row hbm"),
+            (d_val, "row"),
             (d_key, "row"),
             (d_read, "row"),
             (d_a, "row"),
@@ -847,39 +902,43 @@
             (bias, "all"),
             (alog, "all"),
         ],
-        [((flat, INNER + 2 * STATE + HEADS), BF16, "half")],
+        [((flat, REST), BF16, "half")],
         [wide, wide],
         cost(2e9, 5e6),
     )
-    late = RowShare(hidden, hidden_theirs, d_rest)
+    late = RowShare([hidden], [hidden_theirs], d_rest)
     late.send, d_rest = together(late.send, d_rest)
     grad_fwd, grad_rc = call(
         input_kernel,
         "input",
-        [(d_rest, "half"), (d_gate, "half"), (win_t, "all hbm"), (d_res, "row hbm")],
+        [(d_rest, "half"), (d_cot, "half"), (win_t, "all")],
         [(h_fwd.shape, BF16, "all"), (h_rc.shape, BF16, "all")],
         (),
         cost(2e9, 7e6),
     )
     while not late.done():
-        shares = [share for share in early + [late] if not share.done()]
-        ce_sum.array, *sends = together(ce_sum.array, *[share.send for share in shares])
-        got = [partner(send, "ctx", share.bit) for share, send in zip(shares, sends)]
+        first = late.bit == 0
+        late.send, ce_sum.array = together(late.send, ce_sum.array)
+        late_got = partner(late.send, "ctx", late.bit)
         ce_sum.step()
-        if late.bit == 0:
-            grad_fwd, grad_rc, *got = together(grad_fwd, grad_rc, *got)
-        else:
-            got = together(*got)
-        for share, arrived in zip(shares, got):
-            share.pass_on(arrived)
+        if first:
+            late_got, grad_fwd, grad_rc = together(late_got, grad_fwd, grad_rc)
+        if not early.done():
+            late_got, early_got = together(late_got, early_got)
+        late.pass_on(late_got)
+        if not early.done():
+            early.pass_on(early_got)
+            if not early.done():
+                late.send, early.send = together(late.send, early.send)
+                early_got = partner(early.send, "ctx", early.bit)
     ce_sums = ce_sum.finish()[0, :kinds]
     grad_w_in = jnp.concatenate(
-        [late.mine[:, :INNER], early[1].mine, late.mine[:, INNER:]], axis=1
-    )
-    scaled = jnp.exp(-log_var) / jnp.maximum(counts[0, 0, :kinds], 1.0)
+        [late.mine[:, :INNER], early.mine[:, width:], late.mine[:, INNER:USED]], axis=1
+    )
+    scaled = jnp.exp(-log_var) / jnp.maximum((counts + their_counts)[0, 0, :kinds], 1.0)
     loss = jnp.sum(scaled * ce_sums + log_var).reshape(1)
     grad_log_var = 1.0 - scaled * ce_sums
-    return (loss, grad_log_var, grad_fwd, grad_rc, grad_w_in, early[0].mine)
+    return (loss, grad_log_var, grad_fwd, grad_rc, grad_w_in, early.mine[:, :width])
 
 
 def solution(mesh):

time: 182 us -> 171 us (0.940)
  waiting for transfers between devices: 70.1 us -> 93.1 us
  starting transfers between devices: 30.8 us -> 17.9 us
  local copies, waits for them, and re-layouts: 12.3 us -> 0.85 us
  Pallas kernels: 55.9 us -> 48.2 us
    ppermute x23 -> x19, waiting for transfers between devices: 68.3 us -> 87 us  [partner(): lax.ppermute(array, axis, [(i, i ^ 1 << bit) for i in range(lax.axis_size...]
    pallas_call x7 -> x6, Pallas kernels: 50.6 us -> 36.7 us  [call(): pl.pallas_call(kernel, name=name, grid=(2,), in_specs=[specs[kind](array....]
    ppermute x23 -> x19, starting transfers between devices: 26.3 us -> 16.4 us  [partner(): lax.ppermute(array, axis, [(i, i ^ 1 << bit) for i in range(lax.axis_size...]
    pallas_call x3 -> x7, Pallas kernels: 5.26 us -> 11.5 us  [the longest x1 6.73 us: on_device(): pl.pallas_call(functools.partial(front_kernel, cuts=cuts), name='front',...]
    unnamed x68 -> x28, local copies, waits for them, and re-layouts: 5.25 us -> 0.08 us
    optimization_barrier x2 -> x0, local copies, waits for them, and re-layouts: 2.64 us -> none  [together(): return lax.optimization_barrier(arrays)]
    ppermute x1, waiting for transfers between devices: 1.79 us -> 4.3 us  [on_device(): got = lax.ppermute(sent, 'ctx', [(i, ctx - 1 - i) for i in range(ctx)])]
    ppermute x1, starting transfers between devices: 3.43 us -> 0.95 us  [on_device(): got = lax.ppermute(sent, 'ctx', [(i, ctx - 1 - i) for i in range(ctx)])]
  transfers between devices with their start and end apart: 29 -> 25, of which waited for: 15 -> 20; matrix products, arithmetic and copies ran while one was open for 6% -> 2% of each run, Pallas kernels for 12% -> 12%
where the time goes in v3:
time: 171 us
  waiting for transfers between devices  93.1 us (54%)
  Pallas kernels  48.2 us (28%)
  starting transfers between devices  17.9 us (10%)
  other arithmetic  8.85 us (5%)
  between operations  1.75 us (1%)
    ppermute x19, waiting for transfers between devices, partner(): lax.ppermute(array, axis, [(i, i ^ 1 << bit) for i in range(lax.axis_size...  87 us
    pallas_call x6, Pallas kernels, call(): pl.pallas_call(kernel, name=name, grid=(2,), in_specs=[specs[kind](array....  36.7 us
    ppermute x19, starting transfers between devices, partner(): lax.ppermute(array, axis, [(i, i ^ 1 << bit) for i in range(lax.axis_size...  16.4 us
    pallas_call x1, Pallas kernels, on_device(): pl.pallas_call(functools.partial(front_kernel, cuts=cuts), name='front',...  6.73 us
    pallas_call x2, Pallas kernels, __init__(): pl.pallas_call(functools.partial(weight_kernel, block=block, widths=(cols...  4.32 us
    ppermute x1, waiting for transfers between devices, on_device(): got = lax.ppermute(sent, 'ctx', [(i, ctx - 1 - i) for i in range(ctx)])  4.3 us
  transfers between devices with their start and end apart: 25, of which 20 were waited for; matrix products, arithmetic and copies ran while one was open for 2% of the time, Pallas kernels for 12%

profile of v3, /device:TPU:0, one launch (start us, length us, event | category | flops | bytes accessed | tf_op | source)
XLA Modules:
  0.0 170.7 jit_solution(15012440635795491897)
XLA Ops:
  1.3 6.7 %front.1 = (bf16[2,128,2192]{2,1,0:T(8,128)(2,1)}, bf16[2,2,64,1024]{3,2,1,0:T(8,128)(2,1)S(1)}, f32[3,1,1024]{2,1,0:T(1,128)S(1)}) custom-call(bf16[1,128,1024]{2,1,0:T(8,128)(2,1)} %fwd_ref.3, bf16[1,128,1024]{2,1,0:T(8,128)(2,1)} %rc_ref.3, bf16[2192,1024]{1,0:T(8,128)(2,1)} %bitcast.67, f32[1,16]{1,0:T(1,128)} %bitcast.77, f32[1,16]{1,0:T(1,128)} %bitcast.83, ...), custom_call_target="tpu_custom_call" | custom-call | flops 2000000000 | bytes 7000000 | tf_op jit(solution)/shard_map/front/pallas_call | solution.py:736
  8.0 3.1 %collective-permute-start.1 = (f32[3,1,1024]{2,1,0:T(1,128)S(1)}, f32[3,1,1024]{2,1,0:T(1,128)S(1)}, u32[]{:S(2)}, u32[]{:S(2)}) collective-permute-start(f32[3,1,1024]{2,1,0:T(1,128)S(1)} %get-tuple-element.78), channel_id=1, source_target_pairs={{0,1},{1,0},{2,3},{3,2},{4,5},{5,4},{6,7},{7,6},{8,9},{9,8},{10,11... | collective-permute-start | bytes 36872 | tf_op jit(solution)/shard_map/ppermute | solution.py:568
  11.2 4.7 %local.1 = (bf16[2,128,1024]{2,1,0:T(8,128)(2,1)}, bf16[2,128,1024]{2,1,0:T(8,128)(2,1)}) custom-call(bf16[2,128,2192]{2,1,0:T(8,128)(2,1)} %get-tuple-element.74.proj_ref, f32[1,16]{1,0:T(1,128)S(1)} %bitcast.78, f32[1,16]{1,0:T(1,128)S(1)} %bitcast.84, f32[1,16]{1,0:T(1,128)S(1)} %bitcast.75), custom_call_target="tpu_custom_call" | custom-call | flops 4000000000 | bytes 4000000 | tf_op jit(solution)/shard_map/local/pallas_call | solution.py:544
  16.1 8.4 %collective-permute-done = bf16[2,2,64,1024]{3,2,1,0:T(8,128)(2,1)S(1)} collective-permute-done((bf16[2,2,64,1024]{3,2,1,0:T(8,128)(2,1)S(1)}, bf16[2,2,64,1024]{3,2,1,0:T(8,128)(2,1)S(1)}, u32[]{:S(2)}, u32[]{:S(2)}) %collective-permute-start) | collective-permute-done | bytes 524320 | tf_op jit(solution)/shard_map/ppermute | solution.py:568
  26.9 1.7 %collective-permute-done.3 = f32[3,1,1024]{2,1,0:T(1,128)S(1)} collective-permute-done((f32[3,1,1024]{2,1,0:T(1,128)S(1)}, f32[3,1,1024]{2,1,0:T(1,128)S(1)}, u32[]{:S(2)}, u32[]{:S(2)}) %collective-permute-start.3) | collective-permute-done | bytes 12320 | tf_op jit(solution)/shard_map/ppermute | solution.py:568
  28.7 10.1 %collective-permute-done.2 = bf16[2,2,64,1024]{3,2,1,0:T(8,128)(2,1)S(1)} collective-permute-done((bf16[2,2,64,1024]{3,2,1,0:T(8,128)(2,1)S(1)}, bf16[2,2,64,1024]{3,2,1,0:T(8,128)(2,1)S(1)}, u32[]{:S(2)}, u32[]{:S(2)}) %collective-permute-start.2) | collective-permute-done | bytes 524320 | tf_op jit(solution)/shard_map/ppermute | solution.py:568
  39.2 2.8 %collective-permute-start.5 = (f32[3,1,1024]{2,1,0:T(1,128)S(1)}, f32[3,1,1024]{2,1,0:T(1,128)S(1)}, u32[]{:S(2)}, u32[]{:S(2)}) collective-permute-start(f32[3,1,1024]{2,1,0:T(1,128)S(1)} %pad_maximum_fusion.3), channel_id=1, source_target_pairs={{0,4},{1,5},{2,6},{3,7},{4,0},{5,1},{6,2},{7,3},{8,12},{9,13},{10,... | collective-permute-start | bytes 36872 | tf_op jit(solution)/shard_map/ppermute | solution.py:568
  42.2 3.8 %collective-permute-done.5 = f32[3,1,1024]{2,1,0:T(1,128)S(1)} collective-permute-done((f32[3,1,1024]{2,1,0:T(1,128)S(1)}, f32[3,1,1024]{2,1,0:T(1,128)S(1)}, u32[]{:S(2)}, u32[]{:S(2)}) %collective-permute-start.5) | collective-permute-done | bytes 12320 | tf_op jit(solution)/shard_map/ppermute | solution.py:568
  46.0 8.2 %collective-permute-done.4 = bf16[2,64,1024]{2,1,0:T(8,128)(2,1)S(1)} collective-permute-done((bf16[2,64,1024]{2,1,0:T(8,128)(2,1)S(1)}, bf16[2,64,1024]{2,1,0:T(8,128)(2,1)S(1)}, u32[]{:S(2)}, u32[]{:S(2)}) %collective-permute-start.4) | collective-permute-done | bytes 262176 | tf_op jit(solution)/shard_map/ppermute | solution.py:568
  54.7 7.1 %out.1 = (bf16[2,128,1024]{2,1,0:T(8,128)(2,1)S(1)}, bf16[2,128,1024]{2,1,0:T(8,128)(2,1)S(1)}, bf16[256,1024]{1,0:T(8,128)(2,1)S(1)}, f32[2,128,1024]{2,1,0:T(8,128)S(1)}, f32[24,128]{1,0:T(8,128)S(1)}) custom-call(bf16[2,128,2192]{2,1,0:T(8,128)(2,1)} %get-tuple-element.74.proj_ref, bf16[2,2,64,1024]{3,2,1,0:T(8,128)(2,1)S(1)} %fusion.2.carry_ref, ...), custom_call_target="tpu_custom_call" | custom-call | flops 2000000000 | bytes 8000000 | tf_op jit(solution)/shard_map/out/pallas_call | solution.py:544
  63.9 4.3 %collective-permute-done.8.got_ref = f32[24,128]{1,0:T(8,128)S(1)} collective-permute-done((f32[24,128]{1,0:T(8,128)S(1)}, f32[24,128]{1,0:T(8,128)S(1)}, u32[]{:S(2)}, u32[]{:S(2)}) %collective-permute-start.8) | collective-permute-done | bytes 12320 | tf_op jit(solution)/shard_map/ppermute | solution.py:808
  68.2 8.7 %head.1 = (f32[1,128]{1,0:T(1,128)S(1)}, bf16[256,2048]{1,0:T(8,128)(2,1)S(1)}, bf16[2,128,1024]{2,1,0:T(8,128)(2,1)}, bf16[2,128,1024]{2,1,0:T(8,128)(2,1)}, bf16[2,2,64,1024]{3,2,1,0:T(8,128)(2,1)S(1)}) custom-call(bf16[2,128,2192]{2,1,0:T(8,128)(2,1)} %get-tuple-element.74.proj_ref, f32[24,128]{1,0:T(8,128)S(1)} %get-tuple-element.87.sent_ref, ...), custom_call_target="tpu_custom_call" | custom-call | flops 2000000000 | bytes 8000000 | tf_op jit(solution)/shard_map/head/pallas_call | solution.py:544
  81.6 2.8 %weight.2 = (bf16[256,2048]{1,0:T(8,128)(2,1)S(1)}, f32[256,2048]{1,0:T(8,128)S(1)}) custom-call(s32[2]{0:T(128)S(1)} %pad_add_fusion.place_ref, bf16[256,1024]{1,0:T(8,128)(2,1)S(1)} %get-tuple-element.92.refs_0_, bf16[256,1024]{1,0:T(8,128)(2,1)S(1)} %pad_maximum_fusion.refs_1_.refs_0_, bf16[256,512]{1,0:T(8,128)(2,1)S(1)} %collective-permute-done.10.refs_2_, ...), custom_call_target="tpu_custom_call" | custom-call | flops 1200000000 | bytes 6000000 | tf_op jit(solution)/shard_map/weight/pallas_call | solution.py:659
  84.4 7.9 %collective-permute-done.9 = bf16[2,2,64,1024]{3,2,1,0:T(8,128)(2,1)} collective-permute-done((bf16[2,2,64,1024]{3,2,1,0:T(8,128)(2,1)S(1)}, bf16[2,2,64,1024]{3,2,1,0:T(8,128)(2,1)}, u32[]{:S(2)}, u32[]{:S(2)}) %collective-permute-start.9) | collective-permute-done | bytes 524320 | tf_op jit(solution)/shard_map/ppermute | solution.py:568
  97.3 9.4 %collective-permute-done.12 = bf16[2,2,64,1024]{3,2,1,0:T(8,128)(2,1)S(1)} collective-permute-done((bf16[2,2,64,1024]{3,2,1,0:T(8,128)(2,1)S(1)}, bf16[2,2,64,1024]{3,2,1,0:T(8,128)(2,1)S(1)}, u32[]{:S(2)}, u32[]{:S(2)}) %collective-permute-start.12) | collective-permute-done | bytes 524320 | tf_op jit(solution)/shard_map/ppermute | solution.py:568
  107.0 9.8 %adjoint.1 = (bf16[2,128,1024]{2,1,0:T(8,128)(2,1)S(1)}, f32[2,128,64]{2,1,0:T(8,128)S(1)}, f32[2,128,64]{2,1,0:T(8,128)S(1)}, f32[2,128,16]{2,1,0:T(8,128)S(1)}, f32[2,128,16]{2,1,0:T(8,128)S(1)}) custom-call(bf16[2,128,2192]{2,1,0:T(8,128)(2,1)} %get-tuple-element.74.proj_ref, bf16[2,2,64,1024]{3,2,1,0:T(8,128)(2,1)S(1)} %fusion.2.carry_ref, ...), custom_call_target="tpu_custom_call" | custom-call | flops 8000000000 | bytes 6000000 | tf_op jit(solution)/shard_map/adjoint/pallas_call | solution.py:544
  116.8 1.7 collective-permute-done.15.got_ref
  121.6 3.9 %finish.1.refs_2_.rest_ref = bf16[256,1280]{1,0:T(8,128)(2,1)S(1)} custom-call(bf16[2,128,2192]{2,1,0:T(8,128)(2,1)} %get-tuple-element.74.proj_ref, bf16[2,2,64,1024]{3,2,1,0:T(8,128)(2,1)S(1)} %fusion.2.carry_ref, bf16[2,2,64,1024]{3,2,1,0:T(8,128)(2,1)S(1)} %fusion.9.next_ref, bf16[2,128,1024]{2,1,0:T(8,128)(2,1)S(1)} %get-tuple-element.107.dval_in, ...), custom_call_target="tpu_custom_call" | custom-call | flops 2000000000 | bytes 5000000 | tf_op jit(solution)/shard_map/finish/pallas_call | solution.py:544
  126.0 3.2 %collective-permute-done.17 = f32[1,128]{1,0:T(1,128)S(1)} collective-permute-done((f32[1,128]{1,0:T(1,128)S(1)}, f32[1,128]{1,0:T(1,128)S(1)}, u32[]{:S(2)}, u32[]{:S(2)}) %collective-permute-start.17) | collective-permute-done | bytes 544 | tf_op jit(solution)/shard_map/ppermute | solution.py:568
  132.9 2.5 %input.1 = (bf16[1,128,1024]{2,1,0:T(8,128)(2,1)}, bf16[1,128,1024]{2,1,0:T(8,128)(2,1)}) custom-call(bf16[256,1280]{1,0:T(8,128)(2,1)S(1)} %finish.1.refs_2_.rest_ref, bf16[256,2048]{1,0:T(8,128)(2,1)S(1)} %get-tuple-element.93.refs_4_.cot_ref, bf16[2192,1024]{1,0:T(8,128)(2,1)S(1)} %bitcast.70), custom_call_target="tpu_custom_call" | custom-call | flops 2000000000 | bytes 7000000 | tf_op jit(solution)/shard_map/input/pallas_call | solution.py:544
  135.4 7.4 %collective-permute-done.20 = f32[1,128]{1,0:T(1,128)S(1)} collective-permute-done((f32[1,128]{1,0:T(1,128)S(1)}, f32[1,128]{1,0:T(1,128)S(1)}, u32[]{:S(2)}, u32[]{:S(2)}) %collective-permute-start.20) | collective-permute-done | bytes 544 | tf_op jit(solution)/shard_map/ppermute | solution.py:568
  142.8 4.0 %collective-permute-done.18.got_ref = bf16[256,1280]{1,0:T(8,128)(2,1)S(1)} collective-permute-done((bf16[256,1280]{1,0:T(8,128)(2,1)S(1)}, bf16[256,1280]{1,0:T(8,128)(2,1)S(1)}, u32[]{:S(2)}, u32[]{:S(2)}) %collective-permute-start.18) | collective-permute-done | bytes 655392 | tf_op jit(solution)/shard_map/ppermute | solution.py:568
  149.4 11.1 %collective-permute-done.22 = bf16[64,2048]{1,0:T(8,128)(2,1)S(1)} collective-permute-done((bf16[64,2048]{1,0:T(8,128)(2,1)S(1)}, bf16[64,2048]{1,0:T(8,128)(2,1)S(1)}, u32[]{:S(2)}, u32[]{:S(2)}) %collective-permute-start.22) | collective-permute-done | bytes 262176 | tf_op jit(solution)/shard_map/ppermute | solution.py:568
  164.1 5.8 %collective-permute-done.24 = bf16[64,1280]{1,0:T(8,128)(2,1)S(1)} collective-permute-done((bf16[64,1280]{1,0:T(8,128)(2,1)S(1)}, bf16[64,1280]{1,0:T(8,128)(2,1)S(1)}, u32[]{:S(2)}, u32[]{:S(2)}) %collective-permute-start.24) | collective-permute-done | bytes 163872 | tf_op jit(solution)/shard_map/ppermute | solution.py:568
  (108 shorter events, 30.0 us)
Async XLA Ops:
  8.0 7.9 %collective-permute-start.1 = (f32[3,1,1024]{2,1,0:T(1,128)S(1)}, f32[3,1,1024]{2,1,0:T(1,128)S(1)}, u32[]{:S(2)}, u32[]{:S(2)}) collective-permute-start(f32[3,1,1024]{2,1,0:T(1,128)S(1)} %get-tuple-element.78), channel_id=1, source_target_pairs={{0,1},{1,0},{2,3},{3,2},{4,5},{5,4},{6,7},{7,6},{8,9},{9,8},{10,11... | collective-permute-start | bytes 36872 | tf_op jit(solution)/shard_map/ppermute | solution.py:568
  11.1 13.4 %collective-permute-start = (bf16[2,2,64,1024]{3,2,1,0:T(8,128)(2,1)S(1)}, bf16[2,2,64,1024]{3,2,1,0:T(8,128)(2,1)S(1)}, u32[]{:S(2)}, u32[]{:S(2)}) collective-permute-start(bf16[2,2,64,1024]{3,2,1,0:T(8,128)(2,1)S(1)} %get-tuple-element.77), channel_id=1, source_target_pairs={{0,1},{1,0},{2,3},{3,2},{4,5},{5,4},{6,7},{7,6},{8,9},{9,8},{10,11... | collective-permute-start | bytes 1572872 | tf_op jit(solution)/shard_map/ppermute | solution.py:568
  24.7 3.9 %collective-permute-start.3 = (f32[3,1,1024]{2,1,0:T(1,128)S(1)}, f32[3,1,1024]{2,1,0:T(1,128)S(1)}, u32[]{:S(2)}, u32[]{:S(2)}) collective-permute-start(f32[3,1,1024]{2,1,0:T(1,128)S(1)} %pad_maximum_fusion.2), channel_id=1, source_target_pairs={{0,2},{1,3},{2,0},{3,1},{4,6},{5,7},{6,4},{7,5},{8,10},{9,11},{10,... | collective-permute-start | bytes 36872 | tf_op jit(solution)/shard_map/ppermute | solution.py:568
  26.4 12.5 %collective-permute-start.2 = (bf16[2,2,64,1024]{3,2,1,0:T(8,128)(2,1)S(1)}, bf16[2,2,64,1024]{3,2,1,0:T(8,128)(2,1)S(1)}, u32[]{:S(2)}, u32[]{:S(2)}) collective-permute-start(bf16[2,2,64,1024]{3,2,1,0:T(8,128)(2,1)S(1)} %fusion.4), channel_id=1, source_target_pairs={{0,2},{1,3},{2,0},{3,1},{4,6},{5,7},{6,4},{7,5},{8,10},{9,11},{10,... | collective-permute-start | bytes 1572872 | tf_op jit(solution)/shard_map/ppermute | solution.py:568
  39.2 6.8 %collective-permute-start.5 = (f32[3,1,1024]{2,1,0:T(1,128)S(1)}, f32[3,1,1024]{2,1,0:T(1,128)S(1)}, u32[]{:S(2)}, u32[]{:S(2)}) collective-permute-start(f32[3,1,1024]{2,1,0:T(1,128)S(1)} %pad_maximum_fusion.3), channel_id=1, source_target_pairs={{0,4},{1,5},{2,6},{3,7},{4,0},{5,1},{6,2},{7,3},{8,12},{9,13},{10,... | collective-permute-start | bytes 36872 | tf_op jit(solution)/shard_map/ppermute | solution.py:568
  42.0 12.2 %collective-permute-start.4 = (bf16[2,64,1024]{2,1,0:T(8,128)(2,1)S(1)}, bf16[2,64,1024]{2,1,0:T(8,128)(2,1)S(1)}, u32[]{:S(2)}, u32[]{:S(2)}) collective-permute-start(bf16[2,64,1024]{2,1,0:T(8,128)(2,1)S(1)} %fusion.18), channel_id=1, source_target_pairs={{0,4},{1,5},{2,6},{3,7},{4,0},{5,1},{6,2},{7,3},{8,12},{9,13},{10,... | collective-permute-start | bytes 786440 | tf_op jit(solution)/shard_map/ppermute | solution.py:568
  61.8 6.4 %collective-permute-start.8 = (f32[24,128]{1,0:T(8,128)S(1)}, f32[24,128]{1,0:T(8,128)S(1)}, u32[]{:S(2)}, u32[]{:S(2)}) collective-permute-start(f32[24,128]{1,0:T(8,128)S(1)} %get-tuple-element.87.sent_ref), channel_id=1, source_target_pairs={{0,7},{1,6},{2,5},{3,4},{4,3},{5,2},{6,1},{7,0},{8,15},{9,14},{10,... | collective-permute-start | bytes 36872 | tf_op jit(solution)/shard_map/ppermute | solution.py:808
  62.8 1.2 collective-permute-start.6
  77.0 4.7 %collective-permute-start.11 = (bf16[256,2048]{1,0:T(8,128)(2,1)S(1)}, bf16[256,2048]{1,0:T(8,128)(2,1)}, u32[]{:S(2)}, u32[]{:S(2)}) collective-permute-start(bf16[256,2048]{1,0:T(8,128)(2,1)S(1)} %get-tuple-element.93.refs_4_.cot_ref), channel_id=1, source_target_pairs={{0,8},{8,0},{1,9},{9,1},{2,10},{10,2},{3,11},{11,3},{4,12},{12,4},... | collective-permute-start | bytes 3145736 | tf_op jit(solution)/shard_map/ppermute | solution.py:641
  77.8 3.1 %collective-permute-start.7 = (bf16[256,512]{1,0:T(8,128)(2,1)}, bf16[256,512]{1,0:T(8,128)(2,1)S(1)}, u32[]{:S(2)}, u32[]{:S(2)}) collective-permute-start(bf16[256,512]{1,0:T(8,128)(2,1)} %fusion.15), channel_id=1, source_target_pairs={{0,8},{8,0},{1,9},{9,1},{2,10},{10,2},{3,11},{11,3},{4,12},{12,4},... | collective-permute-start | bytes 786440 | tf_op jit(solution)/shard_map/ppermute | solution.py:641
  78.3 14.0 %collective-permute-start.9 = (bf16[2,2,64,1024]{3,2,1,0:T(8,128)(2,1)S(1)}, bf16[2,2,64,1024]{3,2,1,0:T(8,128)(2,1)}, u32[]{:S(2)}, u32[]{:S(2)}) collective-permute-start(bf16[2,2,64,1024]{3,2,1,0:T(8,128)(2,1)S(1)} %get-tuple-element.91), channel_id=1, source_target_pairs={{0,1},{1,0},{2,3},{3,2},{4,5},{5,4},{6,7},{7,6},{8,9},{9,8},{10,11... | collective-permute-start | bytes 1572872 | tf_op jit(solution)/shard_map/ppermute | solution.py:568
  79.9 1.7 %collective-permute-start.10 = (bf16[256,512]{1,0:T(8,128)(2,1)}, bf16[256,512]{1,0:T(8,128)(2,1)S(1)}, u32[]{:S(2)}, u32[]{:S(2)}) collective-permute-start(bf16[256,512]{1,0:T(8,128)(2,1)} %slice_select_fusion.2), channel_id=1, source_target_pairs={{0,8},{8,0},{1,9},{9,1},{2,10},{10,2},{3,11},{11,3},{4,12},{12,4},... | collective-permute-start | bytes 786440 | tf_op jit(solution)/shard_map/ppermute | solution.py:641
  93.6 13.1 %collective-permute-start.12 = (bf16[2,2,64,1024]{3,2,1,0:T(8,128)(2,1)S(1)}, bf16[2,2,64,1024]{3,2,1,0:T(8,128)(2,1)S(1)}, u32[]{:S(2)}, u32[]{:S(2)}) collective-permute-start(bf16[2,2,64,1024]{3,2,1,0:T(8,128)(2,1)S(1)} %fusion.11), channel_id=1, source_target_pairs={{0,2},{1,3},{2,0},{3,1},{4,6},{5,7},{6,4},{7,5},{8,10},{9,11},{10,... | collective-permute-start | bytes 1572872 | tf_op jit(solution)/shard_map/ppermute | solution.py:568
  93.6 3.6 %collective-permute-start.13 = (f32[1,128]{1,0:T(1,128)S(1)}, f32[1,128]{1,0:T(1,128)S(1)}, u32[]{:S(2)}, u32[]{:S(2)}) collective-permute-start(f32[1,128]{1,0:T(1,128)S(1)} %get-tuple-element.99), channel_id=1, source_target_pairs={{0,1},{1,0},{2,3},{3,2},{4,5},{5,4},{6,7},{7,6},{8,9},{9,8},{10,11... | collective-permute-start | bytes 1544 | tf_op jit(solution)/shard_map/ppermute | solution.py:568
  94.5 24.0 %collective-permute-start.15 = (bf16[256,2048]{1,0:T(8,128)(2,1)S(1)}, bf16[256,2048]{1,0:T(8,128)(2,1)S(1)}, u32[]{:S(2)}, u32[]{:S(2)}) collective-permute-start(bf16[256,2048]{1,0:T(8,128)(2,1)S(1)} %get-tuple-element.102), channel_id=1, source_target_pairs={{0,1},{1,0},{2,3},{3,2},{4,5},{5,4},{6,7},{7,6},{8,9},{9,8},{10,11... | collective-permute-start | bytes 3145736 | tf_op jit(solution)/shard_map/ppermute | solution.py:568
  106.9 13.1 %collective-permute-start.14 = (bf16[2,64,1024]{2,1,0:T(8,128)(2,1)S(1)}, bf16[2,64,1024]{2,1,0:T(8,128)(2,1)S(1)}, u32[]{:S(2)}, u32[]{:S(2)}) collective-permute-start(bf16[2,64,1024]{2,1,0:T(8,128)(2,1)S(1)} %fusion.17), channel_id=1, source_target_pairs={{0,4},{1,5},{2,6},{3,7},{4,0},{5,1},{6,2},{7,3},{8,12},{9,13},{10,... | collective-permute-start | bytes 786440 | tf_op jit(solution)/shard_map/ppermute | solution.py:568
  125.5 3.7 %collective-permute-start.16 = (bf16[256,1280]{1,0:T(8,128)(2,1)S(1)}, bf16[256,1280]{1,0:T(8,128)(2,1)S(1)}, u32[]{:S(2)}, u32[]{:S(2)}) collective-permute-start(bf16[256,1280]{1,0:T(8,128)(2,1)S(1)} %finish.1.refs_2_.rest_ref), channel_id=1, source_target_pairs={{0,8},{8,0},{1,9},{9,1},{2,10},{10,2},{3,11},{11,3},{4,12},{12,4},... | collective-permute-start | bytes 1966088 | tf_op jit(solution)/shard_map/ppermute | solution.py:641
  125.6 3.6 %collective-permute-start.17 = (f32[1,128]{1,0:T(1,128)S(1)}, f32[1,128]{1,0:T(1,128)S(1)}, u32[]{:S(2)}, u32[]{:S(2)}) collective-permute-start(f32[1,128]{1,0:T(1,128)S(1)} %add.72), channel_id=1, source_target_pairs={{0,2},{1,3},{2,0},{3,1},{4,6},{5,7},{6,4},{7,5},{8,10},{9,11},{10,... | collective-permute-start | bytes 1544 | tf_op jit(solution)/shard_map/ppermute | solution.py:568
  130.8 16.0 %collective-permute-start.18 = (bf16[256,1280]{1,0:T(8,128)(2,1)S(1)}, bf16[256,1280]{1,0:T(8,128)(2,1)S(1)}, u32[]{:S(2)}, u32[]{:S(2)}) collective-permute-start(bf16[256,1280]{1,0:T(8,128)(2,1)S(1)} %get-tuple-element.116), channel_id=1, source_target_pairs={{0,1},{1,0},{2,3},{3,2},{4,5},{5,4},{6,7},{7,6},{8,9},{9,8},{10,11... | collective-permute-start | bytes 1966088 | tf_op jit(solution)/shard_map/ppermute | solution.py:568
  131.7 15.1 %collective-permute-start.19 = (bf16[128,2048]{1,0:T(8,128)(2,1)S(1)}, bf16[128,2048]{1,0:T(8,128)(2,1)S(1)}, u32[]{:S(2)}, u32[]{:S(2)}) collective-permute-start(bf16[128,2048]{1,0:T(8,128)(2,1)S(1)} %get-tuple-element.121), channel_id=1, source_target_pairs={{0,2},{1,3},{2,0},{3,1},{4,6},{5,7},{6,4},{7,5},{8,10},{9,11},{10,... | collective-permute-start | bytes 1572872 | tf_op jit(solution)/shard_map/ppermute | solution.py:568
  132.4 10.4 %collective-permute-start.20 = (f32[1,128]{1,0:T(1,128)S(1)}, f32[1,128]{1,0:T(1,128)S(1)}, u32[]{:S(2)}, u32[]{:S(2)}) collective-permute-start(f32[1,128]{1,0:T(1,128)S(1)} %add.74), channel_id=1, source_target_pairs={{0,4},{1,5},{2,6},{3,7},{4,0},{5,1},{6,2},{7,3},{8,12},{9,13},{10,... | collective-permute-start | bytes 1544 | tf_op jit(solution)/shard_map/ppermute | solution.py:568
  147.1 13.7 %collective-permute-start.21 = (bf16[128,1280]{1,0:T(8,128)(2,1)S(1)}, bf16[128,1280]{1,0:T(8,128)(2,1)S(1)}, u32[]{:S(2)}, u32[]{:S(2)}) collective-permute-start(bf16[128,1280]{1,0:T(8,128)(2,1)S(1)} %get-tuple-element.130), channel_id=1, source_target_pairs={{0,2},{1,3},{2,0},{3,1},{4,6},{5,7},{6,4},{7,5},{8,10},{9,11},{10,... | collective-permute-start | bytes 983048 | tf_op jit(solution)/shard_map/ppermute | solution.py:568
  147.5 13.0 %collective-permute-start.22 = (bf16[64,2048]{1,0:T(8,128)(2,1)S(1)}, bf16[64,2048]{1,0:T(8,128)(2,1)S(1)}, u32[]{:S(2)}, u32[]{:S(2)}) collective-permute-start(bf16[64,2048]{1,0:T(8,128)(2,1)S(1)} %get-tuple-element.131), channel_id=1, source_target_pairs={{0,4},{1,5},{2,6},{3,7},{4,0},{5,1},{6,2},{7,3},{8,12},{9,13},{10,... | collective-permute-start | bytes 786440 | tf_op jit(solution)/shard_map/ppermute | solution.py:568
  161.6 8.2 %collective-permute-start.24 = (bf16[64,1280]{1,0:T(8,128)(2,1)S(1)}, bf16[64,1280]{1,0:T(8,128)(2,1)S(1)}, u32[]{:S(2)}, u32[]{:S(2)}) collective-permute-start(bf16[64,1280]{1,0:T(8,128)(2,1)S(1)} %get-tuple-element.139), channel_id=1, source_target_pairs={{0,4},{1,5},{2,6},{3,7},{4,0},{5,1},{6,2},{7,3},{8,12},{9,13},{10,... | collective-permute-start | bytes 491528 | tf_op jit(solution)/shard_map/ppermute | solution.py:568
  (15 other events, 168.5 us)
